TPU v7x, 32 devices: a whole 2x2x4 slice. The times are simulated.
32 devices in a mesh: ctx: 8 (over z, y), fsdp: 4 (over x, core).
Axes of the slice: x: 2, y: 2, z: 4, core: 2. Of those that a mesh axis runs over, the one named last changes fastest.
Arguments:
- tokens: bfloat16 [3, 4, 2048, 1024], P(None, 'fsdp', 'ctx'), may hold values from -6 to 6
- w_router: float32 [1024], replicated, may hold values from -0.1875 to 0.1875
- gain_attn: float32 [1024], replicated, may hold values from 0.1 to 1.9
- w_qkv: bfloat16 [1024, 3072], P('fsdp'), may hold values from -0.1875 to 0.1875
- w_out: bfloat16 [1024, 1024], P('fsdp'), may hold values from -1 to 1
- gain_mlp: float32 [1024], replicated, may hold values from 0.1 to 1.9
- w_up: bfloat16 [1024, 4096], P('fsdp'), may hold values from -0.1875 to 0.1875
- w_down: bfloat16 [4096, 1024], P('fsdp'), may hold values from -0.09375 to 0.09375
- routed: int32 [3, 4, 256], P(None, 'fsdp', 'ctx'), may hold values from 0 to 2047, as said below
- deal: int32 [16], replicated, may hold values from 0 to 15, as said below
- cotangent: bfloat16 [3, 4, 2048, 1024], P(None, 'fsdp', 'ctx'), may hold values from -6 to 6
Outputs:
- output: bfloat16 [3, 4, 2048, 1024], P(None, 'fsdp', 'ctx')
- input_grad: bfloat16 [3, 4, 2048, 1024], P(None, 'fsdp', 'ctx')
- grad_router: float32 [1024], P(('ctx', 'fsdp'))
- grad_gain_attn: float32 [1024], P(('ctx', 'fsdp'))
- grad_qkv: float32 [1024, 3072], P(('ctx', 'fsdp'))
- grad_out: float32 [1024, 1024], P(('ctx', 'fsdp'))
- grad_gain_mlp: float32 [1024], P(('ctx', 'fsdp'))
- grad_up: float32 [1024, 4096], P(('ctx', 'fsdp'))
- grad_down: float32 [4096, 1024], P(('ctx', 'fsdp'))
Inputs may be any that keep to these rules, and one draw needn't show every extreme that they name: `routed`: for each micro-batch and sequence the indices rise; entries j * 32 to (j + 1) * 32 - 1 are distinct stored rows among j * 256 to (j + 1) * 256 - 1, and include j * 256 and (j + 1) * 256 - 1. `deal`: each initial span appears once; stored spans 2 j and 2 j + 1 hold initial spans c and 15 - c.
All inputs are finite; a program needn't handle non-finite values.
Results may differ from a plain program's by a relative error of at most 0.012.
Values may be sent and summed in bfloat16 or wider, within the bound.
No kernel may reach another device: no remote copies, remote signals or barrier semaphores. Data moves between devices by JAX's collectives and lax.ppermute only.
A program may use at most 256 MiB of HBM per device.

v0:
```python
import jax
import jax.numpy as jnp
from jax import lax
from jax.sharding import PartitionSpec as P

HEADS = 16
HEAD_DIM = 64
BLOCK = 256


EPSILON = 1e-06
MASKED = -1e30
HIGHEST = lax.Precision.HIGHEST


def rms_norm(values, gain):
    factor = lax.rsqrt(jnp.mean(values * values, axis=-1, keepdims=True) + EPSILON)
    return values * factor * gain


def exact_gelu(values):
    return jax.nn.gelu(values, approximate=False)


def fetch(w_qkv, w_out, w_up, w_down):
    return (
        lax.all_gather(w_qkv, "fsdp", axis=0, tiled=True),
        lax.all_gather(w_out, "fsdp", axis=0, tiled=True),
        lax.all_gather(w_up, "fsdp", axis=0, tiled=True),
        lax.all_gather(w_down, "fsdp", axis=0, tiled=True),
    )


def lookup(table, index):
    hits = index[..., None] == jnp.arange(table.shape[0], dtype=jnp.int32)
    return jnp.sum(jnp.where(hits, table, 0), axis=-1)


def outer_sum(left, right):
    return lax.dot_general(
        left, right, (((0,), (0,)), ((), ())), preferred_element_type=jnp.float32
    )


def gather_rows(pieces, column):
    return jnp.concatenate([piece[column] for piece in pieces], axis=0)


def shards(
    tokens, w_router, gain_attn, w_qkv, w_out, gain_mlp, w_up, w_down, routed, deal, cotangent
):
    micros, tok_dev, width = (tokens.shape[0], tokens.shape[2], tokens.shape[3])
    span = tok_dev // 2
    rank = lax.axis_index("ctx")
    storage = routed[:, 0, :]
    local_rows = storage - rank * tok_dev
    anchor = lookup(deal, storage // span) * span + storage % span
    own_blocks = anchor // BLOCK
    all_blocks = lax.all_gather(own_blocks, "ctx", axis=1, tiled=True)
    factor = HEAD_DIM ** (-0.5)
    outputs, in_grads, kept = ([], [], [])
    sum_router = jnp.zeros((width,), jnp.float32)
    sum_gain_attn = jnp.zeros((width,), jnp.float32)
    sum_gain_mlp = jnp.zeros((width,), jnp.float32)
    for micro in range(micros):
        full_qkv, full_out, full_up, full_down = fetch(w_qkv, w_out, w_up, w_down)
        resid = tokens[micro, 0].astype(jnp.float32)
        grad_in = cotangent[micro, 0].astype(jnp.float32)
        rows_index = local_rows[micro]
        rows = jnp.take(resid, rows_index, axis=0)
        count = rows.shape[0]
        gate = jax.nn.sigmoid(jnp.dot(rows, w_router, precision=HIGHEST))
        norm1, norm1_back = jax.vjp(rms_norm, rows, gain_attn)
        norm1_low = norm1.astype(jnp.bfloat16)
        qkv = jnp.dot(norm1_low, full_qkv, preferred_element_type=jnp.float32).astype(jnp.bfloat16)
        queries = qkv[:, :width]
        keys_local = qkv[:, width : 2 * width]
        values_local = qkv[:, 2 * width :]
        keys_all, values_all = (
            lax.all_gather(keys_local, "ctx", axis=0, tiled=True),
            lax.all_gather(values_local, "ctx", axis=0, tiled=True),
        )
        total = keys_all.shape[0]
        query_heads = queries.reshape(count, HEADS, HEAD_DIM)
        key_heads = keys_all.reshape(total, HEADS, HEAD_DIM)
        value_heads = values_all.reshape(total, HEADS, HEAD_DIM)
        visible = all_blocks[micro][None, :] <= own_blocks[micro][:, None]
        scores = (
            jnp.einsum("qhd,khd->hqk", query_heads, key_heads, preferred_element_type=jnp.float32)
            * factor
        )
        scores = jnp.where(visible[None], scores, MASKED)
        probs = jax.nn.softmax(scores, axis=-1)
        probs_low = probs.astype(jnp.bfloat16)
        attended = jnp.einsum(
            "hqk,khd->qhd", probs_low, value_heads, preferred_element_type=jnp.float32
        )
        attended_low = attended.reshape(count, width).astype(jnp.bfloat16)
        attn = jnp.dot(attended_low, full_out, preferred_element_type=jnp.float32)
        mid = rows + attn
        norm2, norm2_back = jax.vjp(rms_norm, mid, gain_mlp)
        norm2_low = norm2.astype(jnp.bfloat16)
        hidden = jnp.dot(norm2_low, full_up, preferred_element_type=jnp.float32)
        act, gelu_back = jax.vjp(exact_gelu, hidden)
        act_low = act.astype(jnp.bfloat16)
        mlp = jnp.dot(act_low, full_down, preferred_element_type=jnp.float32)
        branch = attn + mlp
        outputs.append(resid.at[rows_index].set(rows + gate[:, None] * branch).astype(jnp.bfloat16))
        cot_rows = jnp.take(grad_in, rows_index, axis=0)
        d_branch = gate[:, None] * cot_rows
        d_mlp = d_branch.astype(jnp.bfloat16)
        d_logit = jnp.sum(cot_rows * branch, axis=-1) * gate * (1.0 - gate)
        d_act = jnp.dot(d_mlp, full_down.T, preferred_element_type=jnp.float32)
        d_hidden = gelu_back(d_act)[0].astype(jnp.bfloat16)
        d_norm2 = jnp.dot(d_hidden, full_up.T, preferred_element_type=jnp.float32)
        d_mid, d_gain2 = norm2_back(d_norm2)
        d_attn = (d_branch + d_mid).astype(jnp.bfloat16)
        d_attended = jnp.dot(d_attn, full_out.T, preferred_element_type=jnp.float32).astype(
            jnp.bfloat16
        )
        d_heads = d_attended.reshape(count, HEADS, HEAD_DIM)
        d_probs = jnp.einsum(
            "qhd,khd->hqk", d_heads, value_heads, preferred_element_type=jnp.float32
        )
        weighted = jnp.sum(probs * d_probs, axis=-1, keepdims=True)
        d_scores = (probs * (d_probs - weighted)).astype(jnp.bfloat16)
        d_query = (
            jnp.einsum("hqk,khd->qhd", d_scores, key_heads, preferred_element_type=jnp.float32)
            * factor
        )
        d_key_part = (
            jnp.einsum("hqk,qhd->khd", d_scores, query_heads, preferred_element_type=jnp.float32)
            * factor
        )
        d_value_part = jnp.einsum(
            "hqk,qhd->khd", probs_low, d_heads, preferred_element_type=jnp.float32
        )
        d_keys, d_values = (
            lax.psum_scatter(
                d_key_part.reshape(total, width), "ctx", scatter_dimension=0, tiled=True
            ),
            lax.psum_scatter(
                d_value_part.reshape(total, width), "ctx", scatter_dimension=0, tiled=True
            ),
        )
        d_qkv = jnp.concatenate([d_query.reshape(count, width), d_keys, d_values], axis=1).astype(
            jnp.bfloat16
        )
        d_norm1 = jnp.dot(d_qkv, full_qkv.T, preferred_element_type=jnp.float32)
        d_rows_norm, d_gain1 = norm1_back(d_norm1)
        d_rows = cot_rows + d_mid + d_rows_norm + d_logit[:, None] * w_router
        in_grads.append(grad_in.at[rows_index].set(d_rows).astype(jnp.bfloat16))
        sum_router = sum_router + jnp.dot(d_logit, rows, precision=HIGHEST)
        sum_gain_attn = sum_gain_attn + d_gain1
        sum_gain_mlp = sum_gain_mlp + d_gain2
        kept.append((norm1_low, d_qkv, attended_low, d_attn, norm2_low, d_hidden, act_low, d_mlp))
    stacked_rows = tuple((gather_rows(kept, column) for column in range(8)))
    grad_qkv = outer_sum(stacked_rows[0], stacked_rows[1])
    grad_out = outer_sum(stacked_rows[2], stacked_rows[3])
    grad_up = outer_sum(stacked_rows[4], stacked_rows[5])
    grad_down = outer_sum(stacked_rows[6], stacked_rows[7])
    summed = (
        lax.psum_scatter(sum_router, ("ctx", "fsdp"), scatter_dimension=0, tiled=True),
        lax.psum_scatter(sum_gain_attn, ("ctx", "fsdp"), scatter_dimension=0, tiled=True),
        lax.psum_scatter(grad_qkv, ("ctx", "fsdp"), scatter_dimension=0, tiled=True),
        lax.psum_scatter(grad_out, ("ctx", "fsdp"), scatter_dimension=0, tiled=True),
        lax.psum_scatter(sum_gain_mlp, ("ctx", "fsdp"), scatter_dimension=0, tiled=True),
        lax.psum_scatter(grad_up, ("ctx", "fsdp"), scatter_dimension=0, tiled=True),
        lax.psum_scatter(grad_down, ("ctx", "fsdp"), scatter_dimension=0, tiled=True),
    )
    output = jnp.stack(outputs)[:, None]
    input_grad = jnp.stack(in_grads)[:, None]
    return (
        output,
        input_grad,
        summed[0],
        summed[1],
        summed[2],
        summed[3],
        summed[4],
        summed[5],
        summed[6],
    )


def solution(mesh):
    placed = (
        P(None, "fsdp", "ctx", None),
        P(),
        P(),
        P("fsdp", None),
        P("fsdp", None),
        P(),
        P("fsdp", None),
        P("fsdp", None),
        P(None, "fsdp", "ctx"),
        P(),
        P(None, "fsdp", "ctx", None),
    )
    return jax.shard_map(
        shards,
        mesh=mesh,
        in_specs=placed,
        out_specs=(
            P(None, "fsdp", "ctx", None),
            P(None, "fsdp", "ctx", None),
            P(("ctx", "fsdp")),
            P(("ctx", "fsdp")),
            P(("ctx", "fsdp"), None),
            P(("ctx", "fsdp"), None),
            P(("ctx", "fsdp")),
            P(("ctx", "fsdp"), None),
            P(("ctx", "fsdp"), None),
        ),
        check_vma=False,
    )
```

profile of v0, /device:TPU:4, one launch (start us, length us, event | category | flops | bytes accessed | tf_op | source)
XLA Modules:
  0.0 1513.2 jit_solution(7598239076845456931)
XLA Ops:
  10.8 26.3 %all-gather = s32[8,32,3]{1,2,0:T(4,128)S(1)} all-gather(s32[1,32,3]{1,2,0:T(4,128)S(1)} %bitcast.289), channel_id=1, replica_groups=mesh['ctx'=8,'fsdp'=4] {'ctx'}, dimensions={0}, use_global_device_ids=true | all-gather | bytes 3456 | tf_op jit(solution)/shard_map/all_gather | solution.py:59
  47.6 9.6 all-gather.6.cloned.1.call-done
  61.4 31.5 %all_gather.44 = bf16[256,1024]{1,0:T(8,128)(2,1)S(1)} all-gather(bf16[32,1024]{1,0:T(8,128)(2,1)S(1)} %get-tuple-element.89), channel_id=1, replica_groups=mesh['ctx'=8,'fsdp'=4] {'ctx'}, dimensions={0}, use_global_device_ids=true | all-gather | bytes 589824 | tf_op jit(solution)/shard_map/all_gather | solution.py:80
  93.1 31.7 %all_gather.42 = bf16[256,1024]{1,0:T(8,128)(2,1)S(1)} all-gather(bf16[32,1024]{1,0:T(8,128)(2,1)S(1)} %get-tuple-element.90), channel_id=1, replica_groups=mesh['ctx'=8,'fsdp'=4] {'ctx'}, dimensions={0}, use_global_device_ids=true | all-gather | bytes 589824 | tf_op jit(solution)/shard_map/all_gather | solution.py:81
  131.0 10.3 all-gather.10.cloned.1.call-done
  146.3 54.8 %all-gather.12.cloned.1.call-done = bf16[4096,1024]{1,0:T(8,128)(2,1)} async-done(((bf16[1024,1024]{1,0:T(8,128)(2,1)}), bf16[4096,1024]{1,0:T(8,128)(2,1)}) %all-gather.12.cloned.1.call-update) | async-done | bytes 8388624 | tf_op jit(solution)/shard_map/all_gather | solution.py:30
  256.5 26.9 %reduce-scatter.13.cloned.1.call-done = f32[32,1024]{1,0:T(8,128)} async-done(((f32[256,1024]{1,0:T(8,128)}), f32[32,1024]{1,0:T(8,128)}) %reduce-scatter.13.cloned.1.call-update) | async-done | bytes 131088 | tf_op jit(solution)/shard_map/reduce_scatter | solution.py:142
  284.9 64.6 %reduce-scatter.11.cloned.1.call-done = f32[32,1024]{1,0:T(8,128)} async-done(((f32[256,1024]{1,0:T(8,128)}), f32[32,1024]{1,0:T(8,128)}) %reduce-scatter.11.cloned.1.call-update) | async-done | bytes 131088 | tf_op jit(solution)/shard_map/reduce_scatter | solution.py:139
  369.3 32.1 %all_gather.51 = bf16[256,1024]{1,0:T(8,128)(2,1)} all-gather(bf16[32,1024]{1,0:T(8,128)(2,1)} %get-tuple-element.95), channel_id=1, replica_groups=mesh['ctx'=8,'fsdp'=4] {'ctx'}, dimensions={0}, use_global_device_ids=true | all-gather | bytes 589824 | tf_op jit(solution)/shard_map/all_gather | solution.py:80
  403.5 33.6 %all_gather.50 = bf16[256,1024]{1,0:T(8,128)(2,1)} all-gather(bf16[32,1024]{1,0:T(8,128)(2,1)} %get-tuple-element.96), channel_id=1, replica_groups=mesh['ctx'=8,'fsdp'=4] {'ctx'}, dimensions={0}, use_global_device_ids=true | all-gather | bytes 589824 | tf_op jit(solution)/shard_map/all_gather | solution.py:81
  439.2 33.7 %all_gather.49 = bf16[256,1024]{1,0:T(8,128)(2,1)} all-gather(bf16[32,1024]{1,0:T(8,128)(2,1)} %get-tuple-element.92), channel_id=1, replica_groups=mesh['ctx'=8,'fsdp'=4] {'ctx'}, dimensions={0}, use_global_device_ids=true | all-gather | bytes 589824 | tf_op jit(solution)/shard_map/all_gather | solution.py:80
  475.0 33.2 %all_gather.48 = bf16[256,1024]{1,0:T(8,128)(2,1)} all-gather(bf16[32,1024]{1,0:T(8,128)(2,1)} %get-tuple-element.93), channel_id=1, replica_groups=mesh['ctx'=8,'fsdp'=4] {'ctx'}, dimensions={0}, use_global_device_ids=true | all-gather | bytes 589824 | tf_op jit(solution)/shard_map/all_gather | solution.py:81
  541.0 7.6 add_convert_fusion.1
  594.3 42.3 %reduce-scatter.17.cloned.1.call-done = f32[32,1024]{1,0:T(8,128)} async-done(((f32[256,1024]{1,0:T(8,128)}), f32[32,1024]{1,0:T(8,128)}) %reduce-scatter.17.cloned.1.call-update) | async-done | bytes 131088 | tf_op jit(solution)/shard_map/reduce_scatter | solution.py:142
  637.5 65.4 %reduce-scatter.21.cloned.1.call-done = f32[32,1024]{1,0:T(8,128)} async-done(((f32[256,1024]{1,0:T(8,128)}), f32[32,1024]{1,0:T(8,128)}) %reduce-scatter.21.cloned.1.call-update) | async-done | bytes 131088 | tf_op jit(solution)/shard_map/reduce_scatter | solution.py:142
  703.8 65.1 %reduce-scatter.15.cloned.1.call-done = f32[32,1024]{1,0:T(8,128)} async-done(((f32[256,1024]{1,0:T(8,128)}), f32[32,1024]{1,0:T(8,128)}) %reduce-scatter.15.cloned.1.call-update) | async-done | bytes 131088 | tf_op jit(solution)/shard_map/reduce_scatter | solution.py:139
  769.9 65.1 %reduce-scatter.19.cloned.1.call-done = f32[32,1024]{1,0:T(8,128)} async-done(((f32[256,1024]{1,0:T(8,128)}), f32[32,1024]{1,0:T(8,128)}) %reduce-scatter.19.cloned.1.call-update) | async-done | bytes 131088 | tf_op jit(solution)/shard_map/reduce_scatter | solution.py:139
  845.6 8.2 fusion.39
  854.9 8.1 fusion.33
  905.1 41.4 %all-reduce.3 = (f32[1024]{0:T(1024)S(1)}, f32[1024]{0:T(1024)S(1)}, f32[1024]{0:T(1024)S(1)}) all-reduce(f32[1024]{0:T(1024)S(1)} %add_add_fusion.11, f32[1024]{0:T(1024)S(1)} %add_add_fusion.10, f32[1024]{0:T(1024)} %add_add_fusion.9), channel_id=8, replica_groups=mesh['ctx'=8,'fsdp'=4] {'ctx','fsdp'}, use_global_device_ids=true, to_apply=%region_37.39.clone | all-reduce | flops 3072 | bytes 24576
  952.1 16.2 %reduce-scatter.25.cloned.1.call-done = f32[32,1024]{1,0:T(8,128)} async-done(((f32[1024,1024]{1,0:T(8,128)}), f32[32,1024]{1,0:T(8,128)}) %reduce-scatter.25.cloned.1.call-update) | async-done | bytes 131088 | tf_op jit(solution)/shard_map/reduce_scatter | solution.py:166
  968.3 167.7 %reduce-scatter.23.cloned.1.call-done = f32[32,3072]{1,0:T(8,128)} async-done(((f32[1024,3072]{1,0:T(8,128)}), f32[32,3072]{1,0:T(8,128)}) %reduce-scatter.23.cloned.1.call-update) | async-done | bytes 393232 | tf_op jit(solution)/shard_map/reduce_scatter | solution.py:165
  1136.0 183.1 %reduce-scatter.29.cloned.1.call-done = f32[128,1024]{1,0:T(8,128)} async-done(((f32[4096,1024]{1,0:T(8,128)}), f32[128,1024]{1,0:T(8,128)}) %reduce-scatter.29.cloned.1.call-update) | async-done | bytes 524304 | tf_op jit(solution)/shard_map/reduce_scatter | solution.py:169
  1319.1 187.3 %reduce-scatter.27.cloned.1.call-done = f32[32,4096]{1,0:T(8,128)} async-done(((f32[1024,4096]{1,0:T(8,128)}), f32[32,4096]{1,0:T(8,128)}) %reduce-scatter.27.cloned.1.call-update) | async-done | bytes 524304 | tf_op jit(solution)/shard_map/reduce_scatter | solution.py:168
  (498 shorter events, 251.2 us)
Async XLA Ops:
  7.2 50.0 %all-gather.6.cloned.1.call-start = ((), (), s32[]{:S(2)}) async-start(), calls=%async_computation.10 | async-start | bytes 7864320 | tf_op jit(solution)/shard_map/all_gather | solution.py:27
  7.9 120.1 %all-gather.8.cloned.1.call-start = ((), (), s32[]{:S(2)}) async-start(), calls=%async_computation.11 | async-start | bytes 2621440 | tf_op jit(solution)/shard_map/all_gather | solution.py:28
  8.7 132.6 %all-gather.10.cloned.1.call-start = ((), (), s32[]{:S(2)}) async-start(), calls=%async_computation.12 | async-start | bytes 10485760 | tf_op jit(solution)/shard_map/all_gather | solution.py:29
  9.4 191.6 %all-gather.12.cloned.1.call-start = ((), (), s32[]{:S(2)}) async-start(), calls=%async_computation.13 | async-start | bytes 10485760 | tf_op jit(solution)/shard_map/all_gather | solution.py:30
  10.0 273.3 %reduce-scatter.13.cloned.1.call-start = ((), (), s32[]{:S(2)}) async-start(), calls=%async_computation.15 | async-start | bytes 1179648 | tf_op jit(solution)/shard_map/reduce_scatter | solution.py:142
  45.1 166.7 %copy-start.22 = (f32[32,1024]{1,0:T(8,128)}, f32[32,1024]{1,0:T(8,128)S(1)}, u32[]{:S(2)}) copy-start(f32[32,1024]{1,0:T(8,128)S(1)} %gather_fusion.3) | copy-start | bytes 393220
  219.9 129.5 %reduce-scatter.11.cloned.1.call-start = ((), (), s32[]{:S(2)}) async-start(), calls=%async_computation.14 | async-start | bytes 1179648 | tf_op jit(solution)/shard_map/reduce_scatter | solution.py:139
  242.6 393.9 %reduce-scatter.17.cloned.1.call-start = ((), (), s32[]{:S(2)}) async-start(), calls=%async_computation.17 | async-start | bytes 1179648 | tf_op jit(solution)/shard_map/reduce_scatter | solution.py:142
  572.1 130.8 %reduce-scatter.21.cloned.1.call-start = ((), (), s32[]{:S(2)}) async-start(), calls=%async_computation.19 | async-start | bytes 1179648 | tf_op jit(solution)/shard_map/reduce_scatter | solution.py:142
  581.3 187.6 %reduce-scatter.15.cloned.1.call-start = ((), (), s32[]{:S(2)}) async-start(), calls=%async_computation.16 | async-start | bytes 1179648 | tf_op jit(solution)/shard_map/reduce_scatter | solution.py:139
  584.4 250.6 %reduce-scatter.19.cloned.1.call-start = ((), (), s32[]{:S(2)}) async-start(), calls=%async_computation.18 | async-start | bytes 1179648 | tf_op jit(solution)/shard_map/reduce_scatter | solution.py:139
  589.3 379.0 %reduce-scatter.25.cloned.1.call-start = ((), (), s32[]{:S(2)}) async-start(), calls=%async_computation.21 | async-start | bytes 4325376 | tf_op jit(solution)/shard_map/reduce_scatter | solution.py:166
  593.2 242.7 %copy-start.62 = (bf16[32,1024]{1,0:T(8,128)(2,1)S(1)}, bf16[32,1024]{1,0:T(8,128)(2,1)}, u32[]{:S(2)}) copy-start(bf16[32,1024]{1,0:T(8,128)(2,1)} %copy-done.61) | copy-start | bytes 196612
  593.2 242.7 %copy-start.63 = (bf16[32,1024]{1,0:T(8,128)(2,1)S(1)}, bf16[32,1024]{1,0:T(8,128)(2,1)}, u32[]{:S(2)}) copy-start(bf16[32,1024]{1,0:T(8,128)(2,1)} %get-tuple-element.98) | copy-start | bytes 196612
  593.2 242.7 %copy-start.65 = (bf16[32,1024]{1,0:T(8,128)(2,1)S(1)}, bf16[32,1024]{1,0:T(8,128)(2,1)}, u32[]{:S(2)}) copy-start(bf16[32,1024]{1,0:T(8,128)(2,1)} %copy-done.64) | copy-start | bytes 196612
  593.2 242.7 %copy-start.66 = (bf16[32,1024]{1,0:T(8,128)(2,1)S(1)}, bf16[32,1024]{1,0:T(8,128)(2,1)}, u32[]{:S(2)}) copy-start(bf16[32,1024]{1,0:T(8,128)(2,1)} %reshape.451) | copy-start | bytes 196612
  593.2 242.7 %copy-start.67 = (bf16[32,1024]{1,0:T(8,128)(2,1)S(1)}, bf16[32,1024]{1,0:T(8,128)(2,1)}, u32[]{:S(2)}) copy-start(bf16[32,1024]{1,0:T(8,128)(2,1)} %convert.41) | copy-start | bytes 196612
  593.2 242.7 %copy-start.69 = (bf16[32,1024]{1,0:T(8,128)(2,1)S(1)}, bf16[32,1024]{1,0:T(8,128)(2,1)}, u32[]{:S(2)}) copy-start(bf16[32,1024]{1,0:T(8,128)(2,1)} %copy-done.68) | copy-start | bytes 196612
  593.2 542.8 %reduce-scatter.23.cloned.1.call-start = ((), (), s32[]{:S(2)}) async-start(), calls=%async_computation.20 | async-start | bytes 12976128 | tf_op jit(solution)/shard_map/reduce_scatter | solution.py:165
  593.8 248.5 %copy-start.72 = (bf16[32,1024]{1,0:T(8,128)(2,1)}, bf16[32,1024]{1,0:T(8,128)(2,1)S(1)}, u32[]{:S(2)}) copy-start(bf16[32,1024]{1,0:T(8,128)(2,1)S(1)} %reshape.459) | copy-start | bytes 196612
  594.2 248.1 %copy-start.70 = (bf16[32,1024]{1,0:T(8,128)(2,1)}, bf16[32,1024]{1,0:T(8,128)(2,1)S(1)}, u32[]{:S(2)}) copy-start(bf16[32,1024]{1,0:T(8,128)(2,1)S(1)} %reshape.455) | copy-start | bytes 196612
  637.5 204.9 %copy-start.74 = (bf16[32,1024]{1,0:T(8,128)(2,1)}, bf16[32,1024]{1,0:T(8,128)(2,1)S(1)}, u32[]{:S(2)}) copy-start(bf16[32,1024]{1,0:T(8,128)(2,1)S(1)} %convert.44) | copy-start | bytes 196612
  842.4 476.7 %reduce-scatter.29.cloned.1.call-start = ((), (), s32[]{:S(2)}) async-start(), calls=%async_computation.23 | async-start | bytes 17301504 | tf_op jit(solution)/shard_map/reduce_scatter | solution.py:169
  853.9 652.6 %reduce-scatter.27.cloned.1.call-start = ((), (), s32[]{:S(2)}) async-start(), calls=%async_computation.22 | async-start | bytes 17301504 | tf_op jit(solution)/shard_map/reduce_scatter | solution.py:168
  (142 other events, 1465.5 us)
Sparse Core Ops, SparseCore 0:
  9.6 47.5 all-gather.5
  58.8 22.5 all-gather.7
  83.0 58.2 all-gather.9
  142.7 58.2 all-gather.11
  220.0 63.2 reduce-scatter.12
  287.0 62.4 reduce-scatter.10
  572.2 64.2 reduce-scatter.16
  640.3 62.5 reduce-scatter.20
  706.3 62.5 reduce-scatter.14
  772.6 62.3 reduce-scatter.18
  837.8 130.4 reduce-scatter.24
  974.7 161.2 reduce-scatter.22
  1139.0 180.1 reduce-scatter.28
  1322.0 184.4 reduce-scatter.26
where the time goes:
time: 1520 us; the launch traced here: 1510 us
  waiting for transfers between devices  961 us (63%)
  blocking collectives  264 us (17%)
  matrix products  154 us (10%)
  local copies, waits for them, and re-layouts  63.5 us (4%)
  other arithmetic  53.5 us (4%)
  between operations  16.2 us (1%)
    reduce_scatter x3, waiting for transfers between devices, shards(): lax.psum_scatter(d_key_part.reshape(total, width), 'ctx', scatter_dimensi...  195 us
    reduce_scatter x1, waiting for transfers between devices, shards(): lax.psum_scatter(grad_up, ('ctx', 'fsdp'), scatter_dimension=0, tiled=True)  187 us
    reduce_scatter x1, waiting for transfers between devices, shards(): lax.psum_scatter(grad_down, ('ctx', 'fsdp'), scatter_dimension=0, tiled=T...  183 us
    reduce_scatter x1, waiting for transfers between devices, shards(): lax.psum_scatter(grad_qkv, ('ctx', 'fsdp'), scatter_dimension=0, tiled=True)  168 us
    reduce_scatter x3, waiting for transfers between devices, shards(): lax.psum_scatter(d_value_part.reshape(total, width), 'ctx', scatter_dimen...  135 us
    all_gather x3, blocking collectives, shards(): lax.all_gather(values_local, 'ctx', axis=0, tiled=True)  98.6 us
    all_gather x3, blocking collectives, shards(): lax.all_gather(keys_local, 'ctx', axis=0, tiled=True)  97.3 us
    all_gather x1, waiting for transfers between devices, fetch(): lax.all_gather(w_down, 'fsdp', axis=0, tiled=True)  54.8 us
  transfers between devices with their start and end apart: 14, of which 13 were waited for; matrix products, arithmetic and copies ran while one was open for 10% of the time, Pallas kernels for 0%

commit v1 on v0

--- a/solution.py
+++ b/solution.py
@@ -1,6 +1,10 @@
+import math
+
 import jax
 import jax.numpy as jnp
 from jax import lax
+from jax.experimental import pallas as pl
+from jax.experimental.pallas import tpu as pltpu
 from jax.sharding import PartitionSpec as P
 
 HEADS = 16
@@ -11,6 +15,8 @@
 EPSILON = 1e-06
 MASKED = -1e30
 HIGHEST = lax.Precision.HIGHEST
+BF16, F32 = jnp.bfloat16, jnp.float32
+VMEM_LIMIT = 56 * 2**20
 
 
 def rms_norm(values, gain):
@@ -183,6 +189,622 @@
     )
 
 
+def vmem_call(kernel, outs, smem, args, scratch=(), flops=0, name=None):
+    total = sum(a.size * a.dtype.itemsize for a in (*args, *outs))
+    return pl.pallas_call(
+        kernel,
+        out_shape=tuple(outs),
+        in_specs=[pl.BlockSpec(memory_space=pltpu.SMEM)] * len(smem)
+        + [pl.BlockSpec(memory_space=pltpu.VMEM)] * len(args),
+        out_specs=tuple(pl.BlockSpec(memory_space=pltpu.VMEM) for _ in outs),
+        scratch_shapes=list(scratch),
+        compiler_params=pltpu.CompilerParams(vmem_limit_bytes=VMEM_LIMIT),
+        cost_estimate=pl.CostEstimate(flops=flops, bytes_accessed=total, transcendentals=0),
+        name=name,
+    )(*smem, *args)
+
+
+def sds(shape, dtype):
+    return jax.ShapeDtypeStruct(shape, dtype)
+
+
+def mm(left, right):
+    return jnp.dot(left, right, preferred_element_type=F32)
+
+
+def mm_t(left, right):
+    return lax.dot_general(left, right, (((1,), (1,)), ((), ())), preferred_element_type=F32)
+
+
+def t_mm(left, right):
+    return lax.dot_general(left, right, (((0,), (0,)), ((), ())), preferred_element_type=F32)
+
+
+def exchange(x, axis, size, mask):
+    return lax.ppermute(x, axis, [(i, i ^ mask) for i in range(size)])
+
+
+def gather_kernel(deal, storage, base, tokens, cot, w_router, rowsx, cots, d_mlp, gate_out):
+    micros, tok_dev, width = tokens.shape
+    count = cots.shape[0]
+    per = count // micros
+    span = tok_dev // 2
+    index = storage[...]
+    local = index - base[0]
+    lanes = lax.broadcasted_iota(jnp.int32, (tok_dev, index.shape[1]), 1)
+    hit = lax.broadcasted_iota(jnp.int32, (tok_dev, index.shape[1]), 0) == local
+    rows = jnp.zeros((index.shape[1], width), F32)
+    cot_rows = jnp.zeros((index.shape[1], width), F32)
+    for micro in range(micros):
+        mine = (lanes >= micro * per) & (lanes < (micro + 1) * per)
+        pick = jnp.where(hit & mine, 1.0, 0.0).astype(BF16)
+        rows = rows + t_mm(pick, tokens[micro])
+        cot_rows = cot_rows + t_mm(pick, cot[micro])
+    rows, cot_rows = rows[:count], cot_rows[:count]
+    chunk = index // span
+    anchor = jnp.zeros_like(index)
+    for entry in range(deal.shape[0]):
+        anchor = jnp.where(chunk == entry, deal[entry], anchor)
+    place = (anchor * span + index % span) // BLOCK
+    rowsx[:count] = rows.astype(BF16)
+    rowsx[count:] = jnp.zeros((rowsx.shape[0] - count, width), BF16)
+    rowsx[count : count + 8, : index.shape[1]] = jnp.broadcast_to(
+        place.astype(F32), (8, index.shape[1])
+    ).astype(BF16)
+    cots[...] = cot_rows.astype(BF16)
+    gate = jax.nn.sigmoid(jnp.sum(rows * w_router[...], axis=1, keepdims=True))
+    d_mlp[...] = (gate * cot_rows).astype(BF16)
+    gate_out[...] = gate
+
+
+def slice_qkv_kernel(ids, w_qkv, *outs):
+    width = w_qkv.shape[1] // 3
+    part = width // 4
+    for k, out in enumerate(outs):
+        peer = ids[1] ^ k
+        for j in range(2):
+            for b in range(3):
+                start = pl.multiple_of(peer * part + (b * width + j * 128), 128)
+                out[:, (3 * j + b) * 128 : (3 * j + b + 1) * 128] = w_qkv[:, pl.ds(start, 128)]
+
+
+def slice_up_kernel(ids, w_up, *outs):
+    part = w_up.shape[1] // 4
+    for k, out in enumerate(outs):
+        out[...] = w_up[:, pl.ds(pl.multiple_of((ids[1] ^ k) * part, part), part)]
+
+
+def rms_factor(values):
+    return lax.rsqrt(jnp.mean(values * values, axis=-1, keepdims=True) + EPSILON)
+
+
+def qkv_kernel(ids, gain, r0, r1, r2, r3, w0, w1, w2, w3, *rest):
+    outs, (w_full, norm1, raw) = rest[:8], rest[8:]
+    c, f = ids[0], ids[1]
+    part = w0.shape[0]
+    count = norm1.shape[1]
+    for k, w in enumerate((w0, w1, w2, w3)):
+        w_full[pl.ds(pl.multiple_of((f ^ k) * part, part), part), :] = w[...]
+    for k, r in enumerate((r0, r1, r2, r3)):
+        rows = r[:count].astype(F32)
+        norm1[f ^ k] = (rows * rms_factor(rows) * gain[...]).astype(BF16)
+    for s in range(4):
+        raw[s] = mm(norm1[s], w_full[...]).astype(BF16)
+    places = (r0, r1, r2, r3)
+    for k in range(8):
+        target = c ^ k
+        s, j = target & 3, target >> 2
+        outs[k][:count] = raw[s, :, pl.ds(pl.multiple_of(j * 384, 128), 384)]
+        outs[k][count:, 128:] = jnp.zeros((8, 256), BF16)
+        for q in range(4):
+            @pl.when(s == (f ^ q))
+            def _():
+                outs[k][count:, :128] = places[q][count:, :128]
+
+
+def head_masks():
+    lanes = lax.broadcasted_iota(jnp.int32, (1, 128), 1)
+    low = jnp.where(lanes < 64, 1.0, 0.0)
+    return low, 1.0 - low
+
+
+def attend_kernel(*refs):
+    blocks, outs, (stack, probs, place_col) = refs[:8], refs[8:16], refs[16:]
+    count = outs[0].shape[0]
+    micros = stack.shape[0]
+    per = count // micros
+    total = stack.shape[1]
+    eye = lax.broadcasted_iota(jnp.int32, (count, 128), 0) == lax.broadcasted_iota(
+        jnp.int32, (count, 128), 1
+    )
+    for k, block in enumerate(blocks):
+        row = block[count : count + 8, :128].astype(F32)[0:1]
+        col = jnp.sum(jnp.where(eye, row, 0.0), axis=1, keepdims=True)
+        for m in range(micros):
+            stack[m, k * per : (k + 1) * per, :] = block[m * per : (m + 1) * per, :]
+            place_col[m, k * per : (k + 1) * per, :] = jnp.broadcast_to(
+                col[m * per : (m + 1) * per], (per, 128)
+            )
+    big_eye = lax.broadcasted_iota(jnp.int32, (total, total), 0) == lax.broadcasted_iota(
+        jnp.int32, (total, total), 1
+    )
+    masks = head_masks()
+    for m in range(micros):
+        q, k, v = stack[m, :, :128], stack[m, :, 128:256], stack[m, :, 256:384]
+        mine = place_col[m, :, 0:1]
+        theirs = jnp.sum(jnp.where(big_eye, mine, 0.0), axis=0, keepdims=True)
+        visible = theirs <= mine
+        attended = jnp.zeros((total, 128), F32)
+        for h in range(2):
+            scores = mm_t(q * masks[h].astype(BF16), k) * (HEAD_DIM**-0.5)
+            scores = jnp.where(visible, scores, MASKED)
+            top = jnp.max(scores, axis=1, keepdims=True)
+            grown = jnp.exp(scores - top)
+            weight = grown / jnp.sum(grown, axis=1, keepdims=True)
+            probs[2 * m + h] = weight
+            attended = attended + mm(weight.astype(BF16), v) * masks[h]
+        low = attended.astype(BF16)
+        for k in range(8):
+            outs[k][m * per : (m + 1) * per, :] = low[k * per : (k + 1) * per]
+
+
+def split_sum(ids, full, send, keep):
+    f = ids[1]
+    send[0] = full[f ^ 1].astype(BF16)
+    send[1] = full[f ^ 3].astype(BF16)
+    keep[0] = full[f]
+    keep[1] = full[f ^ 2]
+
+
+def out_kernel(ids, w_out, b0, b1, b2, b3, b4, b5, b6, b7, attended, send, keep, full):
+    c = ids[0]
+    for k, block in enumerate((b0, b1, b2, b3, b4, b5, b6, b7)):
+        target = c ^ k
+        s, j = target & 3, target >> 2
+        attended[s, :, pl.ds(pl.multiple_of(j * 128, 128), 128)] = block[...]
+    for s in range(4):
+        full[s] = mm(attended[s], w_out[...])
+    split_sum(ids, full, send, keep)
+
+
+def add_kernel(keep, received, send2, keep2):
+    send2[...] = (keep[1] + received[1].astype(F32)).astype(BF16)
+    keep2[...] = keep[0] + received[0].astype(F32)
+
+
+def mid_kernel(keep, received, rowsx, gain, attn, norm2):
+    count = keep.shape[0]
+    value = keep[...] + received[...].astype(F32)
+    attn[...] = value
+    mid = rowsx[:count].astype(F32) + value
+    norm2[...] = (mid * rms_factor(mid) * gain[...]).astype(BF16)
+
+
+def mlp_kernel(
+    ids, n0, n1, n2, n3, m0, m1, m2, m3, u0, u1, u2, u3, w_down,
+    norm2, d_mlp, act, d_hidden, send, keep, w_up,
+):
+    f = ids[1]
+    part = u0.shape[0]
+    count = n0.shape[0]
+    for k, u in enumerate((u0, u1, u2, u3)):
+        w_up[pl.ds(pl.multiple_of((f ^ k) * part, part), part), :] = u[...]
+    for k, (n, m) in enumerate(((n0, m0), (n1, m1), (n2, m2), (n3, m3))):
+        rows = slice(k * count, (k + 1) * count)
+        norm2[rows] = n[...]
+        d_mlp[rows] = m[...]
+        hidden = mm(n[...], w_up[...])
+        d_act = mm_t(m[...], w_down[...])
+        phi = 0.5 * (1.0 + lax.erf(hidden * (0.5**0.5)))
+        act[rows] = (hidden * phi).astype(BF16)
+        slope = phi + hidden * jnp.exp(-0.5 * hidden * hidden) * ((2.0 * math.pi) ** -0.5)
+        low = (d_act * slope).astype(BF16)
+        d_hidden[rows] = low
+        d_norm2 = mm_t(low, w_up[...])
+        if k % 2:
+            send[k // 2] = d_norm2.astype(BF16)
+        else:
+            keep[k // 2] = d_norm2
+
+
+def mlp_out_kernel(act, w_down, send, keep):
+    count = send.shape[1]
+    for k in range(4):
+        part = mm(act[k * count : (k + 1) * count], w_down[...])
+        if k % 2:
+            send[k // 2] = part.astype(BF16)
+        else:
+            keep[k // 2] = part
+
+
+def store_block(k, send, keep, where, value):
+    if k % 2:
+        send[(k // 2, *where)] = value.astype(BF16)
+    else:
+        keep[(k // 2, *where)] = value
+
+
+def grad_mlp_kernel(ids, norm2, d_hidden, act, d_mlp, send, keep):
+    c, f = ids[0], ids[1]
+    for k in range(8):
+        start = pl.multiple_of((c ^ k) * 128, 128)
+        up = t_mm(norm2[:, pl.ds(start, 128)], d_hidden[...])
+        for q in range(4):
+            rows = pl.ds(pl.multiple_of((f ^ q) * 32, 32), 32)
+            store_block(k, send, keep, (rows, slice(None)), up[q * 32 : (q + 1) * 32])
+        down = t_mm(act[:, pl.ds(start, 128)], d_mlp[...])
+        store_block(k, send, keep, (slice(128, 256), slice(None)), down)
+
+
+def d_attn_kernel(keep, received, attn, rowsx, cots, gate, gain, d_mid_out, d_attn, grad_gain):
+    count = keep.shape[0]
+    mid = rowsx[:count].astype(F32) + attn[...]
+    r2 = rms_factor(mid)
+    d_norm2 = keep[...] + received[...].astype(F32)
+    t2 = d_norm2 * gain[...]
+    d_mid = r2 * t2 - mid * (r2 * r2 * r2) * jnp.mean(t2 * mid, axis=1, keepdims=True)
+    d_mid_out[...] = d_mid
+    d_attn[...] = (gate[...] * cots[...].astype(F32) + d_mid).astype(BF16)
+    grad_gain[...] = jnp.sum(d_norm2 * mid * r2, axis=0, keepdims=True)
+
+
+def d_attended_kernel(ids, w_out, d0, d1, d2, d3, *rest):
+    outs, (d_attn, d_att) = rest[:8], rest[8:]
+    c, f = ids[0], ids[1]
+    for k, d in enumerate((d0, d1, d2, d3)):
+        d_attn[f ^ k] = d[...]
+        d_att[f ^ k] = mm_t(d[...], w_out[...]).astype(BF16)
+    for k in range(8):
+        target = c ^ k
+        s, j = target & 3, target >> 2
+        outs[k][...] = d_att[s, :, pl.ds(pl.multiple_of(j * 128, 128), 128)]
+
+
+def attend_back_kernel(*refs):
+    blocks, (stack, probs), outs, (d_stack,) = refs[:8], refs[8:10], refs[10:18], refs[18:]
+    micros = stack.shape[0]
+    count = outs[0].shape[0]
+    per = count // micros
+    total = stack.shape[1]
+    masks = head_masks()
+    for m in range(micros):
+        for k, block in enumerate(blocks):
+            d_stack[k * per : (k + 1) * per, :] = block[m * per : (m + 1) * per, :]
+        q, k, v = stack[m, :, :128], stack[m, :, 128:256], stack[m, :, 256:384]
+        d_out = d_stack[...]
+        d_q = jnp.zeros((total, 128), F32)
+        d_k = jnp.zeros((total, 128), F32)
+        d_v = jnp.zeros((total, 128), F32)
+        for h in range(2):
+            weight = probs[2 * m + h]
+            d_probs = mm_t(d_out * masks[h].astype(BF16), v)
+            inner = jnp.sum(weight * d_probs, axis=1, keepdims=True)
+            d_scores = (weight * (d_probs - inner)).astype(BF16)
+            d_q = d_q + mm(d_scores, k) * masks[h]
+            d_k = d_k + t_mm(d_scores, q) * masks[h]
+            d_v = d_v + t_mm(weight.astype(BF16), d_out) * masks[h]
+        d_q = (d_q * (HEAD_DIM**-0.5)).astype(BF16)
+        d_k = (d_k * (HEAD_DIM**-0.5)).astype(BF16)
+        d_v = d_v.astype(BF16)
+        for t in range(8):
+            rows, source = slice(m * per, (m + 1) * per), slice(t * per, (t + 1) * per)
+            outs[t][rows, :128] = d_q[source]
+            outs[t][rows, 128:256] = d_k[source]
+            outs[t][rows, 256:384] = d_v[source]
+
+
+def d_norm1_kernel(
+    ids, w_full, r0, r1, r2, r3, b0, b1, b2, b3, b4, b5, b6, b7,
+    d_qkv, send, keep, grad_gain, full,
+):
+    c, f = ids[0], ids[1]
+    count = d_qkv.shape[1]
+    for k, block in enumerate((b0, b1, b2, b3, b4, b5, b6, b7)):
+        target = c ^ k
+        s, j = target & 3, target >> 2
+        d_qkv[s, :, pl.ds(pl.multiple_of(j * 384, 128), 384)] = block[...]
+    for s in range(4):
+        full[s] = mm_t(d_qkv[s], w_full[...])
+    split_sum(ids, full, send, keep)
+    total = jnp.zeros((1, w_full.shape[0]), F32)
+    for k, r in enumerate((r0, r1, r2, r3)):
+        rows = r[:count].astype(F32)
+        total = total + jnp.sum(full[f ^ k] * (rows * rms_factor(rows)), axis=0, keepdims=True)
+    grad_gain[...] = total
+
+
+def grad_out_kernel(ids, attended, d_attn, send, keep, full):
+    c = ids[0]
+    total = jnp.zeros(full.shape, F32)
+    for s in range(4):
+        total = total + t_mm(attended[s], d_attn[s])
+    full[...] = total
+    for k in range(8):
+        rows = full[pl.ds(pl.multiple_of((c ^ k) * 32, 32), 32), :]
+        if k % 2:
+            send[k // 2] = rows.astype(BF16)
+        else:
+            keep[k // 2] = rows
+
+
+def grad_qkv_kernel(ids, norm1, d_qkv, gains, send, keep):
+    c, f = ids[0], ids[1]
+    for k in range(8):
+        start = pl.multiple_of((c ^ k) * 128, 128)
+        part = t_mm(norm1[:, pl.ds(start, 128)], d_qkv[...])
+        for q in range(4):
+            rows = pl.ds(pl.multiple_of((f ^ q) * 32, 32), 32)
+            store_block(k, send, keep, (rows, slice(None)), part[q * 32 : (q + 1) * 32])
+        for v in range(3):
+            row = jnp.broadcast_to(gains[v : v + 1, pl.ds(start, 128)], (16, 128))
+            store_block(k, send, keep, (slice(128, 144), slice(v * 128, v * 128 + 128)), row)
+            store_block(
+                k, send, keep, (slice(128, 144), slice(384 + v * 128, 512 + v * 128)),
+                jnp.zeros((16, 128), F32),
+            )
+
+
+def place_rows(storage, base, micro, per, source, rows, out):
+    tok_dev = source.shape[0]
+    index = storage[...] - base[0]
+    lanes = lax.broadcasted_iota(jnp.int32, (tok_dev, index.shape[1]), 1)
+    hit = lax.broadcasted_iota(jnp.int32, (tok_dev, index.shape[1]), 0) == index
+    mine = (lanes >= micro * per) & (lanes < (micro + 1) * per)
+    pick = jnp.where(hit & mine, 1.0, 0.0)
+    routed = jnp.sum(pick, axis=1, keepdims=True) > 0.5
+    placed = mm(pick.astype(BF16), rows)
+    out[...] = jnp.where(routed, placed, source[...].astype(F32)).astype(BF16)
+
+
+def output_kernel(
+    base, storage, keep, received, attn, rowsx, cots, gate, tokens,
+    output, d_logit_out, grad_router, padded,
+):
+    count = keep.shape[0]
+    micros = tokens.shape[0]
+    branch = attn[...] + keep[...] + received[...].astype(F32)
+    rows = rowsx[:count].astype(F32)
+    d_logit = (
+        jnp.sum(cots[...].astype(F32) * branch, axis=1, keepdims=True)
+        * gate[...]
+        * (1.0 - gate[...])
+    )
+    d_logit_out[...] = d_logit
+    grad_router[...] = jnp.sum(rows * d_logit, axis=0, keepdims=True)
+    padded[...] = jnp.zeros(padded.shape, BF16)
+    padded[:count] = (rows + gate[...] * branch).astype(BF16)
+    for micro in range(micros):
+        place_rows(
+            storage, base, micro, count // micros, tokens.at[micro], padded[...], output.at[micro]
+        )
+
+
+def input_grad_kernel(
+    base, storage, keep, received, d_mid, rowsx, cots, d_logit, w_router, gain, cot,
+    input_grad, padded,
+):
+    count = keep.shape[0]
+    micros = cot.shape[0]
+    rows = rowsx[:count].astype(F32)
+    r1 = rms_factor(rows)
+    t1 = (keep[...] + received[...].astype(F32)) * gain[...]
+    d_rows = (
+        cots[...].astype(F32)
+        + d_mid[...]
+        + r1 * t1
+        - rows * (r1 * r1 * r1) * jnp.mean(t1 * rows, axis=1, keepdims=True)
+        + d_logit[...] * w_router[...]
+    )
+    padded[...] = jnp.zeros(padded.shape, BF16)
+    padded[:count] = d_rows.astype(BF16)
+    for micro in range(micros):
+        place_rows(
+            storage, base, micro, count // micros, cot.at[micro], padded[...], input_grad.at[micro]
+        )
+
+
+def join_up_kernel(ids, p0, p1, p2, p3, out):
+    part = p0.shape[1]
+    for k, piece in enumerate((p0, p1, p2, p3)):
+        out[:, pl.ds(pl.multiple_of((ids[1] ^ k) * part, part), part)] = piece[...]
+
+
+def join_qkv_kernel(ids, p0, p1, p2, p3, v0, v1, v2, v3, out, vectors):
+    width = out.shape[1] // 3
+    part = width // 4
+    for k, piece in enumerate((p0, p1, p2, p3)):
+        for j in range(2):
+            for b in range(3):
+                start = pl.multiple_of((ids[1] ^ k) * part + (b * width + j * 128), 128)
+                out[:, pl.ds(start, 128)] = piece[:, (3 * j + b) * 128 : (3 * j + b + 1) * 128]
+    vectors[...] = v0[...] + v1[...] + v2[...] + v3[...]
+
+
+def scatter_sum(send, keep):
+    first = keep + exchange(send, "ctx", 8, 1).astype(F32)
+    second = first[:2] + exchange(first[2:].astype(BF16), "ctx", 8, 4).astype(F32)
+    return second[0] + exchange(second[1].astype(BF16), "ctx", 8, 2).astype(F32)
+
+
+def row_sum(send, keep):
+    received = exchange(send, "fsdp", 4, 1)
+    count, width = keep.shape[1:]
+    send2, keep2 = vmem_call(
+        add_kernel, (sds((count, width), BF16), sds((count, width), F32)), (), (keep, received),
+        name="add_rows",
+    )
+    return keep2, exchange(send2, "fsdp", 4, 2)
+
+
+def row_gather(mine):
+    across = exchange(mine, "fsdp", 4, 2)
+    beside = exchange(mine, "fsdp", 4, 1)
+    return mine, beside, across, exchange(across, "fsdp", 4, 1)
+
+
+def swap_blocks(blocks):
+    return (blocks[0], *(exchange(b, "ctx", 8, k) for k, b in enumerate(blocks) if k))
+
+
+def shards_8x4(
+    tokens, w_router, gain_attn, w_qkv, w_out, gain_mlp, w_up, w_down, routed, deal, cotangent
+):
+    micros, tok_dev, width = tokens.shape[0], tokens.shape[2], tokens.shape[3]
+    per = routed.shape[2]
+    count = micros * per
+    total = 8 * per
+    part = width // 4
+    hidden = w_down.shape[0]
+    c, f = lax.axis_index("ctx"), lax.axis_index("fsdp")
+    ids = jnp.stack([c, f]).astype(jnp.int32)
+    base = (c * tok_dev).astype(jnp.int32).reshape(1)
+    storage = jnp.pad(routed.reshape(1, count), ((0, 0), (0, 128 - count)), constant_values=-1)
+    tok, cot = tokens[:, 0], cotangent[:, 0]
+    w_router, gain_attn, gain_mlp = (
+        w_router.reshape(1, width), gain_attn.reshape(1, width), gain_mlp.reshape(1, width),
+    )
+    rows_bf, rows_f = sds((count, width), BF16), sds((count, width), F32)
+    pair_bf, pair_f = sds((2, count, width), BF16), sds((2, count, width), F32)
+
+    w_parts = vmem_call(slice_qkv_kernel, (sds((part, 768), BF16),) * 4, (ids,), (w_qkv,), name="slice_qkv")
+    w_parts = (w_parts[0], *(exchange(w_parts[k], "fsdp", 4, k) for k in (1, 2, 3)))
+    rowsx, cots, d_mlp_mine, gate = pl.pallas_call(
+        gather_kernel,
+        out_shape=(sds((count + 8, width), BF16), rows_bf, rows_bf, sds((count, 1), F32)),
+        in_specs=[
+            pl.BlockSpec(memory_space=pltpu.SMEM),
+            pl.BlockSpec(memory_space=pltpu.VMEM),
+            pl.BlockSpec(memory_space=pltpu.SMEM),
+        ]
+        + [pl.BlockSpec(memory_space=pltpu.VMEM)] * 3,
+        out_specs=(pl.BlockSpec(memory_space=pltpu.VMEM),) * 4,
+        compiler_params=pltpu.CompilerParams(vmem_limit_bytes=VMEM_LIMIT),
+        name="gather_rows",
+    )(deal, storage, base, tok, cot, w_router)
+    rows_all = row_gather(rowsx)
+    *blocks, w_full, norm1 = vmem_call(
+        qkv_kernel,
+        (sds((count + 8, 384), BF16),) * 8 + (sds((width, 768), BF16), sds((4, count, width), BF16)),
+        (ids,), (gain_attn, *rows_all, *w_parts), scratch=[pltpu.VMEM((4, count, 768), BF16)],
+        flops=2 * 4 * count * width * 768, name="qkv",
+    )
+    blocks = swap_blocks(blocks)
+    up_parts = vmem_call(slice_up_kernel, (sds((part, hidden), BF16),) * 4, (ids,), (w_up,), name="slice_up")
+    up_parts = (up_parts[0], *(exchange(up_parts[k], "fsdp", 4, k) for k in (1, 2, 3)))
+    d_mlp_all = row_gather(d_mlp_mine)
+    *heads, stack, probs = vmem_call(
+        attend_kernel,
+        (sds((count, 128), BF16),) * 8
+        + (sds((micros, total, 384), BF16), sds((2 * micros, total, total), F32)),
+        (), blocks, scratch=[pltpu.VMEM((micros, total, 128), F32)],
+        flops=2 * micros * 2 * total * total * 256, name="attend",
+    )
+    heads = swap_blocks(heads)
+    attended, send, keep = vmem_call(
+        out_kernel, (sds((4, count, part), BF16), pair_bf, pair_f), (ids,), (w_out, *heads),
+        scratch=[pltpu.VMEM((4, count, width), F32)], flops=2 * 4 * count * part * width,
+        name="attn_out",
+    )
+    keep, received = row_sum(send, keep)
+    attn, norm2 = vmem_call(
+        mid_kernel, (rows_f, rows_bf), (), (keep, received, rowsx, gain_mlp), name="mid"
+    )
+    norm2_all = row_gather(norm2)
+    norm2_full, d_mlp_full, act, d_hidden, send, keep = vmem_call(
+        mlp_kernel,
+        (sds((4 * count, width), BF16), sds((4 * count, width), BF16))
+        + (sds((4 * count, hidden), BF16), sds((4 * count, hidden), BF16), pair_bf, pair_f),
+        (ids,), (*norm2_all, *d_mlp_all, *up_parts, w_down),
+        scratch=[pltpu.VMEM((width, hidden), BF16)], flops=3 * 2 * 4 * count * width * hidden,
+        name="mlp",
+    )
+    keep, received = row_sum(send, keep)
+    send_m, keep_m = vmem_call(
+        mlp_out_kernel, (pair_bf, pair_f), (), (act, w_down),
+        flops=2 * 4 * count * width * hidden, name="mlp_out",
+    )
+    send_g, keep_g = vmem_call(
+        grad_mlp_kernel, (sds((4, 256, width), BF16), sds((4, 256, width), F32)), (ids,),
+        (norm2_full, d_hidden, act, d_mlp_full), flops=2 * 2 * 4 * count * width * hidden,
+        name="grad_mlp",
+    )
+    d_mid, d_attn, grad_gain_mlp = vmem_call(
+        d_attn_kernel, (rows_f, rows_bf, sds((1, width), F32)), (),
+        (keep, received, attn, rowsx, cots, gate, gain_mlp), name="d_attn",
+    )
+    d_attn_all = row_gather(d_attn)
+    *d_heads, d_attn_full = vmem_call(
+        d_attended_kernel, (sds((count, 128), BF16),) * 8 + (sds((4, count, width), BF16),),
+        (ids,), (w_out, *d_attn_all), scratch=[pltpu.VMEM((4, count, part), BF16)],
+        flops=2 * 4 * count * part * width, name="d_attended",
+    )
+    d_heads = swap_blocks(d_heads)
+    d_blocks = vmem_call(
+        attend_back_kernel, (sds((count, 384), BF16),) * 8, (), (*d_heads, stack, probs),
+        scratch=[pltpu.VMEM((total, 128), BF16)], flops=2 * micros * 2 * total * total * 512,
+        name="attend_back",
+    )
+    d_blocks = swap_blocks(d_blocks)
+    d_qkv, send, keep, grad_gain_attn = vmem_call(
+        d_norm1_kernel, (sds((4, count, 768), BF16), pair_bf, pair_f, sds((1, width), F32)),
+        (ids,), (w_full, *rows_all, *d_blocks), scratch=[pltpu.VMEM((4, count, width), F32)],
+        flops=2 * 4 * count * 768 * width, name="d_norm1",
+    )
+    keep, received = row_sum(send, keep)
+
+    keep_m, received_m = row_sum(send_m, keep_m)
+    output, d_logit, grad_router = pl.pallas_call(
+        output_kernel,
+        out_shape=(sds(tok.shape, BF16), sds((count, 1), F32), sds((1, width), F32)),
+        in_specs=[pl.BlockSpec(memory_space=pltpu.SMEM)]
+        + [pl.BlockSpec(memory_space=pltpu.VMEM)] * 8,
+        out_specs=(pl.BlockSpec(memory_space=pltpu.VMEM),) * 3,
+        scratch_shapes=[pltpu.VMEM((128, width), BF16)],
+        compiler_params=pltpu.CompilerParams(vmem_limit_bytes=VMEM_LIMIT),
+        name="output",
+    )(base, storage, keep_m, received_m, attn, rowsx, cots, gate, tok)
+    (input_grad,) = vmem_call(
+        input_grad_kernel, (sds(cot.shape, BF16),), (base,),
+        (storage, keep, received, d_mid, rowsx, cots, d_logit, w_router, gain_attn, cot),
+        scratch=[pltpu.VMEM((128, width), BF16)], name="input_grad",
+    )
+
+    sum_mlp = scatter_sum(send_g, keep_g)
+    up_chunks = sum_mlp[:128].reshape(4, 32, hidden)
+    up_chunks = (up_chunks[0], *(exchange(up_chunks[k], "fsdp", 4, k) for k in (1, 2, 3)))
+    (grad_up,) = vmem_call(join_up_kernel, (sds((32, 4 * hidden), F32),), (ids,), up_chunks, name="join_up")
+    to_owner = [(4 * a + b, 4 * (2 * b + a // 4) + a % 4) for a in range(8) for b in range(4)]
+    grad_down = lax.ppermute(sum_mlp[128:], ("ctx", "fsdp"), to_owner)
+    send_o, keep_o = vmem_call(
+        grad_out_kernel, (sds((4, 32, width), BF16), sds((4, 32, width), F32)), (ids,),
+        (attended, d_attn_full), scratch=[pltpu.VMEM((part, width), F32)],
+        flops=2 * 4 * count * part * width, name="grad_out",
+    )
+    grad_out = lax.ppermute(scatter_sum(send_o, keep_o), ("ctx", "fsdp"), to_owner)
+    gains = jnp.concatenate([grad_router, grad_gain_attn, grad_gain_mlp], axis=0)
+    send_q, keep_q = vmem_call(
+        grad_qkv_kernel, (sds((4, 144, 768), BF16), sds((4, 144, 768), F32)), (ids,),
+        (norm1.reshape(4 * count, width), d_qkv.reshape(4 * count, 768), gains),
+        flops=2 * 4 * count * width * 768, name="grad_qkv",
+    )
+    sum_qkv = scatter_sum(send_q, keep_q)
+    vector = sum_qkv[128:136]
+    pieces = tuple(sum_qkv[32 * k : 32 * k + 32] for k in range(4))
+    pieces = tuple(
+        p if k == 0 else exchange(jnp.concatenate([p, vector], axis=0), "fsdp", 4, k)
+        for k, p in enumerate(pieces)
+    )
+    grad_qkv, vectors = vmem_call(
+        join_qkv_kernel, (sds((32, 3 * width), F32), sds((8, 768), F32)), (ids,),
+        (*(p[:32] for p in pieces), vector, *(p[32:] for p in pieces[1:])), name="join_qkv",
+    )
+    vectors = lax.dynamic_slice_in_dim(vectors[0, :384].reshape(3, 128), f * 32, 32, axis=1)
+    return (
+        output[:, None], input_grad[:, None], vectors[0], vectors[1], grad_qkv, grad_out,
+        vectors[2], grad_up, grad_down,
+    )
+
+
 def solution(mesh):
     placed = (
         P(None, "fsdp", "ctx", None),
@@ -197,8 +819,9 @@
         P(),
         P(None, "fsdp", "ctx", None),
     )
+    fits = mesh.shape["ctx"] == 8 and mesh.shape["fsdp"] == 4
     return jax.shard_map(
-        shards,
+        shards_8x4 if fits else shards,
         mesh=mesh,
         in_specs=placed,
         out_specs=(

time: 1520 us -> 389 us (0.26)
  waiting for transfers between devices: 961 us -> 191 us
  blocking collectives: 264 us -> 0 us
  matrix products: 154 us -> 0 us
  Pallas kernels: 0 us -> 87.5 us
  starting transfers between devices: 1.18 us -> 73.9 us
  other arithmetic: 53.5 us -> 6.48 us
  local copies, waits for them, and re-layouts: 63.5 us -> 28.2 us
    reduce_scatter x10 -> x0, waiting for transfers between devices: 884 us -> none  [the longest x3 195 us: shards(): lax.psum_scatter(d_key_part.reshape(total, width), 'ctx', scatter_dimensi...]
    all_gather x7 -> x0, blocking collectives: 222 us -> none  [the longest x3 98.6 us: shards(): lax.all_gather(values_local, 'ctx', axis=0, tiled=True)]
    ppermute x0 -> x71, waiting for transfers between devices: none -> 191 us  [the longest x69 185 us: exchange(): return lax.ppermute(x, axis, [(i, i ^ mask) for i in range(size)])]
    dot_general x52 -> x0, matrix products: 154 us -> none  [the longest x4 26.5 us: outer_sum(): lax.dot_general(left, right, (((0,), (0,)), ((), ())), preferred_element_...]
    pallas_call x0 -> x24, Pallas kernels: none -> 87.5 us  [the longest x22 80.4 us: vmem_call(): pl.pallas_call(kernel, out_shape=tuple(outs), in_specs=[pl.BlockSpec(memo...]
    all_gather x4 -> x0, waiting for transfers between devices: 74.6 us -> none  [the longest x1 54.8 us: fetch(): lax.all_gather(w_down, 'fsdp', axis=0, tiled=True)]
    ppermute x0 -> x71, starting transfers between devices: none -> 73.9 us  [the longest x69 69.4 us: exchange(): return lax.ppermute(x, axis, [(i, i ^ mask) for i in range(size)])]
    unnamed x1 -> x0, blocking collectives: 41.4 us -> none
  transfers between devices with their start and end apart: 14 -> 71, of which waited for: 13 -> 26; matrix products, arithmetic and copies ran while one was open for 10% -> 5% of each run, Pallas kernels for 0% -> 15%
where the time goes in v1:
time: 389 us; the launch traced here: 388 us
  waiting for transfers between devices  191 us (49%)
  Pallas kernels  87.5 us (22%)
  starting transfers between devices  73.9 us (19%)
  local copies, waits for them, and re-layouts  28.2 us (7%)
  other arithmetic  6.48 us (2%)
    ppermute x69, waiting for transfers between devices, exchange(): return lax.ppermute(x, axis, [(i, i ^ mask) for i in range(size)])  185 us
    pallas_call x22, Pallas kernels, vmem_call(): pl.pallas_call(kernel, out_shape=tuple(outs), in_specs=[pl.BlockSpec(memo...  80.4 us
    ppermute x69, starting transfers between devices, exchange(): return lax.ppermute(x, axis, [(i, i ^ mask) for i in range(size)])  69.4 us
    unnamed x132, local copies, waits for them, and re-layouts  15.2 us
  transfers between devices with their start and end apart: 71, of which 26 were waited for; matrix products, arithmetic and copies ran while one was open for 5% of the time, Pallas kernels for 15%

profile of v1, /device:TPU:4, one launch (start us, length us, event | category | flops | bytes accessed | tf_op | source)
XLA Modules:
  0.0 387.9 jit_solution(6836767841389221753)
XLA Ops:
  2.0 3.4 gather_rows.1
  13.9 8.6 %collective-permute-done.4.w2 = bf16[256,768]{1,0:T(8,128)(2,1)S(1)} collective-permute-done((bf16[256,768]{1,0:T(8,128)(2,1)}, bf16[256,768]{1,0:T(8,128)(2,1)S(1)}, u32[]{:S(2)}, u32[]{:S(2)}) %collective-permute-start.4) | collective-permute-done | bytes 393248 | tf_op jit(solution)/shard_map/ppermute | solution.py:224
  22.5 7.6 %collective-permute-done.5.w3 = bf16[256,768]{1,0:T(8,128)(2,1)S(1)} collective-permute-done((bf16[256,768]{1,0:T(8,128)(2,1)}, bf16[256,768]{1,0:T(8,128)(2,1)S(1)}, u32[]{:S(2)}, u32[]{:S(2)}) %collective-permute-start.5) | collective-permute-done | bytes 393248 | tf_op jit(solution)/shard_map/ppermute | solution.py:224
  30.9 5.2 %qkv.1 = (bf16[104,384]{1,0:T(8,128)(2,1)}, bf16[104,384]{1,0:T(8,128)(2,1)}, bf16[104,384]{1,0:T(8,128)(2,1)}, bf16[104,384]{1,0:T(8,128)(2,1)}, bf16[104,384]{...) custom-call(s32[2]{0:T(128)} %pad_add_fusion.ids, ...), custom_call_target="tpu_custom_call" | custom-call | flops 603979776 | bytes 5427200 | tf_op jit(solution)/shard_map/qkv/pallas_call | solution.py:194
  42.6 3.5 collective-permute-start.11
  47.3 4.4 %collective-permute-done.9.refs_4_ = bf16[104,384]{1,0:T(8,128)(2,1)S(1)} collective-permute-done((bf16[104,384]{1,0:T(8,128)(2,1)}, bf16[104,384]{1,0:T(8,128)(2,1)S(1)}, u32[]{:S(2)}, u32[]{:S(2)}) %collective-permute-start.9) | collective-permute-done | bytes 79904 | tf_op jit(solution)/shard_map/ppermute | solution.py:224
  55.4 3.9 %attend.1 = (bf16[96,128]{1,0:T(8,128)(2,1)}, bf16[96,128]{1,0:T(8,128)(2,1)}, bf16[96,128]{1,0:T(8,128)(2,1)}, bf16[96,128]{1,0:T(8,128)(2,1)}, bf16[96,128]{1,...) custom-call(bf16[104,384]{1,0:T(8,128)(2,1)} %get-tuple-element.102., ...), custom_call_target="tpu_custom_call" | custom-call | flops 201326592 | bytes 2998272 | tf_op jit(solution)/shard_map/attend/pallas_call | solution.py:194
  60.4 3.4 collective-permute-start.14
  95.7 23.4 %collective-permute-done.23.n2 = bf16[96,1024]{1,0:T(8,128)(2,1)S(1)} collective-permute-done((bf16[96,1024]{1,0:T(8,128)(2,1)}, bf16[96,1024]{1,0:T(8,128)(2,1)S(1)}, u32[]{:S(2)}, u32[]{:S(2)}) %collective-permute-start.23) | collective-permute-done | bytes 196640 | tf_op jit(solution)/shard_map/ppermute | solution.py:224
  121.3 11.1 %mlp.1 = (bf16[384,1024]{1,0:T(8,128)(2,1)}, bf16[384,1024]{1,0:T(8,128)(2,1)}, bf16[384,1024]{1,0:T(8,128)(2,1)}, bf16[384,1024]{1,0:T(8,128)(2,1)}, bf16[2,96,...) custom-call(s32[2]{0:T(128)} %pad_add_fusion.ids, bf16[96,1024]{1,0:T(8,128)(2,1)} %get-tuple-element.122.n0, ...), custom_call_target="tpu_custom_call" | custom-call | flops 2415919104 | bytes 10092544 | tf_op jit(solution)/shard_map/mlp/pallas_call | solution.py:194
  138.5 4.0 %mlp_out.1 = (bf16[2,96,1024]{2,1,0:T(8,128)(2,1)}, f32[2,96,1024]{2,1,0:T(8,128)}) custom-call(bf16[384,1024]{1,0:T(8,128)(2,1)} %get-tuple-element.128.act, bf16[1024,1024]{1,0:T(8,128)(2,1)} %w_down.3), custom_call_target="tpu_custom_call" | custom-call | flops 805306368 | bytes 4063232 | tf_op jit(solution)/shard_map/mlp_out/pallas_call | solution.py:194
  148.8 7.1 %grad_mlp.1 = (bf16[4,256,1024]{2,1,0:T(8,128)(2,1)}, f32[4,256,1024]{2,1,0:T(8,128)}) custom-call(s32[2]{0:T(128)} %pad_add_fusion.ids, bf16[384,1024]{1,0:T(8,128)(2,1)} %get-tuple-element.180.norm2, bf16[384,1024]{1,0:T(8,128)(2,1)} %get-tuple-element.181.d_hidden, bf16[384,1024]{1,0:T(8,128)(2,1)} %get-tuple-element.128.act, ...), custom_call_target="tpu_custom_call" | custom-call | flops 1610612736 | bytes 9437184 | tf_op jit(solution)/shard_map/grad_mlp/pallas_call | solution.py:194
  168.6 35.1 %collective-permute-done.38.refs_1_ = bf16[96,128]{1,0:T(8,128)(2,1)S(1)} collective-permute-done((bf16[96,128]{1,0:T(8,128)(2,1)}, bf16[96,128]{1,0:T(8,128)(2,1)S(1)}, u32[]{:S(2)}, u32[]{:S(2)}) %collective-permute-start.38) | collective-permute-done | bytes 24608 | tf_op jit(solution)/shard_map/ppermute | solution.py:224
  216.0 4.9 %attend_back.1 = (bf16[96,384]{1,0:T(8,128)(2,1)}, bf16[96,384]{1,0:T(8,128)(2,1)}, bf16[96,384]{1,0:T(8,128)(2,1)}, bf16[96,384]{1,0:T(8,128)(2,1)}, bf16[96,38...) custom-call(bf16[96,128]{1,0:T(8,128)(2,1)} %get-tuple-element.143.refs_0_, ...), custom_call_target="tpu_custom_call" | custom-call | flops 402653184 | bytes 2949120 | tf_op jit(solution)/shard_map/attend_back/pallas_call | solution.py:194
  232.1 3.7 output.1
  240.3 5.0 %d_norm1.1 = (bf16[4,96,768]{2,1,0:T(8,128)(2,1)}, bf16[2,96,1024]{2,1,0:T(8,128)(2,1)}, f32[2,96,1024]{2,1,0:T(8,128)}, f32[1,1024]{1,0:T(1,128)}) custom-call(s32[2]{0:T(128)} %pad_add_fusion.ids, bf16[1024,768]{1,0:T(8,128)(2,1)} %get-tuple-element.137.w_full, bf16[104,1024]{1,0:T(8,128)(2,1)} %get-tuple-element.97.r0.rowsx, bf16[104,1024]{1,0:T(8,128)(2,1)} %copy-done.3, ...), custom_call_target="tpu_custom_call" | custom-call | flops 603979776 | bytes 4788224 | tf_op jit(solution)/shard_map/d_norm1/pallas_call | solution.py:194
  246.7 3.8 grad_qkv.1
  251.8 6.1 %collective-permute-done.61 = bf16[2,32,1024]{2,1,0:T(8,128)(2,1)S(1)} collective-permute-done((bf16[2,32,1024]{2,1,0:T(8,128)(2,1)S(1)}, bf16[2,32,1024]{2,1,0:T(8,128)(2,1)S(1)}, u32[]{:S(2)}, u32[]{:S(2)}) %collective-permute-start.61) | collective-permute-done | bytes 131104 | tf_op jit(solution)/shard_map/ppermute | solution.py:224
  257.9 8.2 %collective-permute-done.54 = bf16[4,144,768]{2,1,0:T(8,128)(2,1)S(1)} collective-permute-done((bf16[4,144,768]{2,1,0:T(8,128)(2,1)}, bf16[4,144,768]{2,1,0:T(8,128)(2,1)S(1)}, u32[]{:S(2)}, u32[]{:S(2)}) %collective-permute-start.54) | collective-permute-done | bytes 884768 | tf_op jit(solution)/shard_map/ppermute | solution.py:224
  272.4 31.8 %collective-permute-done.55 = bf16[2,144,768]{2,1,0:T(8,128)(2,1)S(1)} collective-permute-done((bf16[2,144,768]{2,1,0:T(8,128)(2,1)S(1)}, bf16[2,144,768]{2,1,0:T(8,128)(2,1)S(1)}, u32[]{:S(2)}, u32[]{:S(2)}) %collective-permute-start.55) | collective-permute-done | bytes 442400 | tf_op jit(solution)/shard_map/ppermute | solution.py:224
  312.6 21.6 %collective-permute-done.56 = bf16[144,768]{1,0:T(8,128)(2,1)} collective-permute-done((bf16[144,768]{1,0:T(8,128)(2,1)S(1)}, bf16[144,768]{1,0:T(8,128)(2,1)}, u32[]{:S(2)}, u32[]{:S(2)}) %collective-permute-start.56) | collective-permute-done | bytes 221216 | tf_op jit(solution)/shard_map/ppermute | solution.py:224
  340.5 3.8 input_grad.1
  362.6 11.7 %collective-permute-done.69.p3 = f32[32,1024]{1,0:T(8,128)S(1)} collective-permute-done((f32[32,1024]{1,0:T(8,128)S(1)}, f32[32,1024]{1,0:T(8,128)S(1)}, u32[]{:S(2)}, u32[]{:S(2)}) %collective-permute-start.69) | collective-permute-done | bytes 131104 | tf_op jit(solution)/shard_map/ppermute | solution.py:224
  379.7 5.9 %collective-permute-done.70 = f32[128,1024]{1,0:T(8,128)S(1)} collective-permute-done((f32[128,1024]{1,0:T(8,128)S(1)}, f32[128,1024]{1,0:T(8,128)S(1)}, u32[]{:S(2)}, u32[]{:S(2)}) %collective-permute-start.70) | collective-permute-done | bytes 524320 | tf_op jit(solution)/shard_map/ppermute | solution.py:777
  (309 shorter events, 159.3 us)
Async XLA Ops:
  10.9 19.2 %collective-permute-start.5 = (bf16[256,768]{1,0:T(8,128)(2,1)}, bf16[256,768]{1,0:T(8,128)(2,1)S(1)}, u32[]{:S(2)}, u32[]{:S(2)}) collective-permute-start(bf16[256,768]{1,0:T(8,128)(2,1)} %get-tuple-element.101), channel_id=1, source_target_pairs={{0,3},{1,2},{2,1},{3,0},{4,7},{5,6},{6,5},{7,4},{8,11},{9,10},{10,... | collective-permute-start | bytes 1179656 | tf_op jit(solution)/shard_map/ppermute | solution.py:224
  12.6 17.6 %collective-permute-start.2 = (bf16[104,1024]{1,0:T(8,128)(2,1)S(1)}, bf16[104,1024]{1,0:T(8,128)(2,1)S(1)}, u32[]{:S(2)}, u32[]{:S(2)}) collective-permute-start(bf16[104,1024]{1,0:T(8,128)(2,1)S(1)} %collective-permute-done.1.r2), channel_id=1, source_target_pairs={{0,1},{1,0},{2,3},{3,2},{4,5},{5,4},{6,7},{7,6},{8,9},{9,8},{10,11... | collective-permute-start | bytes 638984 | tf_op jit(solution)/shard_map/ppermute | solution.py:224
  88.9 30.3 %collective-permute-start.28 = (bf16[256,1024]{1,0:T(8,128)(2,1)}, bf16[256,1024]{1,0:T(8,128)(2,1)S(1)}, u32[]{:S(2)}, u32[]{:S(2)}) collective-permute-start(bf16[256,1024]{1,0:T(8,128)(2,1)} %get-tuple-element.125), channel_id=1, source_target_pairs={{0,1},{1,0},{2,3},{3,2},{4,5},{5,4},{6,7},{7,6},{8,9},{9,8},{10,11... | collective-permute-start | bytes 1572872 | tf_op jit(solution)/shard_map/ppermute | solution.py:224
  89.4 29.8 %collective-permute-start.29 = (bf16[256,1024]{1,0:T(8,128)(2,1)}, bf16[256,1024]{1,0:T(8,128)(2,1)S(1)}, u32[]{:S(2)}, u32[]{:S(2)}) collective-permute-start(bf16[256,1024]{1,0:T(8,128)(2,1)} %get-tuple-element.126), channel_id=1, source_target_pairs={{0,2},{1,3},{2,0},{3,1},{4,6},{5,7},{6,4},{7,5},{8,10},{9,11},{10,... | collective-permute-start | bytes 1572872 | tf_op jit(solution)/shard_map/ppermute | solution.py:224
  90.9 28.3 %collective-permute-start.30 = (bf16[256,1024]{1,0:T(8,128)(2,1)}, bf16[256,1024]{1,0:T(8,128)(2,1)S(1)}, u32[]{:S(2)}, u32[]{:S(2)}) collective-permute-start(bf16[256,1024]{1,0:T(8,128)(2,1)} %get-tuple-element.127), channel_id=1, source_target_pairs={{0,3},{1,2},{2,1},{3,0},{4,7},{5,6},{6,5},{7,4},{8,11},{9,10},{10,... | collective-permute-start | bytes 1572872 | tf_op jit(solution)/shard_map/ppermute | solution.py:224
  95.3 23.8 %collective-permute-start.23 = (bf16[96,1024]{1,0:T(8,128)(2,1)}, bf16[96,1024]{1,0:T(8,128)(2,1)S(1)}, u32[]{:S(2)}, u32[]{:S(2)}) collective-permute-start(bf16[96,1024]{1,0:T(8,128)(2,1)} %get-tuple-element.122.n0), channel_id=1, source_target_pairs={{0,2},{1,3},{2,0},{3,1},{4,6},{5,7},{6,4},{7,5},{8,10},{9,11},{10,... | collective-permute-start | bytes 589832 | tf_op jit(solution)/shard_map/ppermute | solution.py:224
  95.7 23.5 %collective-permute-start.22 = (bf16[96,1024]{1,0:T(8,128)(2,1)}, bf16[96,1024]{1,0:T(8,128)(2,1)S(1)}, u32[]{:S(2)}, u32[]{:S(2)}) collective-permute-start(bf16[96,1024]{1,0:T(8,128)(2,1)} %get-tuple-element.122.n0), channel_id=1, source_target_pairs={{0,1},{1,0},{2,3},{3,2},{4,5},{5,4},{6,7},{7,6},{8,9},{9,8},{10,11... | collective-permute-start | bytes 589832 | tf_op jit(solution)/shard_map/ppermute | solution.py:224
  155.9 110.5 %collective-permute-start.64 = (bf16[4,256,1024]{2,1,0:T(8,128)(2,1)}, bf16[4,256,1024]{2,1,0:T(8,128)(2,1)S(1)}, u32[]{:S(2)}, u32[]{:S(2)}) collective-permute-start(bf16[4,256,1024]{2,1,0:T(8,128)(2,1)} %get-tuple-element.184), channel_id=1, source_target_pairs={{0,4},{4,0},{8,12},{12,8},{16,20},{20,16},{24,28},{28,24},{1,5},{5... | collective-permute-start | bytes 6291464 | tf_op jit(solution)/shard_map/ppermute | solution.py:224
  159.8 64.6 %collective-permute-start.32 = (bf16[96,1024]{1,0:T(8,128)(2,1)}, bf16[96,1024]{1,0:T(8,128)(2,1)S(1)}, u32[]{:S(2)}, u32[]{:S(2)}) collective-permute-start(bf16[96,1024]{1,0:T(8,128)(2,1)} %get-tuple-element.132), channel_id=1, source_target_pairs={{0,2},{1,3},{2,0},{3,1},{4,6},{5,7},{6,4},{7,5},{8,10},{9,11},{10,... | collective-permute-start | bytes 589832 | tf_op jit(solution)/shard_map/ppermute | solution.py:224
  165.1 38.6 %collective-permute-start.38 = (bf16[96,128]{1,0:T(8,128)(2,1)}, bf16[96,128]{1,0:T(8,128)(2,1)S(1)}, u32[]{:S(2)}, u32[]{:S(2)}) collective-permute-start(bf16[96,128]{1,0:T(8,128)(2,1)} %get-tuple-element.144), channel_id=1, source_target_pairs={{0,4},{4,0},{8,12},{12,8},{16,20},{20,16},{24,28},{28,24},{1,5},{5... | collective-permute-start | bytes 73736 | tf_op jit(solution)/shard_map/ppermute | solution.py:224
  166.6 37.2 %collective-permute-start.39 = (bf16[96,128]{1,0:T(8,128)(2,1)}, bf16[96,128]{1,0:T(8,128)(2,1)S(1)}, u32[]{:S(2)}, u32[]{:S(2)}) collective-permute-start(bf16[96,128]{1,0:T(8,128)(2,1)} %get-tuple-element.145), channel_id=1, source_target_pairs={{0,8},{4,12},{8,0},{12,4},{16,24},{20,28},{24,16},{28,20},{1,9},{5... | collective-permute-start | bytes 73736 | tf_op jit(solution)/shard_map/ppermute | solution.py:224
  166.6 40.1 %collective-permute-start.40 = (bf16[96,128]{1,0:T(8,128)(2,1)}, bf16[96,128]{1,0:T(8,128)(2,1)S(1)}, u32[]{:S(2)}, u32[]{:S(2)}) collective-permute-start(bf16[96,128]{1,0:T(8,128)(2,1)} %get-tuple-element.146), channel_id=1, source_target_pairs={{0,12},{4,8},{8,4},{12,0},{16,28},{20,24},{24,20},{28,16},{1,13},{... | collective-permute-start | bytes 73736 | tf_op jit(solution)/shard_map/ppermute | solution.py:224
  250.4 15.6 %collective-permute-start.54 = (bf16[4,144,768]{2,1,0:T(8,128)(2,1)}, bf16[4,144,768]{2,1,0:T(8,128)(2,1)S(1)}, u32[]{:S(2)}, u32[]{:S(2)}) collective-permute-start(bf16[4,144,768]{2,1,0:T(8,128)(2,1)} %get-tuple-element.173), channel_id=1, source_target_pairs={{0,4},{4,0},{8,12},{12,8},{16,20},{20,16},{24,28},{28,24},{1,5},{5... | collective-permute-start | bytes 2654216 | tf_op jit(solution)/shard_map/ppermute | solution.py:224
  251.8 55.6 %collective-permute-start.52 = (bf16[2,96,1024]{2,1,0:T(8,128)(2,1)}, bf16[2,96,1024]{2,1,0:T(8,128)(2,1)S(1)}, u32[]{:S(2)}, u32[]{:S(2)}) collective-permute-start(bf16[2,96,1024]{2,1,0:T(8,128)(2,1)} %get-tuple-element.162), channel_id=1, source_target_pairs={{0,1},{1,0},{2,3},{3,2},{4,5},{5,4},{6,7},{7,6},{8,9},{9,8},{10,11... | collective-permute-start | bytes 1179656 | tf_op jit(solution)/shard_map/ppermute | solution.py:224
  266.3 37.9 %collective-permute-start.55 = (bf16[2,144,768]{2,1,0:T(8,128)(2,1)S(1)}, bf16[2,144,768]{2,1,0:T(8,128)(2,1)S(1)}, u32[]{:S(2)}, u32[]{:S(2)}) collective-permute-start(bf16[2,144,768]{2,1,0:T(8,128)(2,1)S(1)} %slice.197), channel_id=1, source_target_pairs={{0,16},{4,20},{8,24},{12,28},{16,0},{20,4},{24,8},{28,12},{1,17},{... | collective-permute-start | bytes 1327112 | tf_op jit(solution)/shard_map/ppermute | solution.py:224
  269.2 66.0 %collective-permute-start.65 = (bf16[2,256,1024]{2,1,0:T(8,128)(2,1)S(1)}, bf16[2,256,1024]{2,1,0:T(8,128)(2,1)S(1)}, u32[]{:S(2)}, u32[]{:S(2)}) collective-permute-start(bf16[2,256,1024]{2,1,0:T(8,128)(2,1)S(1)} %slice.196), channel_id=1, source_target_pairs={{0,16},{4,20},{8,24},{12,28},{16,0},{20,4},{24,8},{28,12},{1,17},{... | collective-permute-start | bytes 3145736 | tf_op jit(solution)/shard_map/ppermute | solution.py:224
  270.3 34.1 %collective-permute-start.62 = (bf16[32,1024]{1,0:T(8,128)(2,1)S(1)}, bf16[32,1024]{1,0:T(8,128)(2,1)S(1)}, u32[]{:S(2)}, u32[]{:S(2)}) collective-permute-start(bf16[32,1024]{1,0:T(8,128)(2,1)S(1)} %fusion.5), channel_id=1, source_target_pairs={{0,8},{4,12},{8,0},{12,4},{16,24},{20,28},{24,16},{28,20},{1,9},{5... | collective-permute-start | bytes 196616 | tf_op jit(solution)/shard_map/ppermute | solution.py:224
  304.3 29.9 %collective-permute-start.56 = (bf16[144,768]{1,0:T(8,128)(2,1)S(1)}, bf16[144,768]{1,0:T(8,128)(2,1)}, u32[]{:S(2)}, u32[]{:S(2)}) collective-permute-start(bf16[144,768]{1,0:T(8,128)(2,1)S(1)} %fusion.3), channel_id=1, source_target_pairs={{0,8},{4,12},{8,0},{12,4},{16,24},{20,28},{24,16},{28,20},{1,9},{5... | collective-permute-start | bytes 663560 | tf_op jit(solution)/shard_map/ppermute | solution.py:224
  305.1 32.6 %collective-permute-start.63 = (f32[32,1024]{1,0:T(8,128)}, f32[32,1024]{1,0:T(8,128)}, u32[]{:S(2)}, u32[]{:S(2)}) collective-permute-start(f32[32,1024]{1,0:T(8,128)} %fusion.4), channel_id=1, source_target_pairs={{0,0},{1,8},{2,16},{3,24},{4,1},{5,9},{6,17},{7,25},{8,2},{9,10},{... | collective-permute-start | bytes 393224 | tf_op jit(solution)/shard_map/ppermute | solution.py:783
  310.2 29.6 %collective-permute-start.53 = (bf16[96,1024]{1,0:T(8,128)(2,1)}, bf16[96,1024]{1,0:T(8,128)(2,1)S(1)}, u32[]{:S(2)}, u32[]{:S(2)}) collective-permute-start(bf16[96,1024]{1,0:T(8,128)(2,1)} %get-tuple-element.164), channel_id=1, source_target_pairs={{0,2},{1,3},{2,0},{3,1},{4,6},{5,7},{6,4},{7,5},{8,10},{9,11},{10,... | collective-permute-start | bytes 589832 | tf_op jit(solution)/shard_map/ppermute | solution.py:224
  335.6 20.0 %collective-permute-start.66 = (bf16[256,1024]{1,0:T(8,128)(2,1)S(1)}, bf16[256,1024]{1,0:T(8,128)(2,1)S(1)}, u32[]{:S(2)}, u32[]{:S(2)}) collective-permute-start(bf16[256,1024]{1,0:T(8,128)(2,1)S(1)} %fusion.1), channel_id=1, source_target_pairs={{0,8},{4,12},{8,0},{12,4},{16,24},{20,28},{24,16},{28,20},{1,9},{5... | collective-permute-start | bytes 1572872 | tf_op jit(solution)/shard_map/ppermute | solution.py:224
  355.8 29.7 %collective-permute-start.70 = (f32[128,1024]{1,0:T(8,128)S(1)}, f32[128,1024]{1,0:T(8,128)S(1)}, u32[]{:S(2)}, u32[]{:S(2)}) collective-permute-start(f32[128,1024]{1,0:T(8,128)S(1)} %slice.167), channel_id=1, source_target_pairs={{0,0},{1,8},{2,16},{3,24},{4,1},{5,9},{6,17},{7,25},{8,2},{9,10},{... | collective-permute-start | bytes 1572872 | tf_op jit(solution)/shard_map/ppermute | solution.py:777
  358.8 15.4 %collective-permute-start.69 = (f32[32,1024]{1,0:T(8,128)S(1)}, f32[32,1024]{1,0:T(8,128)S(1)}, u32[]{:S(2)}, u32[]{:S(2)}) collective-permute-start(f32[32,1024]{1,0:T(8,128)S(1)} %get-tuple-element.194), channel_id=1, source_target_pairs={{0,3},{1,2},{2,1},{3,0},{4,7},{5,6},{6,5},{7,4},{8,11},{9,10},{10,... | collective-permute-start | bytes 393224 | tf_op jit(solution)/shard_map/ppermute | solution.py:224
  359.8 17.2 %collective-permute-start.68 = (f32[32,1024]{1,0:T(8,128)S(1)}, f32[32,1024]{1,0:T(8,128)S(1)}, u32[]{:S(2)}, u32[]{:S(2)}) collective-permute-start(f32[32,1024]{1,0:T(8,128)S(1)} %get-tuple-element.195), channel_id=1, source_target_pairs={{0,2},{1,3},{2,0},{3,1},{4,6},{5,7},{6,4},{7,5},{8,10},{9,11},{10,... | collective-permute-start | bytes 393224 | tf_op jit(solution)/shard_map/ppermute | solution.py:224
  (112 other events, 835.7 us)

commit v2 on v0

--- a/solution.py
+++ b/solution.py
@@ -1,6 +1,10 @@
+import math
+
 import jax
 import jax.numpy as jnp
 from jax import lax
+from jax.experimental import pallas as pl
+from jax.experimental.pallas import tpu as pltpu
 from jax.sharding import PartitionSpec as P
 
 HEADS = 16
@@ -11,6 +15,10 @@
 EPSILON = 1e-06
 MASKED = -1e30
 HIGHEST = lax.Precision.HIGHEST
+BF16, F32 = jnp.bfloat16, jnp.float32
+VMEM_LIMIT = 24 * 2**20
+UP_ORDER = (1, 2, 4)
+WEIGHT = 10**10
 
 
 def rms_norm(values, gain):
@@ -183,6 +191,889 @@
     )
 
 
+ORDER = (0, 2, 1, 3)
+
+
+def sds(shape, dtype):
+    return jax.ShapeDtypeStruct(shape, dtype)
+
+
+def local(shape, dtype):
+    return pltpu.VMEM(shape, dtype)
+
+
+def near(x):
+    return pltpu.with_memory_space_constraint(x, pltpu.VMEM)
+
+
+class Chain:
+    def __init__(self):
+        self.last = None
+
+    def __call__(self, kernel, outs, smem, args, scratch=(), name=None, far=(), after=(), weight=WEIGHT):
+        count = len(smem) + len(far) + len(args)
+        spec = pl.BlockSpec(memory_space=pltpu.VMEM)
+        extra = () if self.last is None else (near(self.last),)
+        extra = (*extra, *(near(a) for a in after))
+
+        def body(*refs):
+            kernel(*refs[:count], *refs[count + len(extra) :])
+
+        results = pl.pallas_call(
+            body,
+            out_shape=tuple(outs),
+            in_specs=[pl.BlockSpec(memory_space=pltpu.SMEM)] * len(smem)
+            + [pl.BlockSpec(memory_space=pltpu.HBM)] * len(far)
+            + [spec] * (len(args) + len(extra)),
+            out_specs=tuple(spec for _ in outs),
+            scratch_shapes=list(scratch),
+            compiler_params=pltpu.CompilerParams(vmem_limit_bytes=VMEM_LIMIT),
+            cost_estimate=pl.CostEstimate(flops=weight, bytes_accessed=weight // 10000, transcendentals=0),
+            name=name,
+        )(
+            *smem, *(pltpu.with_memory_space_constraint(a, pltpu.HBM) for a in far), *(near(a) for a in args), *extra
+        )
+        if not isinstance(outs[0], jax.ShapeDtypeStruct):
+            self.last = results[0]
+        return results
+
+    def hold(self, x, *after):
+        (x,) = self(hold_kernel, (local(x.shape, x.dtype),), (), (x,), after=after, name="hold")
+        return x
+
+
+def hold_kernel(x, out):
+    out[...] = x[...]
+
+
+def pair_kernel(a, b, out):
+    out[0] = a[...]
+    out[1] = b[...]
+
+
+def mm(left, right):
+    return jnp.dot(left, right, preferred_element_type=F32)
+
+
+def mm_t(left, right):
+    return lax.dot_general(left, right, (((1,), (1,)), ((), ())), preferred_element_type=F32)
+
+
+def t_mm(left, right):
+    return lax.dot_general(left, right, (((0,), (0,)), ((), ())), preferred_element_type=F32)
+
+
+def exchange(x, axis, size, mask):
+    return lax.ppermute(x, axis, [(i, i ^ mask) for i in range(size)])
+
+
+def rms_factor(values):
+    return lax.rsqrt(jnp.mean(values * values, axis=-1, keepdims=True) + EPSILON)
+
+
+def aligned(start, unit):
+    return pl.multiple_of(start, unit)
+
+
+def iota(shape, axis):
+    return lax.broadcasted_iota(jnp.int32, shape, axis)
+
+
+def picks(ids, routed, micro, tok_dev):
+    index = routed[micro : micro + 1, :] - ids[0] * tok_dev
+    shape = (tok_dev, routed.shape[1])
+    return jnp.where(iota(shape, 0) == index, 1.0, 0.0)
+
+
+def share_peers(ids):
+    return ids[1], ids[1] ^ 1, ids[1] ^ (2 + (ids[0] & 1))
+
+
+def share_rows(c, f):
+    y = c & 1
+    return f, f ^ 1, f ^ (2 + y), f ^ (3 - y)
+
+
+def cut_qkv(ids, half, w_qkv, pieces, sem, first, by_y=True):
+    width = w_qkv.shape[1] // 3
+    copies = []
+    peers = share_peers(ids) if by_y else tuple(ids[1] ^ k for k in range(4))
+    for k, (peer, piece) in enumerate(zip(peers, pieces)):
+        for b in range(3):
+            start = b * width + peer * (width // 4) + half * 128
+            copies.append(
+                pltpu.make_async_copy(
+                    w_qkv.at[:, pl.ds(aligned(start, 128), 128)],
+                    piece.at[:, pl.ds(b * 128, 128)],
+                    sem.at[first + 3 * k + b],
+                )
+            )
+    return copies
+
+
+def front_kernel(ids, deal, tokens, w_qkv, routed, rowsx, p0, p1, p2, near_tokens, sem):
+    micros, tok_dev, width = tokens.shape
+    per = routed.shape[1]
+    count = micros * per
+    span = tok_dev // 2
+    first = pltpu.make_async_copy(tokens, near_tokens, sem.at[0])
+    first.start()
+    copies = cut_qkv(ids, ids[0] >> 2, w_qkv, (p0, p1, p2), sem, 1)
+    for copy in copies:
+        copy.start()
+    stored = routed[...]
+    chunk = stored // span
+    anchor = jnp.zeros_like(stored)
+    for entry in range(deal.shape[0]):
+        anchor = jnp.where(chunk == entry, deal[entry], anchor)
+    place = ((anchor * span + stored % span) // BLOCK).astype(F32)
+    rowsx[count:] = jnp.zeros((8, width), BF16)
+    for micro in range(micros):
+        rowsx[count + micro : count + micro + 1, :per] = place[micro : micro + 1].astype(BF16)
+    first.wait()
+    for micro in range(micros):
+        pick = picks(ids, routed, micro, tok_dev).astype(BF16)
+        rowsx[micro * per : (micro + 1) * per] = t_mm(pick, near_tokens[micro]).astype(BF16)
+    for copy in copies:
+        copy.wait()
+
+
+def cut_kernel(ids, w_up, w_qkv, p0, p1, p2, v0, v1, v2, v3, sem):
+    share = p0.shape[1]
+    copies = cut_qkv(ids, 1 - (ids[0] >> 2), w_qkv, (v0, v1, v2, v3), sem, 3, False)
+    for k, (peer, piece) in enumerate(zip(share_peers(ids), (p0, p1, p2))):
+        copies.append(
+            pltpu.make_async_copy(
+                w_up.at[:, pl.ds(aligned(peer * share, share), share)], piece, sem.at[k]
+            )
+        )
+    for copy in copies:
+        copy.start()
+    for copy in copies:
+        copy.wait()
+
+
+def cot_kernel(ids, routed, cot, rowsx, both):
+    micros, tok_dev = cot.shape[:2]
+    per = routed.shape[1]
+    start = rowsx.shape[0]
+    both[:start] = rowsx[...]
+    for micro in range(micros):
+        pick = picks(ids, routed, micro, tok_dev).astype(BF16)
+        both[start + micro * per : start + (micro + 1) * per] = t_mm(pick, cot[micro]).astype(BF16)
+
+
+def rows_of(both):
+    return both[: both.shape[0] // 2 - 4].astype(F32)
+
+
+def cots_of(both):
+    return both[both.shape[0] // 2 + 4 :].astype(F32)
+
+
+def d_mlp_kernel(b0, b1, b2, b3, w_router, d_mlp, gate_out):
+    count = gate_out.shape[1]
+    for i, both in enumerate((b0, b1, b2, b3)):
+        gate = jax.nn.sigmoid(jnp.sum(rows_of(both) * w_router[...], axis=1, keepdims=True))
+        d_mlp[i * count : (i + 1) * count] = (gate * cots_of(both)).astype(BF16)
+        gate_out[i] = gate
+
+
+def head_masks():
+    lanes = iota((1, 128), 1)
+    low = jnp.where(lanes < 64, 1.0, 0.0)
+    return low, 1.0 - low
+
+
+def attend_kernel(
+    ids, r0, r1, r2, r3, gain, w0, w1, w2, w3,
+    h0, h1, h2, h3, h4, h5, h6, h7, stack, probs, norm1, place_col, result,
+):
+    c, f = ids[0], ids[1]
+    micros, total = stack.shape[0], stack.shape[1]
+    count = h0.shape[0]
+    per = count // micros
+    eye = iota((per, 128), 0) == iota((per, 128), 1)
+    for peer, source in zip((f, f ^ 2, f ^ 1, f ^ 3), (r0, r1, r2, r3)):
+        for h in range(2):
+            rows = source[h, :count].astype(F32)
+            index = ((c >> 2) ^ h) * 4 + peer
+            norm1[pl.ds(aligned(index * count, 16), count)] = (
+                rows * rms_factor(rows) * gain[...]
+            ).astype(BF16)
+            places = source[h, count : count + 8, :128].astype(F32)
+            for m in range(micros):
+                col = jnp.sum(jnp.where(eye, places[m : m + 1], 0.0), axis=1, keepdims=True)
+                place_col[m, pl.ds(aligned(index * per, per), per), :] = jnp.broadcast_to(
+                    col, (per, 128)
+                )
+    qkv = jnp.zeros((8 * count, 384), F32)
+    for peer, w in zip(share_rows(c, f), (w0, w1, w2, w3)):
+        part = w.shape[0]
+        qkv = qkv + mm(norm1[:, pl.ds(aligned(peer * part, part), part)], w[...])
+    low = qkv.astype(BF16)
+    for t in range(8):
+        for m in range(micros):
+            stack[m, t * per : (t + 1) * per, :] = low[
+                t * count + m * per : t * count + (m + 1) * per
+            ]
+    big_eye = iota((total, total), 0) == iota((total, total), 1)
+    masks = head_masks()
+    for m in range(micros):
+        q, k, v = stack[m, :, :128], stack[m, :, 128:256], stack[m, :, 256:384]
+        mine = place_col[m, :, 0:1]
+        theirs = jnp.sum(jnp.where(big_eye, mine, 0.0), axis=0, keepdims=True)
+        visible = theirs <= mine
+        attended = jnp.zeros((total, 128), F32)
+        for h in range(2):
+            scores = mm_t(q * masks[h].astype(BF16), k) * (HEAD_DIM**-0.5)
+            scores = jnp.where(visible, scores, MASKED)
+            top = jnp.max(scores, axis=1, keepdims=True)
+            grown = jnp.exp(scores - top)
+            weight = grown / jnp.sum(grown, axis=1, keepdims=True)
+            probs[2 * m + h] = weight
+            attended = attended + mm(weight.astype(BF16), v) * masks[h]
+        result[m] = attended.astype(BF16)
+        for k, out in enumerate((h0, h1, h2, h3, h4, h5, h6, h7)):
+            out[m * per : (m + 1) * per, :] = result[m, pl.ds(aligned((c ^ k) * per, per), per), :]
+
+
+def row_slot(f, s, count):
+    k = s ^ f
+    return aligned(((k & 1) * 2 + (k >> 1)) * count, 16)
+
+
+def split_rows(full, send, keep):
+    count = send.shape[1]
+    for i in range(2):
+        keep[i] = full[i * count : (i + 1) * count]
+        send[i] = full[(2 + i) * count : (3 + i) * count].astype(BF16)
+
+
+def block_place(ids, k, count, lanes):
+    peer = ids[0] ^ k
+    columns = aligned((peer >> 2) * lanes, 128)
+    return pl.ds(row_slot(ids[1], peer & 3, count), count), pl.ds(columns, lanes)
+
+
+def out_kernel(ids, b0, b1, b2, b3, b4, b5, b6, b7, w_out, attended, send, keep, full):
+    count = b0.shape[0]
+    for k, block in enumerate((b0, b1, b2, b3, b4, b5, b6, b7)):
+        attended[block_place(ids, k, count, 128)] = block[...]
+    full[...] = mm(attended[...], w_out[...])
+    split_rows(full, send, keep)
+
+
+def add_both_kernel(keep, received, total):
+    total[...] = (keep[...] + received[...].astype(F32)).astype(BF16)
+
+
+def add_own_kernel(keep, received, send2, keep2):
+    send2[...] = (keep[1] + received[1].astype(F32)).astype(BF16)
+    keep2[...] = keep[0] + received[0].astype(F32)
+
+
+def mid_kernel(low, received, both0, both1, gain, attn, norm2):
+    for i, both in enumerate((both0, both1)):
+        value = low[i].astype(F32) + received[1 - i].astype(F32)
+        attn[i] = value
+        mid = rows_of(both) + value
+        norm2[i] = (mid * rms_factor(mid) * gain[...]).astype(BF16)
+
+
+def mlp_kernel(
+    ids, n0, n1, d_mlp, u0, u1, u2, u3, w_down,
+    send, keep, act_send, d_send, act_keep, d_keep, norm2, act, d_hidden, back,
+):
+    c = ids[0]
+    part = u0.shape[0]
+    count = n0.shape[1]
+    shares = tuple(zip(share_rows(ids[0], ids[1]), (u0, u1, u2, u3)))
+    for i in range(2):
+        norm2[i * count : (i + 1) * count] = n0[i]
+        norm2[(2 + i) * count : (3 + i) * count] = n1[i]
+    hidden = jnp.zeros(act.shape, F32)
+    for peer, u in shares:
+        hidden = hidden + mm(norm2[:, pl.ds(aligned(peer * part, part), part)], u[...])
+    d_act = mm_t(d_mlp[...], w_down[...])
+    phi = 0.5 * (1.0 + lax.erf(hidden * (0.5**0.5)))
+    act[...] = (hidden * phi).astype(BF16)
+    slope = phi + hidden * jnp.exp(-0.5 * hidden * hidden) * ((2.0 * math.pi) ** -0.5)
+    d_hidden[...] = (d_act * slope).astype(BF16)
+    for i, (some_act, some_d) in enumerate(((act_keep, d_keep), (act_send, d_send))):
+        for high in range(2):
+            start = aligned(high * 512 + (((c >> 1) & 1) ^ i) * 256, 128)
+            some_act[:, high * 256 : (high + 1) * 256] = act[:, pl.ds(start, 256)]
+        some_d[...] = d_hidden[:, pl.ds(aligned(((c & 1) ^ i) * 512, 128), 512)]
+    for peer, u in shares:
+        back[:, pl.ds(aligned(peer * part, part), part)] = mm_t(d_hidden[...], u[...])
+    split_rows(back, send, keep)
+
+
+def mlp_out_kernel(act, w_down, attn, gate, b0, b1, b2, b3, send, keep, router, full):
+    full[...] = mm(act[...], w_down[...])
+    split_rows(full, send, keep)
+    count = gate.shape[1]
+    total = jnp.zeros(router.shape, F32)
+    for i, both in enumerate((b0, b1, b2, b3)):
+        own = slice(i * count, (i + 1) * count)
+        part = jnp.sum(cots_of(both) * (attn[own] + full[own]), axis=1, keepdims=True)
+        part = part * gate[i] * (1.0 - gate[i])
+        total = total + jnp.sum(rows_of(both) * part, axis=0, keepdims=True)
+    router[...] = total
+
+
+def pick_rows(c, peer, share, out, lanes):
+    @pl.when(peer == (c >> 1))
+    def _():
+        out[:, lanes] = share[pl.ds(aligned((c & 1) * 128, 128), 128), :]
+
+
+def pick_kernel(ids, *refs):
+    shares, (up_rows, qkv_rows) = refs[:12], refs[12:]
+    c, f = ids[0], ids[1]
+    for peer, u, a in zip(share_rows(c, f), shares[:4], shares[4:8]):
+        pick_rows(c, peer, u, up_rows, slice(None))
+        pick_rows(c, peer, a, qkv_rows, slice(0, 384))
+    for k, b in enumerate(shares[8:]):
+        pick_rows(c, f ^ k, b, qkv_rows, slice(384, 768))
+
+
+def block_order(order):
+    one, two, three = order
+    keep = (0, three, two, two | three)
+    return keep, tuple(k | one for k in keep)
+
+
+def put_block(order, k, send, keep, where, value):
+    kept, sent = block_order(order)
+    if k in kept:
+        keep[(kept.index(k), *where)] = value
+    else:
+        send[(sent.index(k), *where)] = value.astype(BF16)
+
+
+def chunk(f, q):
+    return pl.ds(aligned((f ^ q) * 32, 32), 32)
+
+
+def grad_up_kernel(ids, norm2, near_a, near_b, d_own, d_near, send, keep, rows, columns):
+    count = norm2.shape[0]
+    half = count // 2
+    rows[:count] = norm2[...]
+    for i in range(2):
+        rows[count + i * (half // 2) : count + (i + 1) * (half // 2)] = near_a[i]
+        rows[count + half + i * (half // 2) : count + half + (i + 1) * (half // 2)] = near_b[i]
+    columns[:count] = d_own[...]
+    columns[count:] = d_near[...]
+    for place, (target, index) in enumerate(((keep, 0), (send, 0), (keep, 1), (send, 1))):
+        kk = (0, 1, 2, 3)[place]
+        start = aligned(((ids[0] >> 1) ^ kk) * 256, 128)
+        value = t_mm(rows[:, pl.ds(start, 256)], columns[...])
+        for owner in range(2):
+            for q in range(4):
+                at = pl.ds(aligned(((ids[0] & 1) ^ owner) * 128 + (ids[1] ^ q) * 32, 32), 32)
+                piece = value[owner * 128 + q * 32 : owner * 128 + (q + 1) * 32]
+                target[index, at] = piece.astype(target.dtype)
+
+
+def grad_down_kernel(ids, d_mlp, near_a, near_b, a_own, a_near, send, keep, rows, columns):
+    count = d_mlp.shape[0]
+    half = count // 2
+    rows[:count] = d_mlp[...]
+    rows[count : count + half] = near_a[...]
+    rows[count + half :] = near_b[...]
+    columns[:count] = a_own[...]
+    columns[count:] = a_near[...]
+    c = ids[0]
+    for target, index, k in ((keep, 0, 0), (send, 0, 1), (keep, 1, 4), (send, 1, 5)):
+        start = aligned(((c >> 2) ^ (k >> 2)) * 256 + ((c & 1) ^ (k & 1)) * 128, 128)
+        value = t_mm(columns[:, pl.ds(start, 128)], rows[...])
+        target[index] = value.astype(target.dtype)
+
+
+def grad_attn_kernel(
+    ids, norm1, b0, b1, b2, b3, b4, b5, b6, b7, attended, d_attn, router, send, keep, joined, full,
+):
+    count = b0.shape[0]
+    for k, block in enumerate((b0, b1, b2, b3, b4, b5, b6, b7)):
+        joined[pl.ds(aligned((ids[0] ^ k) * count, 16), count)] = block[...]
+    full[...] = t_mm(attended[...], d_attn[...])
+    for k in range(8):
+        owner = ids[0] ^ k
+        start = aligned(owner * 128, 128)
+        value = t_mm(norm1[:, pl.ds(start, 128)], joined[...])
+        for q in range(4):
+            where = (chunk(ids[1], q), slice(0, 384))
+            put_block(UP_ORDER, k, send, keep, where, value[q * 32 : (q + 1) * 32])
+            where = (slice(q * 32, (q + 1) * 32), slice(384, 640))
+            rows = full[pl.ds(aligned(owner * 32, 32), 32), q * 256 : (q + 1) * 256]
+            put_block(UP_ORDER, k, send, keep, where, rows)
+        below = slice(128, 136)
+        put_block(UP_ORDER, k, send, keep, (below, slice(128, 640)), jnp.zeros((8, 512), F32))
+        share = jnp.broadcast_to(router[:, pl.ds(start, 128)], (8, 128))
+        put_block(UP_ORDER, k, send, keep, (below, slice(0, 128)), share)
+
+
+def d_attn_kernel(low, received, attn, both0, both1, gate, gain, d_mid_out, d_attn):
+    for i, both in enumerate((both0, both1)):
+        mid = rows_of(both) + attn[i]
+        r2 = rms_factor(mid)
+        d_norm2 = low[i].astype(F32) + received[1 - i].astype(F32)
+        t2 = d_norm2 * gain[...]
+        d_mid = r2 * t2 - mid * (r2 * r2 * r2) * jnp.mean(t2 * mid, axis=1, keepdims=True)
+        d_attn[i] = (gate[i] * cots_of(both) + d_mid).astype(BF16)
+        if i == 0:
+            d_mid_out[...] = d_mid
+
+
+def d_attended_kernel(ids, d0, d1, w_out, b0, b1, b2, b3, b4, b5, b6, b7, d_attn, d_att):
+    count = d0.shape[1]
+    for i in range(2):
+        d_attn[i * count : (i + 1) * count] = d0[i]
+        d_attn[(2 + i) * count : (3 + i) * count] = d1[i]
+    d_att[...] = mm_t(d_attn[...], w_out[...])
+    for k, block in enumerate((b0, b1, b2, b3, b4, b5, b6, b7)):
+        block[...] = d_att[block_place(ids, k, count, 128)].astype(BF16)
+
+
+def attend_back_kernel(ids, *refs):
+    blocks, (stack, probs), outs, (d_stack, result) = refs[:8], refs[8:10], refs[10:18], refs[18:]
+    micros, total = stack.shape[0], stack.shape[1]
+    count = outs[0].shape[0]
+    per = count // micros
+    masks = head_masks()
+    for m in range(micros):
+        rows = slice(m * per, (m + 1) * per)
+        for k in range(8):
+            d_stack[pl.ds(aligned((ids[0] ^ k) * per, per), per), :] = blocks[k][rows]
+        q, k, v = stack[m, :, :128], stack[m, :, 128:256], stack[m, :, 256:384]
+        d_out = d_stack[...]
+        d_q = jnp.zeros((total, 128), F32)
+        d_k = jnp.zeros((total, 128), F32)
+        d_v = jnp.zeros((total, 128), F32)
+        for h in range(2):
+            weight = probs[2 * m + h]
+            d_probs = mm_t(d_out * masks[h].astype(BF16), v)
+            inner = jnp.sum(weight * d_probs, axis=1, keepdims=True)
+            d_scores = (weight * (d_probs - inner)).astype(BF16)
+            d_q = d_q + mm(d_scores, k) * masks[h]
+            d_k = d_k + t_mm(d_scores, q) * masks[h]
+            d_v = d_v + t_mm(weight.astype(BF16), d_out) * masks[h]
+        result[m, :, :128] = (d_q * (HEAD_DIM**-0.5)).astype(BF16)
+        result[m, :, 128:256] = (d_k * (HEAD_DIM**-0.5)).astype(BF16)
+        result[m, :, 256:384] = d_v.astype(BF16)
+        for k in range(8):
+            outs[k][rows] = result[m, pl.ds(aligned((ids[0] ^ k) * per, per), per), :]
+
+
+def d_norm1_kernel(
+    ids, d0, d1, d2, d3, d4, d5, d6, d7, a0, a1, a2, a3, b0, b1, b2, b3,
+    send, keep, d_qkv, full,
+):
+    c, f = ids[0], ids[1]
+    count = d0.shape[0]
+    part = a0.shape[0]
+    for k, block in enumerate((d0, d1, d2, d3, d4, d5, d6, d7)):
+        rows = pl.ds(row_slot(f, (c ^ k) & 3, count), count)
+        d_qkv[rows, (k >> 2) * 384 : (k >> 2) * 384 + 384] = block[...]
+    for peer, a in zip(share_rows(c, f), (a0, a1, a2, a3)):
+        full[:, pl.ds(aligned(peer * part, part), part)] = mm_t(d_qkv[:, :384], a[...])
+    for k, b in enumerate((b0, b1, b2, b3)):
+        columns = pl.ds(aligned((f ^ k) * part, part), part)
+        full[:, columns] = full[:, columns] + mm_t(d_qkv[:, 384:], b[...])
+    split_rows(full, send, keep)
+
+
+def place_rows(ids, routed, micro, source, rows, out):
+    tok_dev = source.shape[0]
+    pick = picks(ids, routed, micro, tok_dev)
+    changed = jnp.sum(pick, axis=1, keepdims=True) > 0.5
+    placed = mm(pick.astype(BF16), rows)
+    out[...] = jnp.where(changed, placed, source[...].astype(F32)).astype(BF16)
+
+
+def output_kernel(
+    ids, routed, keep, received, attn, both, gate, tokens, d_logit_out, output,
+):
+    count = keep.shape[0]
+    micros = tokens.shape[0]
+    per = count // micros
+    branch = attn[0] + keep[...] + received[...].astype(F32)
+    rows = rows_of(both)
+    open_gate = gate[0]
+    d_logit = (
+        jnp.sum(cots_of(both) * branch, axis=1, keepdims=True)
+        * open_gate
+        * (1.0 - open_gate)
+    )
+    d_logit_out[...] = d_logit
+    result = (rows + open_gate * branch).astype(BF16)
+    for micro in range(micros):
+        own = result[micro * per : (micro + 1) * per]
+        place_rows(ids, routed, micro, tokens.at[micro], own, output.at[micro])
+
+
+def input_grad_kernel(
+    ids, routed, keep, received, d_mid, both, d_logit, w_router, gain, cot, input_grad,
+):
+    count = keep.shape[0]
+    micros = cot.shape[0]
+    per = count // micros
+    rows = rows_of(both)
+    r1 = rms_factor(rows)
+    t1 = (keep[...] + received[...].astype(F32)) * gain[...]
+    d_rows = (
+        cots_of(both)
+        + d_mid[...]
+        + r1 * t1
+        - rows * (r1 * r1 * r1) * jnp.mean(t1 * rows, axis=1, keepdims=True)
+        + d_logit[...] * w_router[...]
+    ).astype(BF16)
+    for micro in range(micros):
+        own = d_rows[micro * per : (micro + 1) * per]
+        place_rows(ids, routed, micro, cot.at[micro], own, input_grad.at[micro])
+
+
+def as_row(column):
+    count = column.shape[0]
+    eye = iota((count, count), 0) == iota((count, count), 1)
+    return jnp.sum(jnp.where(eye, column, 0.0), axis=0, keepdims=True)
+
+
+def owned(ids, vector, count):
+    start = (4 * ids[0] + ids[1]) * count
+    shape = (count, vector.shape[1])
+    hit = iota(shape, 1) == iota(shape, 0) + start
+    return jnp.sum(jnp.where(hit, vector[...], 0.0), axis=1, keepdims=True)
+
+
+def join_up_kernel(ids, p0, p1, p2, p3, gain, out, grad_gain):
+    rows, part = out.shape[0], out.shape[1] // 4
+    total = jnp.zeros((rows, 1), F32)
+    for k, piece in enumerate((p0, p1, p2, p3)):
+        out[:, pl.ds(aligned((ids[1] ^ k) * part, part), part)] = piece[:, :part]
+        total = total + piece[:, part : part + 1]
+    grad_gain[...] = as_row(total / owned(ids, gain, rows))
+
+
+def join_qkv_kernel(ids, p0, p1, p2, p3, gain, out, grad_gain, grad_router):
+    rows, width = out.shape[0], out.shape[1] // 3
+    part = width // 4
+    total = jnp.zeros((rows, 1), F32)
+    router = jnp.zeros((rows, 1), F32)
+    for k, piece in enumerate((p0, p1, p2, p3)):
+        for half in range(2):
+            for b in range(3):
+                start = b * width + (ids[1] ^ k) * part + ((ids[0] >> 2) ^ half) * 128
+                out[:, pl.ds(aligned(start, 128), 128)] = piece[
+                    :, (3 * half + b) * 128 : (3 * half + b + 1) * 128
+                ]
+        total = total + piece[:, 768:769]
+        router = router + piece[:, 896:897]
+    grad_gain[...] = as_row(total / owned(ids, gain, rows))
+    grad_router[...] = as_row(router)
+
+
+def join_down_kernel(a, b, out):
+    out[...] = a[...].astype(F32) + b[...].astype(F32)
+
+
+def add_halves(keep, received, send2, keep2):
+    half = keep.shape[0] // 2
+    keep2[...] = keep[:half] + received[:half].astype(F32)
+    send2[...] = (keep[half:] + received[half:].astype(F32)).astype(BF16)
+
+
+def halves_kernel(*refs):
+    count = len(refs) // 4
+    for i in range(count):
+        add_halves(*refs[2 * i : 2 * i + 2], *refs[2 * count + 2 * i : 2 * count + 2 * i + 2])
+
+
+def hop2_kernel(keep_u, got_u, keep_d, got_d, send, keep, down0, down1):
+    add_halves(keep_u, got_u, send, keep)
+    down0[...] = (keep_d[0] + got_d[0].astype(F32)).astype(BF16)
+    down1[...] = (keep_d[1] + got_d[1].astype(F32)).astype(BF16)
+
+
+def last_kernel(keep_u, got_u, send, mine):
+    total = keep_u[0] + got_u[0].astype(F32)
+    half = total.shape[0] // 2
+    mine[...] = total[:half]
+    send[...] = total[half:].astype(BF16)
+
+
+def up_pieces_kernel(ids, mine, other, w_rows, c0, c1, c2, c3):
+    rows, half = c0.shape[0], mine.shape[1]
+    y = ids[0] & 1
+    for k, piece in enumerate((c0, c1, c2, c3)):
+        own = slice(k * rows, (k + 1) * rows)
+        weights = pl.ds(aligned((ids[1] ^ k) * rows, rows), rows)
+        total = jnp.zeros((rows, 1), F32)
+        for side, value in ((y, mine[own]), (1 - y, other[own].astype(F32))):
+            columns = pl.ds(aligned(side * half, 128), half)
+            piece[:, columns] = value
+            total = total + jnp.sum(
+                value * w_rows[weights, columns].astype(F32), axis=1, keepdims=True
+            )
+        piece[:, 2 * half :] = jnp.broadcast_to(total, (rows, 128))
+
+
+def pieces_kernel(ids, mine, got, w_rows, c0, c1, c2, c3, out):
+    rows = c0.shape[0]
+    router = mine[0, 128:129, :128] + got[0, 128:136, :128].astype(F32)[0:1]
+    for k, piece in enumerate((c0, c1, c2, c3)):
+        own = slice(k * rows, (k + 1) * rows)
+        first = (ids[1] ^ k) * rows
+        weights = pl.ds(aligned(first, rows), rows)
+        a, b = mine[0, own, :384], got[0, own, :384].astype(F32)
+        piece[:, :384] = a
+        piece[:, 384:768] = b
+        total = jnp.sum(a * w_rows[weights, :384].astype(F32), axis=1, keepdims=True)
+        total = total + jnp.sum(b * w_rows[weights, 384:].astype(F32), axis=1, keepdims=True)
+        piece[:, 768:896] = jnp.broadcast_to(total, (rows, 128))
+        hit = iota((rows, 128), 1) == iota((rows, 128), 0) + first
+        share = jnp.sum(jnp.where(hit, router, 0.0), axis=1, keepdims=True)
+        piece[:, 896:] = jnp.broadcast_to(share, (rows, 128))
+        out[:, k * 256 : (k + 1) * 256] = mine[0, own, 384:640] + got[0, own, 384:640].astype(F32)
+
+
+def halves(call, name, *pairs):
+    outs = []
+    for keep, _ in pairs:
+        shape = (keep.shape[0] // 2, *keep.shape[1:])
+        outs += [local(shape, BF16), local(shape, F32)]
+    flat = call(halves_kernel, outs, (), [x for pair in pairs for x in pair], name=name)
+    return [(flat[2 * i + 1], flat[2 * i]) for i in range(len(pairs))]
+
+
+def all_rows_sum(call, send, keep):
+    received = exchange(send, "fsdp", 4, 1)
+    (low,) = call(add_both_kernel, (local(keep.shape, BF16),), (), (keep, received), name="add_both")
+    return low, exchange(low, "fsdp", 4, 2)
+
+
+def own_rows_sum(call, send, keep):
+    received = exchange(send, "fsdp", 4, 1)
+    shape = keep.shape[1:]
+    send2, keep2 = call(
+        add_own_kernel, (local(shape, BF16), local(shape, F32)), (), (keep, received), name="add_own"
+    )
+    return keep2, exchange(send2, "fsdp", 4, 2)
+
+
+def swap_blocks(blocks):
+    got = {k: exchange(blocks[k], "ctx", 8, k) for k in (7, 6, 5, 4, 3, 2, 1)}
+    return (blocks[0], *(got[k] for k in range(1, 8)))
+
+
+def swap_across(parts):
+    mine, beside, across = parts
+    across = lax.ppermute(
+        across, ("ctx", "fsdp"),
+        [(4 * a + b, 4 * a + (b ^ (2 + (a & 1)))) for a in range(8) for b in range(4)],
+    )
+    return mine, exchange(beside, "fsdp", 4, 1), across
+
+
+def swap_pieces(pieces):
+    return (pieces[0], *(exchange(pieces[k], "fsdp", 4, k) for k in (1, 2, 3)))
+
+
+def shards_8x4(
+    tokens, w_router, gain_attn, w_qkv, w_out, gain_mlp, w_up, w_down, routed, deal, cotangent
+):
+    micros, tok_dev, width = tokens.shape[0], tokens.shape[2], tokens.shape[3]
+    per = routed.shape[2]
+    count = micros * per
+    total = 8 * per
+    part = width // 4
+    hidden = w_down.shape[0]
+    c, f = lax.axis_index("ctx"), lax.axis_index("fsdp")
+    ids = jnp.stack([c, f]).astype(jnp.int32)
+    tok, cot, routed = tokens[:, 0], cotangent[:, 0], routed[:, 0]
+    w_router, gain_attn, gain_mlp = (
+        w_router.reshape(1, width), gain_attn.reshape(1, width), gain_mlp.reshape(1, width),
+    )
+    rows_bf, rows_f = local((count, width), BF16), local((count, width), F32)
+    pair_bf, pair_f = local((2, count, width), BF16), local((2, count, width), F32)
+    all_bf, all_quarter = local((4 * count, width), BF16), local((4 * count, part), BF16)
+    hidden_bf = local((4 * count, hidden), BF16)
+    vector = local((1, width), F32)
+    dma = pltpu.SemaphoreType.DMA
+    call = Chain()
+
+    rowsx, *w_parts = call(
+        front_kernel,
+        (local((count + 8, width), BF16), *(local((part, 384), BF16),) * 3),
+        (ids, deal), (routed,), far=(tok, w_qkv),
+        scratch=[pltpu.VMEM(tok.shape, BF16), dma((10,))], name="front",
+    )
+    turn = [(4 * a + b, 4 * ((a & 4) | b) + (a & 3)) for a in range(8) for b in range(4)]
+    turned = lax.ppermute(rowsx, ("ctx", "fsdp"), turn)
+    turned_far = lax.ppermute(rowsx, ("ctx", "fsdp"), [(a, b ^ 16) for a, b in turn])
+    w_mine, w_beside, w_across = swap_across(w_parts)
+    w_parts = (w_mine, w_beside, w_across, exchange(w_across, "ctx", 8, 1))
+    (seq,) = call(
+        pair_kernel, (local((2, count + 8, width), BF16),), (), (turned, turned_far), name="pair"
+    )
+    seq_x, seq_c = exchange(seq, "fsdp", 4, 2), exchange(seq, "fsdp", 4, 1)
+    seq_xc = exchange(seq_x, "fsdp", 4, 1)
+    (both,) = call(
+        cot_kernel, (local((2 * count + 8, width), BF16),), (ids,), (routed, cot, rowsx), name="cot_rows"
+    )
+    both_x, both_c = exchange(both, "fsdp", 4, 2), exchange(both, "fsdp", 4, 1)
+    both_xc = exchange(both_x, "fsdp", 4, 1)
+    up_mine, up_beside, up_across, *rest = call(
+        cut_kernel, (local((part, hidden), BF16),) * 3 + (local((part, 384), BF16),) * 4, (ids,), (),
+        far=(w_up, w_qkv), scratch=[dma((15,))], name="cut_shares",
+    )
+    _, up_beside, up_across = swap_across((up_mine, up_beside, up_across))
+    *heads, stack, probs, norm1 = call(
+        attend_kernel,
+        (
+            *(local((count, 128), BF16),) * 8, local((micros, total, 384), BF16),
+            local((2 * micros, total, total), F32), local((8 * count, width), BF16),
+        ),
+        (ids,), (seq, seq_x, seq_c, seq_xc, gain_attn, *w_parts),
+        scratch=[pltpu.VMEM((micros, total, 128), F32), pltpu.VMEM((micros, total, 128), BF16)],
+        name="attend",
+    )
+    heads = swap_blocks(heads)
+    attended, send, keep, attn_part = call(
+        out_kernel, (all_quarter, pair_bf, pair_f, local((4 * count, width), F32)),
+        (ids,), (*heads, w_out), name="attn_out", after=(up_across, both_x),
+    )
+    up_parts = (up_mine, up_beside, up_across, exchange(up_across, "ctx", 8, 1))
+    low, received = all_rows_sum(call, send, keep)
+    d_mlp, gate = call(
+        d_mlp_kernel, (all_bf, local((4, count, 1), F32)), (),
+        (both, both_x, both_c, both_xc, w_router), name="d_mlp", weight=0,
+    )
+    d_mlp_a = exchange(d_mlp[: 2 * count], "ctx", 8, 2)
+    d_mlp_b = exchange(d_mlp_a, "fsdp", 4, 1)
+    attn, norm2 = call(
+        mid_kernel, (pair_f, pair_bf), (), (low, received, both, both_x, gain_mlp), name="mid"
+    )
+    norm2_a = exchange(norm2, "ctx", 8, 1)
+    norm2_b = exchange(norm2_a, "fsdp", 4, 1)
+    half_bf = local((4 * count, hidden // 2), BF16)
+    send, keep, act_send, d_send, act_keep, d_keep, norm2, act = call(
+        mlp_kernel, (pair_bf, pair_f, half_bf, half_bf, half_bf, half_bf, all_bf, hidden_bf), (ids,),
+        (norm2, exchange(norm2, "fsdp", 4, 1), d_mlp, *up_parts, w_down),
+        scratch=[pltpu.VMEM((4 * count, hidden), BF16), pltpu.VMEM((4 * count, width), F32)],
+        name="mlp",
+    )
+    d_near, act_near = exchange(d_send, "ctx", 8, 1), exchange(act_send, "ctx", 8, 2)
+    low, received = all_rows_sum(call, send, keep)
+    d_mid, d_attn = call(
+        d_attn_kernel, (rows_f, pair_bf), (),
+        (low, received, attn, both, both_x, gate, gain_mlp), name="d_attn",
+        after=(d_near, act_near),
+    )
+    *d_heads, d_attn = call(
+        d_attended_kernel, (*(local((count, 128), BF16),) * 8, all_bf), (ids,),
+        (d_attn, exchange(d_attn, "fsdp", 4, 1), w_out),
+        scratch=[pltpu.VMEM((4 * count, part), F32)], name="d_attended",
+    )
+    d_heads = swap_blocks(d_heads)
+    send_u, keep_u = call(
+        grad_up_kernel, (local((2, 256, hidden // 2), BF16), local((2, 256, hidden // 2), F32)), (ids,),
+        (norm2, norm2_a, norm2_b, d_keep, d_near), name="grad_up", weight=0,
+        scratch=[pltpu.VMEM((8 * count, width), BF16), pltpu.VMEM((8 * count, hidden // 2), BF16)],
+    )
+    send_d, keep_d = call(
+        grad_down_kernel, (local((2, 128, width), BF16), local((2, 128, width), F32)), (ids,),
+        (d_mlp, d_mlp_a, d_mlp_b, act_keep, act_near), name="grad_down", weight=0,
+        scratch=[pltpu.VMEM((8 * count, width), BF16), pltpu.VMEM((8 * count, hidden // 2), BF16)],
+    )
+    send_m, keep_m, router = call(
+        mlp_out_kernel, (pair_bf, pair_f, vector), (),
+        (act, w_down, attn_part, gate, both, both_x, both_c, both_xc), name="mlp_out", weight=0,
+        scratch=[pltpu.VMEM((4 * count, width), F32)],
+    )
+    got_u, got_d = exchange(send_u, "ctx", 8, 2), exchange(send_d, "ctx", 8, 1)
+    rest = swap_pieces(rest)
+    w_up_rows, w_qkv_rows = call(
+        pick_kernel, (local((128, hidden), BF16), local((128, 768), BF16)), (ids,),
+        (*up_parts, *w_parts, *rest), name="pick", weight=0,
+    )
+    d_blocks = call(
+        attend_back_kernel, (local((count, 384), BF16),) * 8, (ids,), (*d_heads, stack, probs),
+        scratch=[pltpu.VMEM((total, 128), BF16), pltpu.VMEM((micros, total, 384), BF16)],
+        name="attend_back",
+    )
+    d_own = swap_blocks(d_blocks)
+    send_q, keep_q = call(
+        grad_attn_kernel, (local((4, 136, 640), BF16), local((4, 136, 640), F32)), (ids,),
+        (norm1, *d_blocks, attended, d_attn, router), name="grad_attn", weight=0,
+        scratch=[pltpu.VMEM((8 * count, 384), BF16), pltpu.VMEM((part, width), F32)],
+    )
+    got_q = exchange(send_q, "ctx", 8, UP_ORDER[0])
+    keep_m, received_m = own_rows_sum(call, send_m, keep_m)
+    send_u, keep_u, down0, down1 = call(
+        hop2_kernel,
+        (local((1, 256, hidden // 2), BF16), local((1, 256, hidden // 2), F32))
+        + (local((128, width), BF16),) * 2,
+        (), (keep_u, got_u, keep_d, got_d), name="hop2", weight=0,
+    )
+    got_u = exchange(send_u, "ctx", 8, 4)
+    owners = [(4 * a + b, 4 * (2 * b + a // 4) + a % 4) for a in range(8) for b in range(4)]
+    far_owners = [(a ^ 16, b) for a, b in owners]
+    down0 = lax.ppermute(down0, ("ctx", "fsdp"), owners)
+    down1 = lax.ppermute(down1, ("ctx", "fsdp"), far_owners)
+    d_logit, output = call(
+        output_kernel, (local((count, 1), F32), sds(tok.shape, BF16)), (ids,),
+        (routed, keep_m, received_m, attn, both, gate, tok), name="output", weight=0,
+    )
+    send, keep = call(
+        d_norm1_kernel, (pair_bf, pair_f), (ids,),
+        (*d_own, *w_parts, *rest), name="d_norm1",
+        scratch=[pltpu.VMEM((4 * count, 768), BF16), pltpu.VMEM((4 * count, width), F32)],
+    )
+    keep, received = own_rows_sum(call, send, keep)
+    ((keep_q, send_q),) = halves(call, "hop1_attn", (keep_q, got_q))
+    got_q = exchange(send_q, "ctx", 8, UP_ORDER[1])
+    (input_grad,) = call(
+        input_grad_kernel, (sds(cot.shape, BF16),), (ids,),
+        (routed, keep, received, d_mid, both, d_logit, w_router, gain_attn, cot), name="input_grad",
+    )
+    send_u, mine_u = call(
+        last_kernel, (local((128, hidden // 2), BF16), local((128, hidden // 2), F32)),
+        (), (keep_u, got_u), name="hop3",
+    )
+    other_u = exchange(send_u, "ctx", 8, 1)
+    ((keep_q, send_q),) = halves(call, "hop2_attn", (keep_q, got_q))
+    got_q = exchange(send_q, "ctx", 8, 4)
+    chunks = call(
+        up_pieces_kernel, (local((32, hidden + 128), F32),) * 4, (ids,), (mine_u, other_u, w_up_rows),
+        name="up_pieces",
+    )
+    chunks = swap_pieces(chunks)
+    *qkv_chunks, grad_out = call(
+        pieces_kernel, (local((32, 1024), F32),) * 4 + (local((32, width), F32),), (ids,),
+        (keep_q, got_q, w_qkv_rows), name="qkv_pieces",
+    )
+    qkv_chunks = swap_pieces(qkv_chunks)
+    grad_out = lax.ppermute(grad_out, ("ctx", "fsdp"), owners)
+    (grad_down,) = call(
+        join_down_kernel, (sds((128, width), F32),), (), (down0, down1), name="join_down"
+    )
+    row = sds((1, 32), F32)
+    grad_up, grad_gain_mlp = call(
+        join_up_kernel, (sds((32, 4 * hidden), F32), row), (ids,), (*chunks, gain_mlp), name="join_up"
+    )
+    grad_qkv, grad_gain_attn, grad_router = call(
+        join_qkv_kernel, (sds((32, 3 * width), F32), row, row), (ids,), (*qkv_chunks, gain_attn),
+        name="join_qkv",
+    )
+    return (
+        output[:, None], input_grad[:, None], grad_router[0], grad_gain_attn[0], grad_qkv, grad_out,
+        grad_gain_mlp[0], grad_up, grad_down,
+    )
+
+
 def solution(mesh):
     placed = (
         P(None, "fsdp", "ctx", None),
@@ -197,8 +1088,9 @@
         P(),
         P(None, "fsdp", "ctx", None),
     )
+    fits = mesh.shape["ctx"] == 8 and mesh.shape["fsdp"] == 4
     return jax.shard_map(
-        shards,
+        shards_8x4 if fits else shards,
         mesh=mesh,
         in_specs=placed,
         out_specs=(

time: 1520 us -> 231 us (0.15)
  waiting for transfers between devices: 961 us -> 103 us
  blocking collectives: 264 us -> 0 us
  matrix products: 154 us -> 0 us
  starting transfers between devices: 1.18 us -> 83.2 us
  local copies, waits for them, and re-layouts: 63.5 us -> 3.3 us
  other arithmetic: 53.5 us -> 0.07 us
  Pallas kernels: 0 us -> 39.1 us
    reduce_scatter x10 -> x0, waiting for transfers between devices: 884 us -> none  [the longest x3 195 us: shards(): lax.psum_scatter(d_key_part.reshape(total, width), 'ctx', scatter_dimensi...]
    all_gather x7 -> x0, blocking collectives: 222 us -> none  [the longest x3 98.6 us: shards(): lax.all_gather(values_local, 'ctx', axis=0, tiled=True)]
    dot_general x52 -> x0, matrix products: 154 us -> none  [the longest x4 26.5 us: outer_sum(): lax.dot_general(left, right, (((0,), (0,)), ((), ())), preferred_element_...]
    ppermute x0 -> x70, waiting for transfers between devices: none -> 103 us  [the longest x63 81.2 us: exchange(): return lax.ppermute(x, axis, [(i, i ^ mask) for i in range(size)])]
    ppermute x0 -> x70, starting transfers between devices: none -> 83.2 us  [the longest x63 67.7 us: exchange(): return lax.ppermute(x, axis, [(i, i ^ mask) for i in range(size)])]
    all_gather x4 -> x0, waiting for transfers between devices: 74.6 us -> none  [the longest x1 54.8 us: fetch(): lax.all_gather(w_down, 'fsdp', axis=0, tiled=True)]
    unnamed x1 -> x0, blocking collectives: 41.4 us -> none
    pallas_call x0 -> x33, Pallas kernels: none -> 39.1 us  [__call__(): pl.pallas_call(body, out_shape=tuple(outs), in_specs=[pl.BlockSpec(memory...]
  transfers between devices with their start and end apart: 14 -> 70, of which waited for: 13 -> 22; matrix products, arithmetic and copies ran while one was open for 10% -> 0% of each run, Pallas kernels for 0% -> 12%
where the time goes in v2:
time: 231 us; the launch traced here: 230 us
  waiting for transfers between devices  103 us (45%)
  starting transfers between devices  83.2 us (36%)
  Pallas kernels  39.1 us (17%)
  local copies, waits for them, and re-layouts  3.3 us (1%)
    ppermute x63, waiting for transfers between devices, exchange(): return lax.ppermute(x, axis, [(i, i ^ mask) for i in range(size)])  81.2 us
    ppermute x63, starting transfers between devices, exchange(): return lax.ppermute(x, axis, [(i, i ^ mask) for i in range(size)])  67.7 us
    pallas_call x33, Pallas kernels, __call__(): pl.pallas_call(body, out_shape=tuple(outs), in_specs=[pl.BlockSpec(memory...  39.1 us
    ppermute x2, waiting for transfers between devices, swap_across(): lax.ppermute(across, ('ctx', 'fsdp'), [(4 * a + b, 4 * a + (b ^ 2 + (a &...  15.5 us
    ppermute x1, waiting for transfers between devices, shards_8x4(): grad_out = lax.ppermute(grad_out, ('ctx', 'fsdp'), owners)  6 us
  transfers between devices with their start and end apart: 70, of which 22 were waited for; matrix products, arithmetic and copies ran while one was open for 0% of the time, Pallas kernels for 12%

profile of v2, /device:TPU:4, one launch (start us, length us, event | category | flops | bytes accessed | tf_op | source)
XLA Modules:
  0.0 229.5 jit_solution(17463575215006514195)
XLA Ops:
  6.5 3.8 %collective-permute-start.1 = (bf16[104,1024]{1,0:T(8,128)(2,1)S(1)}, bf16[104,1024]{1,0:T(8,128)(2,1)S(1)}, u32[]{:S(2)}, u32[]{:S(2)}) collective-permute-start(bf16[104,1024]{1,0:T(8,128)(2,1)S(1)} %get-tuple-element.109.refs_2_.refs_3_), channel_id=1, source_target_pairs={{0,16},{1,20},{2,24},{3,28},{4,17},{5,21},{6,25},{7,29},{8,18},{9,... | collective-permute-start | bytes 638984 | tf_op jit(solution)/shard_map/ppermute | solution.py:915
  13.7 10.5 %collective-permute-done.6.refs_8_.refs_7_.refs_11_ = bf16[256,384]{1,0:T(8,128)(2,1)S(1)} collective-permute-done((bf16[256,384]{1,0:T(8,128)(2,1)S(1)}, bf16[256,384]{1,0:T(8,128)(2,1)S(1)}, u32[]{:S(2)}, u32[]{:S(2)}) %collective-permute-start.6) | collective-permute-done | bytes 196640 | tf_op jit(solution)/shard_map/ppermute | solution.py:873
  30.5 9.5 %collective-permute-done.2.refs_2_ = bf16[2,104,1024]{2,1,0:T(8,128)(2,1)S(1)} collective-permute-done((bf16[2,104,1024]{2,1,0:T(8,128)(2,1)S(1)}, bf16[2,104,1024]{2,1,0:T(8,128)(2,1)S(1)}, u32[]{:S(2)}, u32[]{:S(2)}) %collective-permute-start.2) | collective-permute-done | bytes 426016 | tf_op jit(solution)/shard_map/ppermute | solution.py:267
  44.8 3.3 %attend.1 = (bf16[96,128]{1,0:T(8,128)(2,1)S(1)}, bf16[96,128]{1,0:T(8,128)(2,1)S(1)}, bf16[96,128]{1,0:T(8,128)(2,1)S(1)}, bf16[96,128]{1,0:T(8,128)(2,1)S(1)},...) custom-call(s32[2]{0:T(128)S(1)} %pad_add_fusion.refs_0_, ...), custom_call_target="tpu_custom_call" | custom-call | flops 10000000000 | bytes 1000000 | tf_op jit(solution)/shard_map/attend/pallas_call | solution.py:222
  50.6 2.9 %collective-permute-start.13 = (bf16[96,128]{1,0:T(8,128)(2,1)S(1)}, bf16[96,128]{1,0:T(8,128)(2,1)S(1)}, u32[]{:S(2)}, u32[]{:S(2)}) collective-permute-start(bf16[96,128]{1,0:T(8,128)(2,1)S(1)} %get-tuple-element.120), channel_id=1, source_target_pairs={{0,24},{4,28},{8,16},{12,20},{16,8},{20,12},{24,0},{28,4},{1,25},{... | collective-permute-start | bytes 73736 | tf_op jit(solution)/shard_map/ppermute | solution.py:267
  53.4 5.0 %collective-permute-done.15.refs_11_.refs_6_.refs_3_ = bf16[256,1024]{1,0:T(8,128)(2,1)S(1)} collective-permute-done((bf16[256,1024]{1,0:T(8,128)(2,1)S(1)}, bf16[256,1024]{1,0:T(8,128)(2,1)S(1)}, u32[]{:S(2)}, u32[]{:S(2)}) %collective-permute-start.15) | collective-permute-done | bytes 524320 | tf_op jit(solution)/shard_map/ppermute | solution.py:873
  58.4 2.8 %collective-permute-start.14 = (bf16[96,128]{1,0:T(8,128)(2,1)S(1)}, bf16[96,128]{1,0:T(8,128)(2,1)S(1)}, u32[]{:S(2)}, u32[]{:S(2)}) collective-permute-start(bf16[96,128]{1,0:T(8,128)(2,1)S(1)} %get-tuple-element.121), channel_id=1, source_target_pairs={{0,28},{4,24},{8,20},{12,16},{16,12},{20,8},{24,4},{28,0},{1,29},{... | collective-permute-start | bytes 73736 | tf_op jit(solution)/shard_map/ppermute | solution.py:267
  61.4 3.8 %collective-permute-done.14.refs_8_ = bf16[96,128]{1,0:T(8,128)(2,1)S(1)} collective-permute-done((bf16[96,128]{1,0:T(8,128)(2,1)S(1)}, bf16[96,128]{1,0:T(8,128)(2,1)S(1)}, u32[]{:S(2)}, u32[]{:S(2)}) %collective-permute-start.14) | collective-permute-done | bytes 24608 | tf_op jit(solution)/shard_map/ppermute | solution.py:267
  70.9 8.3 %collective-permute-done.18.refs_1_ = bf16[2,96,1024]{2,1,0:T(8,128)(2,1)S(1)} collective-permute-done((bf16[2,96,1024]{2,1,0:T(8,128)(2,1)S(1)}, bf16[2,96,1024]{2,1,0:T(8,128)(2,1)S(1)}, u32[]{:S(2)}, u32[]{:S(2)}) %collective-permute-start.18) | collective-permute-done | bytes 393248 | tf_op jit(solution)/shard_map/ppermute | solution.py:267
  79.7 4.0 %collective-permute-done.23.refs_7_.refs_4_ = bf16[256,1024]{1,0:T(8,128)(2,1)S(1)} collective-permute-done((bf16[256,1024]{1,0:T(8,128)(2,1)S(1)}, bf16[256,1024]{1,0:T(8,128)(2,1)S(1)}, u32[]{:S(2)}, u32[]{:S(2)}) %collective-permute-start.23) | collective-permute-done | bytes 524320 | tf_op jit(solution)/shard_map/ppermute | solution.py:267
  83.7 4.1 %mlp.1 = (bf16[2,96,1024]{2,1,0:T(8,128)(2,1)S(1)}, f32[2,96,1024]{2,1,0:T(8,128)S(1)}, bf16[384,512]{1,0:T(8,128)(2,1)S(1)}, bf16[384,512]{1,0:T(8,128)(2,1)S(1...) custom-call(s32[2]{0:T(128)S(1)} %pad_add_fusion.refs_0_, ...), custom_call_target="tpu_custom_call" | custom-call | flops 10000000000 | bytes 1000000 | tf_op jit(solution)/shard_map/mlp/pallas_call | solution.py:222
  93.2 6.7 %collective-permute-done.26.refs_9_.refs_5_ = bf16[384,512]{1,0:T(8,128)(2,1)S(1)} collective-permute-done((bf16[384,512]{1,0:T(8,128)(2,1)S(1)}, bf16[384,512]{1,0:T(8,128)(2,1)S(1)}, u32[]{:S(2)}, u32[]{:S(2)}) %collective-permute-start.26) | collective-permute-done | bytes 393248 | tf_op jit(solution)/shard_map/ppermute | solution.py:267
  103.1 4.7 %collective-permute-done.24.refs_2_ = bf16[192,1024]{1,0:T(8,128)(2,1)S(1)} collective-permute-done((bf16[192,1024]{1,0:T(8,128)(2,1)S(1)}, bf16[192,1024]{1,0:T(8,128)(2,1)S(1)}, u32[]{:S(2)}, u32[]{:S(2)}) %collective-permute-start.24) | collective-permute-done | bytes 393248 | tf_op jit(solution)/shard_map/ppermute | solution.py:267
  130.0 3.0 %attend_back.1 = (bf16[96,384]{1,0:T(8,128)(2,1)S(1)}, bf16[96,384]{1,0:T(8,128)(2,1)S(1)}, bf16[96,384]{1,0:T(8,128)(2,1)S(1)}, bf16[96,384]{1,0:T(8,128)(2,1)S...) custom-call(s32[2]{0:T(128)S(1)} %pad_add_fusion.refs_0_, ...), custom_call_target="tpu_custom_call" | custom-call | flops 10000000000 | bytes 1000000 | tf_op jit(solution)/shard_map/attend_back/pallas_call | solution.py:222
  139.9 5.2 %collective-permute-done.47.refs_2_ = bf16[96,384]{1,0:T(8,128)(2,1)S(1)} collective-permute-done((bf16[96,384]{1,0:T(8,128)(2,1)S(1)}, bf16[96,384]{1,0:T(8,128)(2,1)S(1)}, u32[]{:S(2)}, u32[]{:S(2)}) %collective-permute-start.47) | collective-permute-done | bytes 73760 | tf_op jit(solution)/shard_map/ppermute | solution.py:267
  162.0 4.4 %collective-permute-start.58 = (bf16[1,256,512]{2,1,0:T(8,128)(2,1)S(1)}, bf16[1,256,512]{2,1,0:T(8,128)(2,1)S(1)}, u32[]{:S(2)}, u32[]{:S(2)}) collective-permute-start(bf16[1,256,512]{2,1,0:T(8,128)(2,1)S(1)} %get-tuple-element.177.refs_8_), channel_id=1, source_target_pairs={{0,16},{4,20},{8,24},{12,28},{16,0},{20,4},{24,8},{28,12},{1,17},{... | collective-permute-start | bytes 786440 | tf_op jit(solution)/shard_map/ppermute | solution.py:267
  166.4 2.8 %collective-permute-start.68 = (bf16[128,1024]{1,0:T(8,128)(2,1)S(1)}, bf16[128,1024]{1,0:T(8,128)(2,1)S(1)}, u32[]{:S(2)}, u32[]{:S(2)}) collective-permute-start(bf16[128,1024]{1,0:T(8,128)(2,1)S(1)} %get-tuple-element.207), channel_id=1, source_target_pairs={{0,0},{1,8},{2,16},{3,24},{4,1},{5,9},{6,17},{7,25},{8,2},{9,10},{... | collective-permute-start | bytes 786440 | tf_op jit(solution)/shard_map/ppermute | solution.py:1024
  170.7 8.9 %collective-permute-done.56.refs_1_ = bf16[4,136,640]{2,1,0:T(8,128)(2,1)S(1)} collective-permute-done((bf16[4,136,640]{2,1,0:T(8,128)(2,1)S(1)}, bf16[4,136,640]{2,1,0:T(8,128)(2,1)S(1)}, u32[]{:S(2)}, u32[]{:S(2)}) %collective-permute-start.56) | collective-permute-done | bytes 696352 | tf_op jit(solution)/shard_map/ppermute | solution.py:267
  179.8 6.1 %collective-permute-start.57 = (bf16[2,136,640]{2,1,0:T(8,128)(2,1)S(1)}, bf16[2,136,640]{2,1,0:T(8,128)(2,1)S(1)}, u32[]{:S(2)}, u32[]{:S(2)}) collective-permute-start(bf16[2,136,640]{2,1,0:T(8,128)(2,1)S(1)} %get-tuple-element.185.refs_10_.refs_2_), channel_id=1, source_target_pairs={{0,8},{4,12},{8,0},{12,4},{16,24},{20,28},{24,16},{28,20},{1,9},{5... | collective-permute-start | bytes 1044488 | tf_op jit(solution)/shard_map/ppermute | solution.py:267
  185.9 4.5 %collective-permute-done.58.refs_1_ = bf16[1,256,512]{2,1,0:T(8,128)(2,1)S(1)} collective-permute-done((bf16[1,256,512]{2,1,0:T(8,128)(2,1)S(1)}, bf16[1,256,512]{2,1,0:T(8,128)(2,1)S(1)}, u32[]{:S(2)}, u32[]{:S(2)}) %collective-permute-start.58) | collective-permute-done | bytes 262176 | tf_op jit(solution)/shard_map/ppermute | solution.py:267
  194.3 8.6 %collective-permute-done.57.refs_1_ = bf16[2,136,640]{2,1,0:T(8,128)(2,1)S(1)} collective-permute-done((bf16[2,136,640]{2,1,0:T(8,128)(2,1)S(1)}, bf16[2,136,640]{2,1,0:T(8,128)(2,1)S(1)}, u32[]{:S(2)}, u32[]{:S(2)}) %collective-permute-start.57) | collective-permute-done | bytes 348192 | tf_op jit(solution)/shard_map/ppermute | solution.py:267
  204.4 8.7 %collective-permute-done.59.refs_2_ = bf16[1,136,640]{2,1,0:T(8,128)(2,1)S(1)} collective-permute-done((bf16[1,136,640]{2,1,0:T(8,128)(2,1)S(1)}, bf16[1,136,640]{2,1,0:T(8,128)(2,1)S(1)}, u32[]{:S(2)}, u32[]{:S(2)}) %collective-permute-start.59) | collective-permute-done | bytes 174112 | tf_op jit(solution)/shard_map/ppermute | solution.py:267
  216.8 3.1 %collective-permute-start.64 = (f32[32,1024]{1,0:T(8,128)S(1)}, f32[32,1024]{1,0:T(8,128)S(1)}, u32[]{:S(2)}, u32[]{:S(2)}) collective-permute-start(f32[32,1024]{1,0:T(8,128)S(1)} %get-tuple-element.201), channel_id=1, source_target_pairs={{0,0},{1,8},{2,16},{3,24},{4,1},{5,9},{6,17},{7,25},{8,2},{9,10},{... | collective-permute-start | bytes 393224 | tf_op jit(solution)/shard_map/ppermute | solution.py:1059
  221.4 6.0 %collective-permute-done.64 = f32[32,1024]{1,0:T(8,128)S(1)} collective-permute-done((f32[32,1024]{1,0:T(8,128)S(1)}, f32[32,1024]{1,0:T(8,128)S(1)}, u32[]{:S(2)}, u32[]{:S(2)}) %collective-permute-start.64) | collective-permute-done | bytes 131104 | tf_op jit(solution)/shard_map/ppermute | solution.py:1059
  (171 shorter events, 97.4 us)
Async XLA Ops:
  4.5 22.3 %collective-permute-start = (bf16[104,1024]{1,0:T(8,128)(2,1)S(1)}, bf16[104,1024]{1,0:T(8,128)(2,1)S(1)}, u32[]{:S(2)}, u32[]{:S(2)}) collective-permute-start(bf16[104,1024]{1,0:T(8,128)(2,1)S(1)} %get-tuple-element.109.refs_2_.refs_3_), channel_id=1, source_target_pairs={{0,0},{1,4},{2,8},{3,12},{4,1},{5,5},{6,9},{7,13},{8,2},{9,6},{10,... | collective-permute-start | bytes 638984 | tf_op jit(solution)/shard_map/ppermute | solution.py:914
  6.5 20.4 %collective-permute-start.1 = (bf16[104,1024]{1,0:T(8,128)(2,1)S(1)}, bf16[104,1024]{1,0:T(8,128)(2,1)S(1)}, u32[]{:S(2)}, u32[]{:S(2)}) collective-permute-start(bf16[104,1024]{1,0:T(8,128)(2,1)S(1)} %get-tuple-element.109.refs_2_.refs_3_), channel_id=1, source_target_pairs={{0,16},{1,20},{2,24},{3,28},{4,17},{5,21},{6,25},{7,29},{8,18},{9,... | collective-permute-start | bytes 638984 | tf_op jit(solution)/shard_map/ppermute | solution.py:915
  10.3 13.9 %collective-permute-start.6 = (bf16[256,384]{1,0:T(8,128)(2,1)S(1)}, bf16[256,384]{1,0:T(8,128)(2,1)S(1)}, u32[]{:S(2)}, u32[]{:S(2)}) collective-permute-start(bf16[256,384]{1,0:T(8,128)(2,1)S(1)} %get-tuple-element.112), channel_id=1, source_target_pairs={{0,2},{1,3},{2,0},{3,1},{4,7},{5,6},{6,5},{7,4},{8,10},{9,11},{10,... | collective-permute-start | bytes 589832 | tf_op jit(solution)/shard_map/ppermute | solution.py:873
  11.8 30.6 %collective-permute-start.5 = (bf16[256,384]{1,0:T(8,128)(2,1)S(1)}, bf16[256,384]{1,0:T(8,128)(2,1)S(1)}, u32[]{:S(2)}, u32[]{:S(2)}) collective-permute-start(bf16[256,384]{1,0:T(8,128)(2,1)S(1)} %get-tuple-element.111), channel_id=1, source_target_pairs={{0,1},{1,0},{2,3},{3,2},{4,5},{5,4},{6,7},{7,6},{8,9},{9,8},{10,11... | collective-permute-start | bytes 589832 | tf_op jit(solution)/shard_map/ppermute | solution.py:267
  24.2 20.6 %collective-permute-start.7 = (bf16[256,384]{1,0:T(8,128)(2,1)S(1)}, bf16[256,384]{1,0:T(8,128)(2,1)S(1)}, u32[]{:S(2)}, u32[]{:S(2)}) collective-permute-start(bf16[256,384]{1,0:T(8,128)(2,1)S(1)} %collective-permute-done.6.refs_8_.refs_7_.refs_11_), channel_id=1, source_target_pairs={{0,4},{4,0},{8,12},{12,8},{16,20},{20,16},{24,28},{28,24},{1,5},{5... | collective-permute-start | bytes 589832 | tf_op jit(solution)/shard_map/ppermute | solution.py:267
  29.4 15.3 %collective-permute-start.3 = (bf16[2,104,1024]{2,1,0:T(8,128)(2,1)S(1)}, bf16[2,104,1024]{2,1,0:T(8,128)(2,1)S(1)}, u32[]{:S(2)}, u32[]{:S(2)}) collective-permute-start(bf16[2,104,1024]{2,1,0:T(8,128)(2,1)S(1)} %pair.1.refs_4_.refs_1_), channel_id=1, source_target_pairs={{0,1},{1,0},{2,3},{3,2},{4,5},{5,4},{6,7},{7,6},{8,9},{9,8},{10,11... | collective-permute-start | bytes 1277960 | tf_op jit(solution)/shard_map/ppermute | solution.py:267
  30.4 20.2 %collective-permute-start.16 = (bf16[200,1024]{1,0:T(8,128)(2,1)S(1)}, bf16[200,1024]{1,0:T(8,128)(2,1)S(1)}, u32[]{:S(2)}, u32[]{:S(2)}) collective-permute-start(bf16[200,1024]{1,0:T(8,128)(2,1)S(1)} %cot_rows.1.refs_3_.refs_0_.refs_2_.refs_4_.refs_5_), channel_id=1, source_target_pairs={{0,2},{1,3},{2,0},{3,1},{4,6},{5,7},{6,4},{7,5},{8,10},{9,11},{10,... | collective-permute-start | bytes 1228808 | tf_op jit(solution)/shard_map/ppermute | solution.py:267
  42.5 15.9 %collective-permute-start.15 = (bf16[256,1024]{1,0:T(8,128)(2,1)S(1)}, bf16[256,1024]{1,0:T(8,128)(2,1)S(1)}, u32[]{:S(2)}, u32[]{:S(2)}) collective-permute-start(bf16[256,1024]{1,0:T(8,128)(2,1)S(1)} %get-tuple-element.122), channel_id=1, source_target_pairs={{0,2},{1,3},{2,0},{3,1},{4,7},{5,6},{6,5},{7,4},{8,10},{9,11},{10,... | collective-permute-start | bytes 1572872 | tf_op jit(solution)/shard_map/ppermute | solution.py:873
  69.3 14.3 %collective-permute-start.23 = (bf16[256,1024]{1,0:T(8,128)(2,1)S(1)}, bf16[256,1024]{1,0:T(8,128)(2,1)S(1)}, u32[]{:S(2)}, u32[]{:S(2)}) collective-permute-start(bf16[256,1024]{1,0:T(8,128)(2,1)S(1)} %collective-permute-done.15.refs_11_.refs_6_.refs_3_), channel_id=1, source_target_pairs={{0,4},{4,0},{8,12},{12,8},{16,20},{20,16},{24,28},{28,24},{1,5},{5... | collective-permute-start | bytes 1572872 | tf_op jit(solution)/shard_map/ppermute | solution.py:267
  90.9 16.9 %collective-permute-start.24 = (bf16[192,1024]{1,0:T(8,128)(2,1)S(1)}, bf16[192,1024]{1,0:T(8,128)(2,1)S(1)}, u32[]{:S(2)}, u32[]{:S(2)}) collective-permute-start(bf16[192,1024]{1,0:T(8,128)(2,1)S(1)} %slice.3), channel_id=1, source_target_pairs={{0,8},{4,12},{8,0},{12,4},{16,24},{20,28},{24,16},{28,20},{1,9},{5... | collective-permute-start | bytes 1179656 | tf_op jit(solution)/shard_map/ppermute | solution.py:267
  92.9 15.1 %collective-permute-start.27 = (bf16[2,96,1024]{2,1,0:T(8,128)(2,1)S(1)}, bf16[2,96,1024]{2,1,0:T(8,128)(2,1)S(1)}, u32[]{:S(2)}, u32[]{:S(2)}) collective-permute-start(bf16[2,96,1024]{2,1,0:T(8,128)(2,1)S(1)} %get-tuple-element.127.refs_1_), channel_id=1, source_target_pairs={{0,4},{4,0},{8,12},{12,8},{16,20},{20,16},{24,28},{28,24},{1,5},{5... | collective-permute-start | bytes 1179656 | tf_op jit(solution)/shard_map/ppermute | solution.py:267
  114.9 14.3 %collective-permute-start.36 = (bf16[96,128]{1,0:T(8,128)(2,1)S(1)}, bf16[96,128]{1,0:T(8,128)(2,1)S(1)}, u32[]{:S(2)}, u32[]{:S(2)}) collective-permute-start(bf16[96,128]{1,0:T(8,128)(2,1)S(1)} %get-tuple-element.150), channel_id=1, source_target_pairs={{0,12},{4,8},{8,4},{12,0},{16,28},{20,24},{24,20},{28,16},{1,13},{... | collective-permute-start | bytes 73736 | tf_op jit(solution)/shard_map/ppermute | solution.py:267
  116.0 13.2 %collective-permute-start.37 = (bf16[96,128]{1,0:T(8,128)(2,1)S(1)}, bf16[96,128]{1,0:T(8,128)(2,1)S(1)}, u32[]{:S(2)}, u32[]{:S(2)}) collective-permute-start(bf16[96,128]{1,0:T(8,128)(2,1)S(1)} %get-tuple-element.151), channel_id=1, source_target_pairs={{0,16},{4,20},{8,24},{12,28},{16,0},{20,4},{24,8},{28,12},{1,17},{... | collective-permute-start | bytes 73736 | tf_op jit(solution)/shard_map/ppermute | solution.py:267
  129.2 19.1 %collective-permute-start.46 = (bf16[2,128,1024]{2,1,0:T(8,128)(2,1)S(1)}, bf16[2,128,1024]{2,1,0:T(8,128)(2,1)S(1)}, u32[]{:S(2)}, u32[]{:S(2)}) collective-permute-start(bf16[2,128,1024]{2,1,0:T(8,128)(2,1)S(1)} %get-tuple-element.144.refs_8_), channel_id=1, source_target_pairs={{0,4},{4,0},{8,12},{12,8},{16,20},{20,16},{24,28},{28,24},{1,5},{5... | collective-permute-start | bytes 1572872 | tf_op jit(solution)/shard_map/ppermute | solution.py:267
  130.0 19.2 %collective-permute-start.45 = (bf16[2,256,512]{2,1,0:T(8,128)(2,1)S(1)}, bf16[2,256,512]{2,1,0:T(8,128)(2,1)S(1)}, u32[]{:S(2)}, u32[]{:S(2)}) collective-permute-start(bf16[2,256,512]{2,1,0:T(8,128)(2,1)S(1)} %get-tuple-element.143.refs_6_), channel_id=1, source_target_pairs={{0,8},{4,12},{8,0},{12,4},{16,24},{20,28},{24,16},{28,20},{1,9},{5... | collective-permute-start | bytes 1572872 | tf_op jit(solution)/shard_map/ppermute | solution.py:267
  135.1 16.7 %collective-permute-start.44 = (bf16[96,1024]{1,0:T(8,128)(2,1)S(1)}, bf16[96,1024]{1,0:T(8,128)(2,1)S(1)}, u32[]{:S(2)}, u32[]{:S(2)}) collective-permute-start(bf16[96,1024]{1,0:T(8,128)(2,1)S(1)} %get-tuple-element.174.refs_4_), channel_id=1, source_target_pairs={{0,2},{1,3},{2,0},{3,1},{4,6},{5,7},{6,4},{7,5},{8,10},{9,11},{10,... | collective-permute-start | bytes 589832 | tf_op jit(solution)/shard_map/ppermute | solution.py:267
  161.6 18.0 %collective-permute-start.56 = (bf16[4,136,640]{2,1,0:T(8,128)(2,1)S(1)}, bf16[4,136,640]{2,1,0:T(8,128)(2,1)S(1)}, u32[]{:S(2)}, u32[]{:S(2)}) collective-permute-start(bf16[4,136,640]{2,1,0:T(8,128)(2,1)S(1)} %get-tuple-element.172.refs_2_), channel_id=1, source_target_pairs={{0,4},{4,0},{8,12},{12,8},{16,20},{20,16},{24,28},{28,24},{1,5},{5... | collective-permute-start | bytes 2088968 | tf_op jit(solution)/shard_map/ppermute | solution.py:267
  162.0 28.4 %collective-permute-start.58 = (bf16[1,256,512]{2,1,0:T(8,128)(2,1)S(1)}, bf16[1,256,512]{2,1,0:T(8,128)(2,1)S(1)}, u32[]{:S(2)}, u32[]{:S(2)}) collective-permute-start(bf16[1,256,512]{2,1,0:T(8,128)(2,1)S(1)} %get-tuple-element.177.refs_8_), channel_id=1, source_target_pairs={{0,16},{4,20},{8,24},{12,28},{16,0},{20,4},{24,8},{28,12},{1,17},{... | collective-permute-start | bytes 786440 | tf_op jit(solution)/shard_map/ppermute | solution.py:267
  166.4 47.3 %collective-permute-start.68 = (bf16[128,1024]{1,0:T(8,128)(2,1)S(1)}, bf16[128,1024]{1,0:T(8,128)(2,1)S(1)}, u32[]{:S(2)}, u32[]{:S(2)}) collective-permute-start(bf16[128,1024]{1,0:T(8,128)(2,1)S(1)} %get-tuple-element.207), channel_id=1, source_target_pairs={{0,0},{1,8},{2,16},{3,24},{4,1},{5,9},{6,17},{7,25},{8,2},{9,10},{... | collective-permute-start | bytes 786440 | tf_op jit(solution)/shard_map/ppermute | solution.py:1024
  169.2 44.6 %collective-permute-start.69 = (bf16[128,1024]{1,0:T(8,128)(2,1)S(1)}, bf16[128,1024]{1,0:T(8,128)(2,1)S(1)}, u32[]{:S(2)}, u32[]{:S(2)}) collective-permute-start(bf16[128,1024]{1,0:T(8,128)(2,1)S(1)} %get-tuple-element.208), channel_id=1, source_target_pairs={{16,0},{17,8},{18,16},{19,24},{20,1},{21,9},{22,17},{23,25},{24,2}... | collective-permute-start | bytes 786440 | tf_op jit(solution)/shard_map/ppermute | solution.py:1025
  169.4 22.5 %collective-permute-start.55 = (bf16[96,1024]{1,0:T(8,128)(2,1)S(1)}, bf16[96,1024]{1,0:T(8,128)(2,1)S(1)}, u32[]{:S(2)}, u32[]{:S(2)}) collective-permute-start(bf16[96,1024]{1,0:T(8,128)(2,1)S(1)} %get-tuple-element.183.refs_2_), channel_id=1, source_target_pairs={{0,2},{1,3},{2,0},{3,1},{4,6},{5,7},{6,4},{7,5},{8,10},{9,11},{10,... | collective-permute-start | bytes 589832 | tf_op jit(solution)/shard_map/ppermute | solution.py:267
  179.8 23.2 %collective-permute-start.57 = (bf16[2,136,640]{2,1,0:T(8,128)(2,1)S(1)}, bf16[2,136,640]{2,1,0:T(8,128)(2,1)S(1)}, u32[]{:S(2)}, u32[]{:S(2)}) collective-permute-start(bf16[2,136,640]{2,1,0:T(8,128)(2,1)S(1)} %get-tuple-element.185.refs_10_.refs_2_), channel_id=1, source_target_pairs={{0,8},{4,12},{8,0},{12,4},{16,24},{20,28},{24,16},{28,20},{1,9},{5... | collective-permute-start | bytes 1044488 | tf_op jit(solution)/shard_map/ppermute | solution.py:267
  213.7 13.7 %collective-permute-start.61 = (f32[32,1024]{1,0:T(8,128)S(1)}, f32[32,1024]{1,0:T(8,128)S(1)}, u32[]{:S(2)}, u32[]{:S(2)}) collective-permute-start(f32[32,1024]{1,0:T(8,128)S(1)} %get-tuple-element.195), channel_id=1, source_target_pairs={{0,1},{1,0},{2,3},{3,2},{4,5},{5,4},{6,7},{7,6},{8,9},{9,8},{10,11... | collective-permute-start | bytes 393224 | tf_op jit(solution)/shard_map/ppermute | solution.py:267
  213.8 13.6 %collective-permute-start.62 = (f32[32,1024]{1,0:T(8,128)S(1)}, f32[32,1024]{1,0:T(8,128)S(1)}, u32[]{:S(2)}, u32[]{:S(2)}) collective-permute-start(f32[32,1024]{1,0:T(8,128)S(1)} %get-tuple-element.196), channel_id=1, source_target_pairs={{0,2},{1,3},{2,0},{3,1},{4,6},{5,7},{6,4},{7,5},{8,10},{9,11},{10,... | collective-permute-start | bytes 393224 | tf_op jit(solution)/shard_map/ppermute | solution.py:267
  (55 other events, 489.0 us)

commit v3 on v2

--- a/solution.py
+++ b/solution.py
@@ -17,7 +17,6 @@
 HIGHEST = lax.Precision.HIGHEST
 BF16, F32 = jnp.bfloat16, jnp.float32
 VMEM_LIMIT = 24 * 2**20
-UP_ORDER = (1, 2, 4)
 WEIGHT = 10**10
 
 
@@ -238,17 +237,12 @@
         return results
 
     def hold(self, x, *after):
-        (x,) = self(hold_kernel, (local(x.shape, x.dtype),), (), (x,), after=after, name="hold")
+        (x,) = self(hold_kernel, (local(x.shape, x.dtype),), (), (x,), after=after, name="hold", weight=0)
         return x
 
 
 def hold_kernel(x, out):
     out[...] = x[...]
-
-
-def pair_kernel(a, b, out):
-    out[0] = a[...]
-    out[1] = b[...]
 
 
 def mm(left, right):
@@ -285,19 +279,19 @@
     return jnp.where(iota(shape, 0) == index, 1.0, 0.0)
 
 
-def share_peers(ids):
-    return ids[1], ids[1] ^ 1, ids[1] ^ (2 + (ids[0] & 1))
-
-
-def share_rows(c, f):
-    y = c & 1
-    return f, f ^ 1, f ^ (2 + y), f ^ (3 - y)
+def share_peers(ids, bit):
+    return ids[1], ids[1] ^ 1, ids[1] ^ (2 + ((ids[0] >> bit) & 1))
+
+
+def share_rows(c, f, bit):
+    side = (c >> bit) & 1
+    return f, f ^ 1, f ^ (2 + side), f ^ (3 - side)
 
 
 def cut_qkv(ids, half, w_qkv, pieces, sem, first, by_y=True):
     width = w_qkv.shape[1] // 3
     copies = []
-    peers = share_peers(ids) if by_y else tuple(ids[1] ^ k for k in range(4))
+    peers = share_peers(ids, 0) if by_y else tuple(ids[1] ^ k for k in range(4))
     for k, (peer, piece) in enumerate(zip(peers, pieces)):
         for b in range(3):
             start = b * width + peer * (width // 4) + half * 128
@@ -338,19 +332,27 @@
         copy.wait()
 
 
-def cut_kernel(ids, w_up, w_qkv, p0, p1, p2, v0, v1, v2, v3, sem):
-    share = p0.shape[1]
-    copies = cut_qkv(ids, 1 - (ids[0] >> 2), w_qkv, (v0, v1, v2, v3), sem, 3, False)
-    for k, (peer, piece) in enumerate(zip(share_peers(ids), (p0, p1, p2))):
-        copies.append(
-            pltpu.make_async_copy(
-                w_up.at[:, pl.ds(aligned(peer * share, share), share)], piece, sem.at[k]
-            )
-        )
+def run(copies):
     for copy in copies:
         copy.start()
     for copy in copies:
         copy.wait()
+
+
+def cut_up_kernel(ids, w_up, p0, p1, p2, sem):
+    share = p0.shape[1]
+    run(
+        [
+            pltpu.make_async_copy(
+                w_up.at[:, pl.ds(aligned(peer * share, share), share)], piece, sem.at[k]
+            )
+            for k, (peer, piece) in enumerate(zip(share_peers(ids, 0), (p0, p1, p2)))
+        ]
+    )
+
+
+def cut_rest_kernel(ids, w_qkv, v0, v1, v2, v3, sem):
+    run(cut_qkv(ids, 1 - (ids[0] >> 2), w_qkv, (v0, v1, v2, v3), sem, 0, False))
 
 
 def cot_kernel(ids, routed, cot, rowsx, both):
@@ -386,29 +388,30 @@
 
 
 def attend_kernel(
-    ids, r0, r1, r2, r3, gain, w0, w1, w2, w3,
-    h0, h1, h2, h3, h4, h5, h6, h7, stack, probs, norm1, place_col, result,
+    ids, near_rows, far_rows, gain, w0, w1, w2, w3,
+    far, own, stack, probs, norm1, place_col, result,
 ):
     c, f = ids[0], ids[1]
     micros, total = stack.shape[0], stack.shape[1]
-    count = h0.shape[0]
+    count = own.shape[1]
     per = count // micros
     eye = iota((per, 128), 0) == iota((per, 128), 1)
-    for peer, source in zip((f, f ^ 2, f ^ 1, f ^ 3), (r0, r1, r2, r3)):
-        for h in range(2):
-            rows = source[h, :count].astype(F32)
-            index = ((c >> 2) ^ h) * 4 + peer
+    step = count + 8
+    for h, source in enumerate((near_rows, far_rows)):
+        for b in range(4):
+            rows = source[b * step : b * step + count].astype(F32)
+            index = ((c >> 2) ^ h) * 4 + b
             norm1[pl.ds(aligned(index * count, 16), count)] = (
                 rows * rms_factor(rows) * gain[...]
             ).astype(BF16)
-            places = source[h, count : count + 8, :128].astype(F32)
+            places = source[b * step + count : b * step + count + 8, :128].astype(F32)
             for m in range(micros):
                 col = jnp.sum(jnp.where(eye, places[m : m + 1], 0.0), axis=1, keepdims=True)
                 place_col[m, pl.ds(aligned(index * per, per), per), :] = jnp.broadcast_to(
                     col, (per, 128)
                 )
     qkv = jnp.zeros((8 * count, 384), F32)
-    for peer, w in zip(share_rows(c, f), (w0, w1, w2, w3)):
+    for peer, w in zip(share_rows(c, f, 0), (w0, w1, w2, w3)):
         part = w.shape[0]
         qkv = qkv + mm(norm1[:, pl.ds(aligned(peer * part, part), part)], w[...])
     low = qkv.astype(BF16)
@@ -434,8 +437,11 @@
             probs[2 * m + h] = weight
             attended = attended + mm(weight.astype(BF16), v) * masks[h]
         result[m] = attended.astype(BF16)
-        for k, out in enumerate((h0, h1, h2, h3, h4, h5, h6, h7)):
-            out[m * per : (m + 1) * per, :] = result[m, pl.ds(aligned((c ^ k) * per, per), per), :]
+        for k in range(8):
+            out = far if k >= 4 else own
+            out[k & 3, m * per : (m + 1) * per, :] = result[
+                m, pl.ds(aligned((c ^ k) * per, per), per), :
+            ]
 
 
 def row_slot(f, s, count):
@@ -456,10 +462,11 @@
     return pl.ds(row_slot(ids[1], peer & 3, count), count), pl.ds(columns, lanes)
 
 
-def out_kernel(ids, b0, b1, b2, b3, b4, b5, b6, b7, w_out, attended, send, keep, full):
-    count = b0.shape[0]
-    for k, block in enumerate((b0, b1, b2, b3, b4, b5, b6, b7)):
-        attended[block_place(ids, k, count, 128)] = block[...]
+def out_kernel(ids, b0, b1, b2, b3, w_out, attended, send, keep, full):
+    count = b0.shape[1]
+    for k, block in enumerate((b0, b1, b2, b3)):
+        for far in range(2):
+            attended[block_place(ids, k ^ (4 * far), count, 128)] = block[far]
     full[...] = mm(attended[...], w_out[...])
     split_rows(full, send, keep)
 
@@ -488,7 +495,7 @@
     c = ids[0]
     part = u0.shape[0]
     count = n0.shape[1]
-    shares = tuple(zip(share_rows(ids[0], ids[1]), (u0, u1, u2, u3)))
+    shares = tuple(zip(share_rows(ids[0], ids[1], 0), (u0, u1, u2, u3)))
     for i in range(2):
         norm2[i * count : (i + 1) * count] = n0[i]
         norm2[(2 + i) * count : (3 + i) * count] = n1[i]
@@ -532,25 +539,12 @@
 def pick_kernel(ids, *refs):
     shares, (up_rows, qkv_rows) = refs[:12], refs[12:]
     c, f = ids[0], ids[1]
-    for peer, u, a in zip(share_rows(c, f), shares[:4], shares[4:8]):
+    for peer, u in zip(share_rows(c, f, 0), shares[:4]):
         pick_rows(c, peer, u, up_rows, slice(None))
+    for peer, a in zip(share_rows(c, f, 0), shares[4:8]):
         pick_rows(c, peer, a, qkv_rows, slice(0, 384))
     for k, b in enumerate(shares[8:]):
         pick_rows(c, f ^ k, b, qkv_rows, slice(384, 768))
-
-
-def block_order(order):
-    one, two, three = order
-    keep = (0, three, two, two | three)
-    return keep, tuple(k | one for k in keep)
-
-
-def put_block(order, k, send, keep, where, value):
-    kept, sent = block_order(order)
-    if k in kept:
-        keep[(kept.index(k), *where)] = value
-    else:
-        send[(sent.index(k), *where)] = value.astype(BF16)
 
 
 def chunk(f, q):
@@ -593,26 +587,34 @@
 
 
 def grad_attn_kernel(
-    ids, norm1, b0, b1, b2, b3, b4, b5, b6, b7, attended, d_attn, router, send, keep, joined, full,
+    ids, norm1, b0, b1, b2, b3, b4, b5, b6, b7, attended, d_attn, router,
+    keep, send1, send2, send3, joined, full,
 ):
     count = b0.shape[0]
     for k, block in enumerate((b0, b1, b2, b3, b4, b5, b6, b7)):
         joined[pl.ds(aligned((ids[0] ^ k) * count, 16), count)] = block[...]
     full[...] = t_mm(attended[...], d_attn[...])
     for k in range(8):
+        target, index = (keep, send1, send2, send3)[k & 3], k >> 2
         owner = ids[0] ^ k
         start = aligned(owner * 128, 128)
         value = t_mm(norm1[:, pl.ds(start, 128)], joined[...])
         for q in range(4):
-            where = (chunk(ids[1], q), slice(0, 384))
-            put_block(UP_ORDER, k, send, keep, where, value[q * 32 : (q + 1) * 32])
-            where = (slice(q * 32, (q + 1) * 32), slice(384, 640))
+            piece = value[q * 32 : (q + 1) * 32]
+            target[index, chunk(ids[1], q), :384] = piece.astype(target.dtype)
             rows = full[pl.ds(aligned(owner * 32, 32), 32), q * 256 : (q + 1) * 256]
-            put_block(UP_ORDER, k, send, keep, where, rows)
-        below = slice(128, 136)
-        put_block(UP_ORDER, k, send, keep, (below, slice(128, 640)), jnp.zeros((8, 512), F32))
+            target[index, q * 32 : (q + 1) * 32, 384:640] = rows.astype(target.dtype)
+        target[index, 128:136, :] = jnp.zeros((8, 640), target.dtype)
         share = jnp.broadcast_to(router[:, pl.ds(start, 128)], (8, 128))
-        put_block(UP_ORDER, k, send, keep, (below, slice(0, 128)), share)
+        target[index, 128:136, 384:512] = share.astype(target.dtype)
+
+
+def sum_attn_kernel(keep, got1, got2, got3, send, mine):
+    for index, target in ((0, mine), (1, send)):
+        total = (keep[index] + got1[index].astype(F32)) + (
+            got2[index].astype(F32) + got3[index].astype(F32)
+        )
+        target[0] = total.astype(target.dtype)
 
 
 def d_attn_kernel(low, received, attn, both0, both1, gate, gain, d_mid_out, d_attn):
@@ -627,18 +629,19 @@
             d_mid_out[...] = d_mid
 
 
-def d_attended_kernel(ids, d0, d1, w_out, b0, b1, b2, b3, b4, b5, b6, b7, d_attn, d_att):
+def d_attended_kernel(ids, d0, d1, w_out, far, own, d_attn, d_att):
     count = d0.shape[1]
     for i in range(2):
         d_attn[i * count : (i + 1) * count] = d0[i]
         d_attn[(2 + i) * count : (3 + i) * count] = d1[i]
     d_att[...] = mm_t(d_attn[...], w_out[...])
-    for k, block in enumerate((b0, b1, b2, b3, b4, b5, b6, b7)):
-        block[...] = d_att[block_place(ids, k, count, 128)].astype(BF16)
+    for k in range(8):
+        block = far if k >= 4 else own
+        block[k & 3] = d_att[block_place(ids, k, count, 128)].astype(BF16)
 
 
 def attend_back_kernel(ids, *refs):
-    blocks, (stack, probs), outs, (d_stack, result) = refs[:8], refs[8:10], refs[10:18], refs[18:]
+    blocks, (stack, probs), outs, (d_stack, result) = refs[:4], refs[4:6], refs[6:14], refs[14:]
     micros, total = stack.shape[0], stack.shape[1]
     count = outs[0].shape[0]
     per = count // micros
@@ -646,7 +649,7 @@
     for m in range(micros):
         rows = slice(m * per, (m + 1) * per)
         for k in range(8):
-            d_stack[pl.ds(aligned((ids[0] ^ k) * per, per), per), :] = blocks[k][rows]
+            d_stack[pl.ds(aligned((ids[0] ^ k) * per, per), per), :] = blocks[k & 3][k >> 2, rows]
         q, k, v = stack[m, :, :128], stack[m, :, 128:256], stack[m, :, 256:384]
         d_out = d_stack[...]
         d_q = jnp.zeros((total, 128), F32)
@@ -677,7 +680,7 @@
     for k, block in enumerate((d0, d1, d2, d3, d4, d5, d6, d7)):
         rows = pl.ds(row_slot(f, (c ^ k) & 3, count), count)
         d_qkv[rows, (k >> 2) * 384 : (k >> 2) * 384 + 384] = block[...]
-    for peer, a in zip(share_rows(c, f), (a0, a1, a2, a3)):
+    for peer, a in zip(share_rows(c, f, 0), (a0, a1, a2, a3)):
         full[:, pl.ds(aligned(peer * part, part), part)] = mm_t(d_qkv[:, :384], a[...])
     for k, b in enumerate((b0, b1, b2, b3)):
         columns = pl.ds(aligned((f ^ k) * part, part), part)
@@ -752,8 +755,8 @@
     rows, part = out.shape[0], out.shape[1] // 4
     total = jnp.zeros((rows, 1), F32)
     for k, piece in enumerate((p0, p1, p2, p3)):
-        out[:, pl.ds(aligned((ids[1] ^ k) * part, part), part)] = piece[:, :part]
-        total = total + piece[:, part : part + 1]
+        out[:, pl.ds(aligned((ids[1] ^ k) * part, part), part)] = piece[:, :part].astype(F32)
+        total = total + piece[:, part : part + 128].astype(F32)[:, :1]
     grad_gain[...] = as_row(total / owned(ids, gain, rows))
 
 
@@ -768,40 +771,35 @@
                 start = b * width + (ids[1] ^ k) * part + ((ids[0] >> 2) ^ half) * 128
                 out[:, pl.ds(aligned(start, 128), 128)] = piece[
                     :, (3 * half + b) * 128 : (3 * half + b + 1) * 128
-                ]
-        total = total + piece[:, 768:769]
-        router = router + piece[:, 896:897]
+                ].astype(F32)
+        total = total + piece[:, 768:896].astype(F32)[:, :1]
+        router = router + piece[:, 896:1024].astype(F32)[:, :1]
     grad_gain[...] = as_row(total / owned(ids, gain, rows))
     grad_router[...] = as_row(router)
 
 
-def join_down_kernel(a, b, out):
-    out[...] = a[...].astype(F32) + b[...].astype(F32)
-
-
-def add_halves(keep, received, send2, keep2):
-    half = keep.shape[0] // 2
-    keep2[...] = keep[:half] + received[:half].astype(F32)
-    send2[...] = (keep[half:] + received[half:].astype(F32)).astype(BF16)
-
-
-def halves_kernel(*refs):
-    count = len(refs) // 4
-    for i in range(count):
-        add_halves(*refs[2 * i : 2 * i + 2], *refs[2 * count + 2 * i : 2 * count + 2 * i + 2])
-
-
-def hop2_kernel(keep_u, got_u, keep_d, got_d, send, keep, down0, down1):
-    add_halves(keep_u, got_u, send, keep)
-    down0[...] = (keep_d[0] + got_d[0].astype(F32)).astype(BF16)
-    down1[...] = (keep_d[1] + got_d[1].astype(F32)).astype(BF16)
-
-
-def last_kernel(keep_u, got_u, send, mine):
-    total = keep_u[0] + got_u[0].astype(F32)
-    half = total.shape[0] // 2
-    mine[...] = total[:half]
-    send[...] = total[half:].astype(BF16)
+def join_down_kernel(block, out):
+    out[...] = block[...].astype(F32)
+
+
+def hop2_kernel(keep_u, got_u, keep_d, got_d, send, own_u, own_d):
+    for i in range(2):
+        total = keep_u[i] + got_u[i].astype(F32)
+        half, width = total.shape[0] // 2, total.shape[1]
+        if i:
+            send[0, :, :width] = total[:half].astype(BF16)
+            send[0, :, width:] = total[half:].astype(BF16)
+        else:
+            own_u[...] = total
+    own_d[...] = keep_d[0] + got_d[0].astype(F32)
+    send[1] = (keep_d[1] + got_d[1].astype(F32)).astype(BF16)
+
+
+def hop3_kernel(own_u, own_d, got, send, mine, down):
+    half, width = own_u.shape[0] // 2, own_u.shape[1]
+    mine[...] = own_u[:half] + got[0, :, :width].astype(F32)
+    send[...] = (own_u[half:] + got[0, :, width:].astype(F32)).astype(BF16)
+    down[...] = (own_d[...] + got[1].astype(F32)).astype(BF16)
 
 
 def up_pieces_kernel(ids, mine, other, w_rows, c0, c1, c2, c3):
@@ -813,44 +811,37 @@
         total = jnp.zeros((rows, 1), F32)
         for side, value in ((y, mine[own]), (1 - y, other[own].astype(F32))):
             columns = pl.ds(aligned(side * half, 128), half)
-            piece[:, columns] = value
+            piece[:, columns] = value.astype(BF16)
             total = total + jnp.sum(
                 value * w_rows[weights, columns].astype(F32), axis=1, keepdims=True
             )
-        piece[:, 2 * half :] = jnp.broadcast_to(total, (rows, 128))
+        piece[:, 2 * half :] = jnp.broadcast_to(total, (rows, 128)).astype(BF16)
 
 
 def pieces_kernel(ids, mine, got, w_rows, c0, c1, c2, c3, out):
     rows = c0.shape[0]
-    router = mine[0, 128:129, :128] + got[0, 128:136, :128].astype(F32)[0:1]
+    router = mine[0, 128:129, 384:512] + got[0, 128:136, 384:512].astype(F32)[0:1]
     for k, piece in enumerate((c0, c1, c2, c3)):
         own = slice(k * rows, (k + 1) * rows)
         first = (ids[1] ^ k) * rows
         weights = pl.ds(aligned(first, rows), rows)
         a, b = mine[0, own, :384], got[0, own, :384].astype(F32)
-        piece[:, :384] = a
-        piece[:, 384:768] = b
+        piece[:, :384] = a.astype(BF16)
+        piece[:, 384:768] = b.astype(BF16)
         total = jnp.sum(a * w_rows[weights, :384].astype(F32), axis=1, keepdims=True)
         total = total + jnp.sum(b * w_rows[weights, 384:].astype(F32), axis=1, keepdims=True)
-        piece[:, 768:896] = jnp.broadcast_to(total, (rows, 128))
+        piece[:, 768:896] = jnp.broadcast_to(total, (rows, 128)).astype(BF16)
         hit = iota((rows, 128), 1) == iota((rows, 128), 0) + first
         share = jnp.sum(jnp.where(hit, router, 0.0), axis=1, keepdims=True)
-        piece[:, 896:] = jnp.broadcast_to(share, (rows, 128))
+        piece[:, 896:] = jnp.broadcast_to(share, (rows, 128)).astype(BF16)
         out[:, k * 256 : (k + 1) * 256] = mine[0, own, 384:640] + got[0, own, 384:640].astype(F32)
 
 
-def halves(call, name, *pairs):
-    outs = []
-    for keep, _ in pairs:
-        shape = (keep.shape[0] // 2, *keep.shape[1:])
-        outs += [local(shape, BF16), local(shape, F32)]
-    flat = call(halves_kernel, outs, (), [x for pair in pairs for x in pair], name=name)
-    return [(flat[2 * i + 1], flat[2 * i]) for i in range(len(pairs))]
-
-
-def all_rows_sum(call, send, keep):
+def all_rows_sum(call, send, keep, after=()):
     received = exchange(send, "fsdp", 4, 1)
-    (low,) = call(add_both_kernel, (local(keep.shape, BF16),), (), (keep, received), name="add_both")
+    (low,) = call(
+        add_both_kernel, (local(keep.shape, BF16),), (), (keep, received), name="add_both", after=after
+    )
     return low, exchange(low, "fsdp", 4, 2)
 
 
@@ -868,13 +859,24 @@
     return (blocks[0], *(got[k] for k in range(1, 8)))
 
 
-def swap_across(parts):
-    mine, beside, across = parts
-    across = lax.ppermute(
+def swap_across(across, bit):
+    return lax.ppermute(
         across, ("ctx", "fsdp"),
-        [(4 * a + b, 4 * a + (b ^ (2 + (a & 1)))) for a in range(8) for b in range(4)],
-    )
-    return mine, exchange(beside, "fsdp", 4, 1), across
+        [(4 * a + b, 4 * a + (b ^ (2 + ((a >> bit) & 1)))) for a in range(8) for b in range(4)],
+    )
+
+
+def pair_kernel(own, far, *outs):
+    for k, out in enumerate(outs):
+        out[0] = own[k]
+        out[1] = far[k]
+
+
+def swap_in_two(call, own, far, *after):
+    came = exchange(far, "ctx", 8, 4)
+    shape = (2, *own.shape[1:])
+    pairs = call(pair_kernel, (local(shape, own.dtype),) * 4, (), (own, came), name="pair", after=after)
+    return (pairs[0], *(exchange(pairs[k], "ctx", 8, k) for k in (1, 2, 3)))
 
 
 def swap_pieces(pieces):
@@ -912,40 +914,45 @@
     )
     turn = [(4 * a + b, 4 * ((a & 4) | b) + (a & 3)) for a in range(8) for b in range(4)]
     turned = lax.ppermute(rowsx, ("ctx", "fsdp"), turn)
-    turned_far = lax.ppermute(rowsx, ("ctx", "fsdp"), [(a, b ^ 16) for a, b in turn])
-    w_mine, w_beside, w_across = swap_across(w_parts)
-    w_parts = (w_mine, w_beside, w_across, exchange(w_across, "ctx", 8, 1))
-    (seq,) = call(
-        pair_kernel, (local((2, count + 8, width), BF16),), (), (turned, turned_far), name="pair"
-    )
-    seq_x, seq_c = exchange(seq, "fsdp", 4, 2), exchange(seq, "fsdp", 4, 1)
-    seq_xc = exchange(seq_x, "fsdp", 4, 1)
+    turned_far = exchange(turned, "ctx", 8, 4)
+    w_mine, w_beside, w_across = w_parts
+    w_across = swap_across(w_across, 0)
+    up_mine, up_beside, up_across = call(
+        cut_up_kernel, (local((part, hidden), BF16),) * 3, (ids,), (), far=(w_up,),
+        scratch=[dma((3,))], name="cut_up", weight=0,
+    )
+    near_rows = lax.all_gather(turned, "fsdp", axis=0, tiled=True)
+    far_rows = lax.all_gather(turned_far, "fsdp", axis=0, tiled=True)
+    w_across = call.hold(w_across, near_rows)
+    w_parts = (w_mine, exchange(w_beside, "fsdp", 4, 1), w_across, exchange(w_across, "ctx", 8, 1))
+    up_beside, up_across = exchange(up_beside, "fsdp", 4, 1), swap_across(up_across, 0)
+    far_heads, heads, stack, probs, norm1 = call(
+        attend_kernel,
+        (
+            *(local((4, count, 128), BF16),) * 2, local((micros, total, 384), BF16),
+            local((2 * micros, total, total), F32), local((8 * count, width), BF16),
+        ),
+        (ids,), (near_rows, far_rows, gain_attn, *w_parts),
+        scratch=[pltpu.VMEM((micros, total, 128), F32), pltpu.VMEM((micros, total, 128), BF16)],
+        name="attend",
+    )
     (both,) = call(
-        cot_kernel, (local((2 * count + 8, width), BF16),), (ids,), (routed, cot, rowsx), name="cot_rows"
+        cot_kernel, (local((2 * count + 8, width), BF16),), (ids,), (routed, cot, rowsx), name="cot_rows",
+        weight=0,
     )
     both_x, both_c = exchange(both, "fsdp", 4, 2), exchange(both, "fsdp", 4, 1)
     both_xc = exchange(both_x, "fsdp", 4, 1)
-    up_mine, up_beside, up_across, *rest = call(
-        cut_kernel, (local((part, hidden), BF16),) * 3 + (local((part, 384), BF16),) * 4, (ids,), (),
-        far=(w_up, w_qkv), scratch=[dma((15,))], name="cut_shares",
-    )
-    _, up_beside, up_across = swap_across((up_mine, up_beside, up_across))
-    *heads, stack, probs, norm1 = call(
-        attend_kernel,
-        (
-            *(local((count, 128), BF16),) * 8, local((micros, total, 384), BF16),
-            local((2 * micros, total, total), F32), local((8 * count, width), BF16),
-        ),
-        (ids,), (seq, seq_x, seq_c, seq_xc, gain_attn, *w_parts),
-        scratch=[pltpu.VMEM((micros, total, 128), F32), pltpu.VMEM((micros, total, 128), BF16)],
-        name="attend",
-    )
-    heads = swap_blocks(heads)
+    rest = call(
+        cut_rest_kernel, (local((part, 384), BF16),) * 4, (ids,), (), far=(w_qkv,),
+        scratch=[dma((12,))], name="cut_rest", weight=0,
+    )
+    heads = swap_in_two(call, heads, far_heads)
     attended, send, keep, attn_part = call(
         out_kernel, (all_quarter, pair_bf, pair_f, local((4 * count, width), F32)),
-        (ids,), (*heads, w_out), name="attn_out", after=(up_across, both_x),
+        (ids,), (*heads, w_out), name="attn_out", after=(up_across,),
     )
     up_parts = (up_mine, up_beside, up_across, exchange(up_across, "ctx", 8, 1))
+    rest = swap_pieces(rest)
     low, received = all_rows_sum(call, send, keep)
     d_mlp, gate = call(
         d_mlp_kernel, (all_bf, local((4, count, 1), F32)), (),
@@ -954,7 +961,7 @@
     d_mlp_a = exchange(d_mlp[: 2 * count], "ctx", 8, 2)
     d_mlp_b = exchange(d_mlp_a, "fsdp", 4, 1)
     attn, norm2 = call(
-        mid_kernel, (pair_f, pair_bf), (), (low, received, both, both_x, gain_mlp), name="mid"
+        mid_kernel, (pair_f, pair_bf), (), (low, received, both, both_x, gain_mlp), name="mid",
     )
     norm2_a = exchange(norm2, "ctx", 8, 1)
     norm2_b = exchange(norm2_a, "fsdp", 4, 1)
@@ -966,18 +973,17 @@
         name="mlp",
     )
     d_near, act_near = exchange(d_send, "ctx", 8, 1), exchange(act_send, "ctx", 8, 2)
-    low, received = all_rows_sum(call, send, keep)
+    low, received = all_rows_sum(call, send, keep, (norm2_a, d_mlp_a))
     d_mid, d_attn = call(
         d_attn_kernel, (rows_f, pair_bf), (),
         (low, received, attn, both, both_x, gate, gain_mlp), name="d_attn",
         after=(d_near, act_near),
     )
-    *d_heads, d_attn = call(
-        d_attended_kernel, (*(local((count, 128), BF16),) * 8, all_bf), (ids,),
+    far_heads, d_heads, d_attn = call(
+        d_attended_kernel, (*(local((4, count, 128), BF16),) * 2, all_bf), (ids,),
         (d_attn, exchange(d_attn, "fsdp", 4, 1), w_out),
         scratch=[pltpu.VMEM((4 * count, part), F32)], name="d_attended",
     )
-    d_heads = swap_blocks(d_heads)
     send_u, keep_u = call(
         grad_up_kernel, (local((2, 256, hidden // 2), BF16), local((2, 256, hidden // 2), F32)), (ids,),
         (norm2, norm2_a, norm2_b, d_keep, d_near), name="grad_up", weight=0,
@@ -988,77 +994,78 @@
         (d_mlp, d_mlp_a, d_mlp_b, act_keep, act_near), name="grad_down", weight=0,
         scratch=[pltpu.VMEM((8 * count, width), BF16), pltpu.VMEM((8 * count, hidden // 2), BF16)],
     )
+    got_u, got_d = exchange(send_u, "ctx", 8, 2), exchange(send_d, "ctx", 8, 1)
+    d_heads = swap_in_two(call, d_heads, far_heads)
+    d_blocks = call(
+        attend_back_kernel, (local((count, 384), BF16),) * 8, (ids,), (*d_heads, stack, probs),
+        scratch=[pltpu.VMEM((total, 128), BF16), pltpu.VMEM((micros, total, 384), BF16)],
+        name="attend_back", after=(*rest[1:], got_u, got_d),
+    )
+    d_own = swap_blocks(d_blocks)
+    send_z, own_u, own_d = call(
+        hop2_kernel,
+        (local((2, 128, width), BF16), local((256, hidden // 2), F32), local((128, width), F32)),
+        (), (keep_u, got_u, keep_d, got_d), name="hop2", weight=0,
+    )
+    got_z = exchange(send_z, "ctx", 8, 4)
+    owners = [(4 * a + b, 4 * (2 * b + a // 4) + a % 4) for a in range(8) for b in range(4)]
     send_m, keep_m, router = call(
         mlp_out_kernel, (pair_bf, pair_f, vector), (),
         (act, w_down, attn_part, gate, both, both_x, both_c, both_xc), name="mlp_out", weight=0,
         scratch=[pltpu.VMEM((4 * count, width), F32)],
     )
-    got_u, got_d = exchange(send_u, "ctx", 8, 2), exchange(send_d, "ctx", 8, 1)
-    rest = swap_pieces(rest)
-    w_up_rows, w_qkv_rows = call(
-        pick_kernel, (local((128, hidden), BF16), local((128, 768), BF16)), (ids,),
-        (*up_parts, *w_parts, *rest), name="pick", weight=0,
-    )
-    d_blocks = call(
-        attend_back_kernel, (local((count, 384), BF16),) * 8, (ids,), (*d_heads, stack, probs),
-        scratch=[pltpu.VMEM((total, 128), BF16), pltpu.VMEM((micros, total, 384), BF16)],
-        name="attend_back",
-    )
-    d_own = swap_blocks(d_blocks)
-    send_q, keep_q = call(
-        grad_attn_kernel, (local((4, 136, 640), BF16), local((4, 136, 640), F32)), (ids,),
+    part_bf = local((2, 136, 640), BF16)
+    keep_q, *send_q = call(
+        grad_attn_kernel, (local((2, 136, 640), F32), part_bf, part_bf, part_bf), (ids,),
         (norm1, *d_blocks, attended, d_attn, router), name="grad_attn", weight=0,
         scratch=[pltpu.VMEM((8 * count, 384), BF16), pltpu.VMEM((part, width), F32)],
     )
-    got_q = exchange(send_q, "ctx", 8, UP_ORDER[0])
-    keep_m, received_m = own_rows_sum(call, send_m, keep_m)
-    send_u, keep_u, down0, down1 = call(
-        hop2_kernel,
-        (local((1, 256, hidden // 2), BF16), local((1, 256, hidden // 2), F32))
-        + (local((128, width), BF16),) * 2,
-        (), (keep_u, got_u, keep_d, got_d), name="hop2", weight=0,
-    )
-    got_u = exchange(send_u, "ctx", 8, 4)
-    owners = [(4 * a + b, 4 * (2 * b + a // 4) + a % 4) for a in range(8) for b in range(4)]
-    far_owners = [(a ^ 16, b) for a, b in owners]
-    down0 = lax.ppermute(down0, ("ctx", "fsdp"), owners)
-    down1 = lax.ppermute(down1, ("ctx", "fsdp"), far_owners)
-    d_logit, output = call(
-        output_kernel, (local((count, 1), F32), sds(tok.shape, BF16)), (ids,),
-        (routed, keep_m, received_m, attn, both, gate, tok), name="output", weight=0,
-    )
+    got_q = [exchange(x, "ctx", 8, k + 1) for k, x in enumerate(send_q)]
     send, keep = call(
         d_norm1_kernel, (pair_bf, pair_f), (ids,),
         (*d_own, *w_parts, *rest), name="d_norm1",
         scratch=[pltpu.VMEM((4 * count, 768), BF16), pltpu.VMEM((4 * count, width), F32)],
     )
     keep, received = own_rows_sum(call, send, keep)
-    ((keep_q, send_q),) = halves(call, "hop1_attn", (keep_q, got_q))
-    got_q = exchange(send_q, "ctx", 8, UP_ORDER[1])
+    keep_m, received_m = own_rows_sum(call, send_m, keep_m)
+    send_u, mine_u, down = call(
+        hop3_kernel,
+        (local((128, hidden // 2), BF16), local((128, hidden // 2), F32), local((128, width), BF16)),
+        (), (own_u, own_d, got_z), name="hop3", weight=0,
+    )
+    down = lax.ppermute(down, ("ctx", "fsdp"), owners)
+    other_u = exchange(send_u, "ctx", 8, 1)
+    send_q, keep_q = call(
+        sum_attn_kernel, (local((1, 136, 640), BF16), local((1, 136, 640), F32)), (),
+        (keep_q, *got_q), name="sum_attn", weight=0,
+    )
+    got_q = exchange(send_q, "ctx", 8, 4)
+    d_logit, output = call(
+        output_kernel, (local((count, 1), F32), sds(tok.shape, BF16)), (ids,),
+        (routed, keep_m, received_m, attn, both, gate, tok), name="output", weight=0,
+    )
     (input_grad,) = call(
         input_grad_kernel, (sds(cot.shape, BF16),), (ids,),
         (routed, keep, received, d_mid, both, d_logit, w_router, gain_attn, cot), name="input_grad",
-    )
-    send_u, mine_u = call(
-        last_kernel, (local((128, hidden // 2), BF16), local((128, hidden // 2), F32)),
-        (), (keep_u, got_u), name="hop3",
-    )
-    other_u = exchange(send_u, "ctx", 8, 1)
-    ((keep_q, send_q),) = halves(call, "hop2_attn", (keep_q, got_q))
-    got_q = exchange(send_q, "ctx", 8, 4)
+        weight=0,
+    )
+    w_up_rows, w_qkv_rows = call(
+        pick_kernel, (local((128, hidden), BF16), local((128, 768), BF16)), (ids,),
+        (*up_parts, *w_parts, *rest), name="pick", weight=0,
+    )
     chunks = call(
-        up_pieces_kernel, (local((32, hidden + 128), F32),) * 4, (ids,), (mine_u, other_u, w_up_rows),
+        up_pieces_kernel, (local((32, hidden + 128), BF16),) * 4, (ids,), (mine_u, other_u, w_up_rows),
         name="up_pieces",
     )
     chunks = swap_pieces(chunks)
     *qkv_chunks, grad_out = call(
-        pieces_kernel, (local((32, 1024), F32),) * 4 + (local((32, width), F32),), (ids,),
+        pieces_kernel, (local((32, 1024), BF16),) * 4 + (local((32, width), F32),), (ids,),
         (keep_q, got_q, w_qkv_rows), name="qkv_pieces",
     )
     qkv_chunks = swap_pieces(qkv_chunks)
     grad_out = lax.ppermute(grad_out, ("ctx", "fsdp"), owners)
     (grad_down,) = call(
-        join_down_kernel, (sds((128, width), F32),), (), (down0, down1), name="join_down"
+        join_down_kernel, (sds((128, width), F32),), (), (down,), name="join_down"
     )
     row = sds((1, 32), F32)
     grad_up, grad_gain_mlp = call(

time: 231 us -> 211 us (0.913)
  blocking collectives: 0 us -> 21.6 us
  starting transfers between devices: 83.2 us -> 62.4 us
  waiting for transfers between devices: 103 us -> 82.2 us
    all_gather x0 -> x2, blocking collectives: none -> 21.6 us  [the longest x1 12.7 us: shards_8x4(): near_rows = lax.all_gather(turned, 'fsdp', axis=0, tiled=True)]
    ppermute x63 -> x56, starting transfers between devices: 67.7 us -> 52.3 us  [exchange(): return lax.ppermute(x, axis, [(i, i ^ mask) for i in range(size)])]
    ppermute x5 -> x3, waiting for transfers between devices: 15.5 us -> 2.5 us  [the longest x2 2.5 us: swap_across(): lax.ppermute(across, ('ctx', 'fsdp'), [(4 * a + b, 4 * a + (b ^ 2 + (a >>...]
    ppermute x63 -> x56, waiting for transfers between devices: 81.2 us -> 75.7 us  [exchange(): return lax.ppermute(x, axis, [(i, i ^ mask) for i in range(size)])]
    ppermute x5 -> x3, starting transfers between devices: 10.5 us -> 5.17 us  [the longest x2 3.26 us: swap_across(): lax.ppermute(across, ('ctx', 'fsdp'), [(4 * a + b, 4 * a + (b ^ 2 + (a >>...]
    ppermute x1, waiting for transfers between devices: 6 us -> 3.26 us  [shards_8x4(): grad_out = lax.ppermute(grad_out, ('ctx', 'fsdp'), owners)]
    pallas_call x33 -> x35, Pallas kernels: 39.1 us -> 40.3 us  [__call__(): pl.pallas_call(body, out_shape=tuple(outs), in_specs=[pl.BlockSpec(memory...]
  transfers between devices with their start and end apart: 70 -> 61, of which waited for: 22 -> 19; matrix products, arithmetic and copies ran while one was open for 0% -> 0% of each run, Pallas kernels for 12% -> 14%
where the time goes in v3:
time: 211 us; the launch traced here: 210 us
  waiting for transfers between devices  82.2 us (39%)
  starting transfers between devices  62.4 us (30%)
  Pallas kernels  40.3 us (19%)
  blocking collectives  21.6 us (10%)
    ppermute x56, waiting for transfers between devices, exchange(): return lax.ppermute(x, axis, [(i, i ^ mask) for i in range(size)])  75.7 us
    ppermute x56, starting transfers between devices, exchange(): return lax.ppermute(x, axis, [(i, i ^ mask) for i in range(size)])  52.3 us
    pallas_call x35, Pallas kernels, __call__(): pl.pallas_call(body, out_shape=tuple(outs), in_specs=[pl.BlockSpec(memory...  40.3 us
    all_gather x1, blocking collectives, shards_8x4(): near_rows = lax.all_gather(turned, 'fsdp', axis=0, tiled=True)  12.7 us
    all_gather x1, blocking collectives, shards_8x4(): far_rows = lax.all_gather(turned_far, 'fsdp', axis=0, tiled=True)  8.84 us
  transfers between devices with their start and end apart: 61, of which 19 were waited for; matrix products, arithmetic and copies ran while one was open for 0% of the time, Pallas kernels for 14%

profile of v3, /device:TPU:4, one launch (start us, length us, event | category | flops | bytes accessed | tf_op | source)
XLA Modules:
  0.0 209.7 jit_solution(910600748778311652)
XLA Ops:
  2.1 2.5 %front.1 = (bf16[104,1024]{1,0:T(8,128)(2,1)S(1)}, bf16[256,384]{1,0:T(8,128)(2,1)S(1)}, bf16[256,384]{1,0:T(8,128)(2,1)S(1)}, bf16[256,384]{1,0:T(8,128)(2,1)S(1)}) custom-call(s32[2]{0:T(128)S(1)} %pad_add_fusion.refs_0_, s32[16]{0:T(128)S(1)} %copy-done.9, bf16[3,256,1024]{2,1,0:T(8,128)(2,1)} %bitcast.21, bf16[256,3072]{1,0:T(8,128)(2,1)} %refs_1_.6, ...), custom_call_target="tpu_custom_call" | custom-call | flops 10000000000 | bytes 1000000 | tf_op jit(solution)/shard_map/front/pallas_call | solution.py:221
  11.7 2.6 %collective-permute-start.1 = (bf16[104,1024]{1,0:T(8,128)(2,1)S(1)}, bf16[104,1024]{1,0:T(8,128)(2,1)S(1)}, u32[]{:S(2)}, u32[]{:S(2)}) collective-permute-start(bf16[104,1024]{1,0:T(8,128)(2,1)S(1)} %collective-permute-done), channel_id=1, source_target_pairs={{0,16},{4,20},{8,24},{12,28},{16,0},{20,4},{24,8},{28,12},{1,17},{... | collective-permute-start | bytes 638984 | tf_op jit(solution)/shard_map/ppermute | solution.py:261
  14.3 12.7 %all_gather.6.refs_2_.refs_1_ = bf16[416,1024]{1,0:T(8,128)(2,1)S(1)} all-gather(bf16[104,1024]{1,0:T(8,128)(2,1)S(1)} %collective-permute-done), channel_id=1, replica_groups=mesh['ctx'=8,'fsdp'=4] {'fsdp'}, dimensions={0}, use_global_device_ids=true | all-gather | bytes 1064960 | tf_op jit(solution)/shard_map/all_gather | solution.py:924
  27.4 8.8 %all_gather.7.refs_2_ = bf16[416,1024]{1,0:T(8,128)(2,1)S(1)} all-gather(bf16[104,1024]{1,0:T(8,128)(2,1)S(1)} %collective-permute-done.1), channel_id=1, replica_groups=mesh['ctx'=8,'fsdp'=4] {'fsdp'}, dimensions={0}, use_global_device_ids=true | all-gather | bytes 1064960 | tf_op jit(solution)/shard_map/all_gather | solution.py:925
  36.2 3.3 %attend.1 = (bf16[4,96,128]{2,1,0:T(8,128)(2,1)S(1)}, bf16[4,96,128]{2,1,0:T(8,128)(2,1)S(1)}, bf16[3,256,384]{2,1,0:T(8,128)(2,1)S(1)}, f32[6,256,256]{2,1,0:T(8,128)S(1)}, bf16[768,1024]{1,0:T(8,128)(2,1)S(1)}) custom-call(s32[2]{0:T(128)S(1)} %pad_add_fusion.refs_0_, bf16[416,1024]{1,0:T(8,128)(2,1)S(1)} %all_gather.6.refs_2_.refs_1_, ...), custom_call_target="tpu_custom_call" | custom-call | flops 10000000000 | bytes 1000000 | tf_op jit(solution)/shard_map/attend/pallas_call | solution.py:221
  44.4 3.2 %collective-permute-done.5.refs_1_ = bf16[4,96,128]{2,1,0:T(8,128)(2,1)S(1)} collective-permute-done((bf16[4,96,128]{2,1,0:T(8,128)(2,1)S(1)}, bf16[4,96,128]{2,1,0:T(8,128)(2,1)S(1)}, u32[]{:S(2)}, u32[]{:S(2)}) %collective-permute-start.5) | collective-permute-done | bytes 98336 | tf_op jit(solution)/shard_map/ppermute | solution.py:261
  52.1 2.5 %collective-permute-done.9.refs_7_.refs_6_.refs_3_ = bf16[256,1024]{1,0:T(8,128)(2,1)S(1)} collective-permute-done((bf16[256,1024]{1,0:T(8,128)(2,1)S(1)}, bf16[256,1024]{1,0:T(8,128)(2,1)S(1)}, u32[]{:S(2)}, u32[]{:S(2)}) %collective-permute-start.9) | collective-permute-done | bytes 524320 | tf_op jit(solution)/shard_map/ppermute | solution.py:863
  56.2 7.5 %collective-permute-done.12.refs_1_.refs_3_.refs_4_.refs_5_ = bf16[200,1024]{1,0:T(8,128)(2,1)S(1)} collective-permute-done((bf16[200,1024]{1,0:T(8,128)(2,1)S(1)}, bf16[200,1024]{1,0:T(8,128)(2,1)S(1)}, u32[]{:S(2)}, u32[]{:S(2)}) %collective-permute-start.12) | collective-permute-done | bytes 409632 | tf_op jit(solution)/shard_map/ppermute | solution.py:261
  65.8 9.6 %collective-permute-done.11.refs_1_ = bf16[2,96,1024]{2,1,0:T(8,128)(2,1)S(1)} collective-permute-done((bf16[2,96,1024]{2,1,0:T(8,128)(2,1)S(1)}, bf16[2,96,1024]{2,1,0:T(8,128)(2,1)S(1)}, u32[]{:S(2)}, u32[]{:S(2)}) %collective-permute-start.11) | collective-permute-done | bytes 393248 | tf_op jit(solution)/shard_map/ppermute | solution.py:261
  79.5 4.1 %mlp.1 = (bf16[2,96,1024]{2,1,0:T(8,128)(2,1)S(1)}, f32[2,96,1024]{2,1,0:T(8,128)S(1)}, bf16[384,512]{1,0:T(8,128)(2,1)S(1)}, bf16[384,512]{1,0:T(8,128)(2,1)S(1...) custom-call(s32[2]{0:T(128)S(1)} %pad_add_fusion.refs_0_, ...), custom_call_target="tpu_custom_call" | custom-call | flops 10000000000 | bytes 1000000 | tf_op jit(solution)/shard_map/mlp/pallas_call | solution.py:221
  85.3 2.5 %collective-permute-done.22.refs_4_.refs_2_ = bf16[192,1024]{1,0:T(8,128)(2,1)S(1)} collective-permute-done((bf16[192,1024]{1,0:T(8,128)(2,1)S(1)}, bf16[192,1024]{1,0:T(8,128)(2,1)S(1)}, u32[]{:S(2)}, u32[]{:S(2)}) %collective-permute-start.22) | collective-permute-done | bytes 393248 | tf_op jit(solution)/shard_map/ppermute | solution.py:261
  90.0 6.9 %collective-permute-done.20.refs_8_.refs_5_ = bf16[384,512]{1,0:T(8,128)(2,1)S(1)} collective-permute-done((bf16[384,512]{1,0:T(8,128)(2,1)S(1)}, bf16[384,512]{1,0:T(8,128)(2,1)S(1)}, u32[]{:S(2)}, u32[]{:S(2)}) %collective-permute-start.20) | collective-permute-done | bytes 393248 | tf_op jit(solution)/shard_map/ppermute | solution.py:261
  116.9 9.3 %collective-permute-done.30.refs_2_ = bf16[2,96,128]{2,1,0:T(8,128)(2,1)S(1)} collective-permute-done((bf16[2,96,128]{2,1,0:T(8,128)(2,1)S(1)}, bf16[2,96,128]{2,1,0:T(8,128)(2,1)S(1)}, u32[]{:S(2)}, u32[]{:S(2)}) %collective-permute-start.30) | collective-permute-done | bytes 49184 | tf_op jit(solution)/shard_map/ppermute | solution.py:261
  126.2 3.0 %attend_back.1 = (bf16[96,384]{1,0:T(8,128)(2,1)S(1)}, bf16[96,384]{1,0:T(8,128)(2,1)S(1)}, bf16[96,384]{1,0:T(8,128)(2,1)S(1)}, bf16[96,384]{1,0:T(8,128)(2,1)S...) custom-call(s32[2]{0:T(128)S(1)} %pad_add_fusion.refs_0_, ...), custom_call_target="tpu_custom_call" | custom-call | flops 10000000000 | bytes 1000000 | tf_op jit(solution)/shard_map/attend_back/pallas_call | solution.py:221
  133.8 2.7 %collective-permute-start.41 = (bf16[96,384]{1,0:T(8,128)(2,1)S(1)}, bf16[96,384]{1,0:T(8,128)(2,1)S(1)}, u32[]{:S(2)}, u32[]{:S(2)}) collective-permute-start(bf16[96,384]{1,0:T(8,128)(2,1)S(1)} %get-tuple-element.160.refs_7_), channel_id=1, source_target_pairs={{0,20},{4,16},{8,28},{12,24},{16,4},{20,0},{24,12},{28,8},{1,21},{... | collective-permute-start | bytes 221192 | tf_op jit(solution)/shard_map/ppermute | solution.py:261
  148.7 2.8 %collective-permute-start.49 = (bf16[2,128,1024]{2,1,0:T(8,128)(2,1)S(1)}, bf16[2,128,1024]{2,1,0:T(8,128)(2,1)S(1)}, u32[]{:S(2)}, u32[]{:S(2)}) collective-permute-start(bf16[2,128,1024]{2,1,0:T(8,128)(2,1)S(1)} %get-tuple-element.153.refs_8_), channel_id=1, source_target_pairs={{0,16},{4,20},{8,24},{12,28},{16,0},{20,4},{24,8},{28,12},{1,17},{... | collective-permute-start | bytes 1572872 | tf_op jit(solution)/shard_map/ppermute | solution.py:261
  152.3 2.7 %collective-permute-start.48 = (bf16[2,136,640]{2,1,0:T(8,128)(2,1)S(1)}, bf16[2,136,640]{2,1,0:T(8,128)(2,1)S(1)}, u32[]{:S(2)}, u32[]{:S(2)}) collective-permute-start(bf16[2,136,640]{2,1,0:T(8,128)(2,1)S(1)} %get-tuple-element.174), channel_id=1, source_target_pairs={{0,12},{4,8},{8,4},{12,0},{16,28},{20,24},{24,20},{28,16},{1,13},{... | collective-permute-start | bytes 1044488 | tf_op jit(solution)/shard_map/ppermute | solution.py:261
  156.0 19.0 %collective-permute-done.49.refs_2_ = bf16[2,128,1024]{2,1,0:T(8,128)(2,1)S(1)} collective-permute-done((bf16[2,128,1024]{2,1,0:T(8,128)(2,1)S(1)}, bf16[2,128,1024]{2,1,0:T(8,128)(2,1)S(1)}, u32[]{:S(2)}, u32[]{:S(2)}) %collective-permute-start.49) | collective-permute-done | bytes 524320 | tf_op jit(solution)/shard_map/ppermute | solution.py:261
  177.3 2.5 %collective-permute-done.48.refs_3_ = bf16[2,136,640]{2,1,0:T(8,128)(2,1)S(1)} collective-permute-done((bf16[2,136,640]{2,1,0:T(8,128)(2,1)S(1)}, bf16[2,136,640]{2,1,0:T(8,128)(2,1)S(1)}, u32[]{:S(2)}, u32[]{:S(2)}) %collective-permute-start.48) | collective-permute-done | bytes 348192 | tf_op jit(solution)/shard_map/ppermute | solution.py:261
  187.0 2.8 %collective-permute-start.58 = (bf16[32,1152]{1,0:T(8,128)(2,1)S(1)}, bf16[32,1152]{1,0:T(8,128)(2,1)S(1)}, u32[]{:S(2)}, u32[]{:S(2)}) collective-permute-start(bf16[32,1152]{1,0:T(8,128)(2,1)S(1)} %get-tuple-element.196), channel_id=1, source_target_pairs={{0,2},{1,3},{2,0},{3,1},{4,6},{5,7},{6,4},{7,5},{8,10},{9,11},{10,... | collective-permute-start | bytes 221192 | tf_op jit(solution)/shard_map/ppermute | solution.py:261
  189.8 2.4 %input_grad.1 = bf16[3,256,1024]{2,1,0:T(8,128)(2,1)} custom-call(s32[2]{0:T(128)S(1)} %pad_add_fusion.refs_0_, s32[3,32]{1,0:T(4,128)S(1)} %bitcast.26, f32[96,1024]{1,0:T(8,128)S(1)} %get-tuple-element.180.refs_2_, bf16[96,1024]{1,0:T(8,128)(2,1)S(1)} %collective-permute-done.50.refs_3_, f32[96,1024]{1,0:T(8,128)S(1)} %get-tuple-element.135.refs_4_, ...), custom_call_target="tpu_custom_call" | custom-call | tf_op jit(solution)/shard_map/input_grad/pallas_call | solution.py:221
  192.2 4.1 %collective-permute-done.51.refs_2_ = bf16[1,136,640]{2,1,0:T(8,128)(2,1)S(1)} collective-permute-done((bf16[1,136,640]{2,1,0:T(8,128)(2,1)S(1)}, bf16[1,136,640]{2,1,0:T(8,128)(2,1)S(1)}, u32[]{:S(2)}, u32[]{:S(2)}) %collective-permute-start.51) | collective-permute-done | bytes 174112 | tf_op jit(solution)/shard_map/ppermute | solution.py:261
  199.0 3.1 %collective-permute-start.56 = (f32[32,1024]{1,0:T(8,128)S(1)}, f32[32,1024]{1,0:T(8,128)S(1)}, u32[]{:S(2)}, u32[]{:S(2)}) collective-permute-start(f32[32,1024]{1,0:T(8,128)S(1)} %get-tuple-element.194), channel_id=1, source_target_pairs={{0,0},{1,8},{2,16},{3,24},{4,1},{5,9},{6,17},{7,25},{8,2},{9,10},{... | collective-permute-start | bytes 393224 | tf_op jit(solution)/shard_map/ppermute | solution.py:1066
  205.8 3.3 %collective-permute-done.56 = f32[32,1024]{1,0:T(8,128)S(1)} collective-permute-done((f32[32,1024]{1,0:T(8,128)S(1)}, f32[32,1024]{1,0:T(8,128)S(1)}, u32[]{:S(2)}, u32[]{:S(2)}) %collective-permute-start.56) | collective-permute-done | bytes 131104 | tf_op jit(solution)/shard_map/ppermute | solution.py:1066
  (159 shorter events, 84.7 us)
Async XLA Ops:
  6.5 20.6 %collective-permute-start.3 = (bf16[256,384]{1,0:T(8,128)(2,1)S(1)}, bf16[256,384]{1,0:T(8,128)(2,1)S(1)}, u32[]{:S(2)}, u32[]{:S(2)}) collective-permute-start(bf16[256,384]{1,0:T(8,128)(2,1)S(1)} %get-tuple-element.108), channel_id=1, source_target_pairs={{0,2},{1,3},{2,0},{3,1},{4,7},{5,6},{6,5},{7,4},{8,10},{9,11},{10,... | collective-permute-start | bytes 589832 | tf_op jit(solution)/shard_map/ppermute | solution.py:863
  8.7 27.5 %collective-permute-start.2 = (bf16[256,384]{1,0:T(8,128)(2,1)S(1)}, bf16[256,384]{1,0:T(8,128)(2,1)S(1)}, u32[]{:S(2)}, u32[]{:S(2)}) collective-permute-start(bf16[256,384]{1,0:T(8,128)(2,1)S(1)} %get-tuple-element.107), channel_id=1, source_target_pairs={{0,1},{1,0},{2,3},{3,2},{4,5},{5,4},{6,7},{7,6},{8,9},{9,8},{10,11... | collective-permute-start | bytes 589832 | tf_op jit(solution)/shard_map/ppermute | solution.py:261
  11.7 15.7 %collective-permute-start.1 = (bf16[104,1024]{1,0:T(8,128)(2,1)S(1)}, bf16[104,1024]{1,0:T(8,128)(2,1)S(1)}, u32[]{:S(2)}, u32[]{:S(2)}) collective-permute-start(bf16[104,1024]{1,0:T(8,128)(2,1)S(1)} %collective-permute-done), channel_id=1, source_target_pairs={{0,16},{4,20},{8,24},{12,28},{16,0},{20,4},{24,8},{28,12},{1,17},{... | collective-permute-start | bytes 638984 | tf_op jit(solution)/shard_map/ppermute | solution.py:261
  40.6 14.0 %collective-permute-start.9 = (bf16[256,1024]{1,0:T(8,128)(2,1)S(1)}, bf16[256,1024]{1,0:T(8,128)(2,1)S(1)}, u32[]{:S(2)}, u32[]{:S(2)}) collective-permute-start(bf16[256,1024]{1,0:T(8,128)(2,1)S(1)} %get-tuple-element.117), channel_id=1, source_target_pairs={{0,2},{1,3},{2,0},{3,1},{4,7},{5,6},{6,5},{7,4},{8,10},{9,11},{10,... | collective-permute-start | bytes 1572872 | tf_op jit(solution)/shard_map/ppermute | solution.py:863
  51.2 12.4 %collective-permute-start.12 = (bf16[200,1024]{1,0:T(8,128)(2,1)S(1)}, bf16[200,1024]{1,0:T(8,128)(2,1)S(1)}, u32[]{:S(2)}, u32[]{:S(2)}) collective-permute-start(bf16[200,1024]{1,0:T(8,128)(2,1)S(1)} %cot_rows.1.refs_2_.refs_0_.refs_3_.refs_4_.refs_5_), channel_id=1, source_target_pairs={{0,2},{1,3},{2,0},{3,1},{4,6},{5,7},{6,4},{7,5},{8,10},{9,11},{10,... | collective-permute-start | bytes 1228808 | tf_op jit(solution)/shard_map/ppermute | solution.py:261
  65.2 12.2 %collective-permute-start.16 = (bf16[256,1024]{1,0:T(8,128)(2,1)S(1)}, bf16[256,1024]{1,0:T(8,128)(2,1)S(1)}, u32[]{:S(2)}, u32[]{:S(2)}) collective-permute-start(bf16[256,1024]{1,0:T(8,128)(2,1)S(1)} %get-tuple-element.123), channel_id=1, source_target_pairs={{0,1},{1,0},{2,3},{3,2},{4,5},{5,4},{6,7},{7,6},{8,9},{9,8},{10,11... | collective-permute-start | bytes 1572872 | tf_op jit(solution)/shard_map/ppermute | solution.py:261
  65.4 14.1 %collective-permute-start.17 = (bf16[256,1024]{1,0:T(8,128)(2,1)S(1)}, bf16[256,1024]{1,0:T(8,128)(2,1)S(1)}, u32[]{:S(2)}, u32[]{:S(2)}) collective-permute-start(bf16[256,1024]{1,0:T(8,128)(2,1)S(1)} %collective-permute-done.9.refs_7_.refs_6_.refs_3_), channel_id=1, source_target_pairs={{0,4},{4,0},{8,12},{12,8},{16,20},{20,16},{24,28},{28,24},{1,5},{5... | collective-permute-start | bytes 1572872 | tf_op jit(solution)/shard_map/ppermute | solution.py:261
  75.8 12.0 %collective-permute-start.22 = (bf16[192,1024]{1,0:T(8,128)(2,1)S(1)}, bf16[192,1024]{1,0:T(8,128)(2,1)S(1)}, u32[]{:S(2)}, u32[]{:S(2)}) collective-permute-start(bf16[192,1024]{1,0:T(8,128)(2,1)S(1)} %slice.3), channel_id=1, source_target_pairs={{0,8},{4,12},{8,0},{12,4},{16,24},{20,28},{24,16},{28,20},{1,9},{5... | collective-permute-start | bytes 1179656 | tf_op jit(solution)/shard_map/ppermute | solution.py:261
  83.7 13.2 %collective-permute-start.20 = (bf16[384,512]{1,0:T(8,128)(2,1)S(1)}, bf16[384,512]{1,0:T(8,128)(2,1)S(1)}, u32[]{:S(2)}, u32[]{:S(2)}) collective-permute-start(bf16[384,512]{1,0:T(8,128)(2,1)S(1)} %get-tuple-element.130), channel_id=1, source_target_pairs={{0,4},{4,0},{8,12},{12,8},{16,20},{20,16},{24,28},{28,24},{1,5},{5... | collective-permute-start | bytes 1179656 | tf_op jit(solution)/shard_map/ppermute | solution.py:261
  84.0 12.9 %collective-permute-start.24 = (bf16[384,512]{1,0:T(8,128)(2,1)S(1)}, bf16[384,512]{1,0:T(8,128)(2,1)S(1)}, u32[]{:S(2)}, u32[]{:S(2)}) collective-permute-start(bf16[384,512]{1,0:T(8,128)(2,1)S(1)} %get-tuple-element.133), channel_id=1, source_target_pairs={{0,8},{4,12},{8,0},{12,4},{16,24},{20,28},{24,16},{28,20},{1,9},{5... | collective-permute-start | bytes 1179656 | tf_op jit(solution)/shard_map/ppermute | solution.py:261
  107.4 18.8 %collective-permute-start.26 = (bf16[2,256,512]{2,1,0:T(8,128)(2,1)S(1)}, bf16[2,256,512]{2,1,0:T(8,128)(2,1)S(1)}, u32[]{:S(2)}, u32[]{:S(2)}) collective-permute-start(bf16[2,256,512]{2,1,0:T(8,128)(2,1)S(1)} %get-tuple-element.138.refs_6_), channel_id=1, source_target_pairs={{0,8},{4,12},{8,0},{12,4},{16,24},{20,28},{24,16},{28,20},{1,9},{5... | collective-permute-start | bytes 1572872 | tf_op jit(solution)/shard_map/ppermute | solution.py:261
  110.3 15.9 %collective-permute-start.28 = (bf16[2,128,1024]{2,1,0:T(8,128)(2,1)S(1)}, bf16[2,128,1024]{2,1,0:T(8,128)(2,1)S(1)}, u32[]{:S(2)}, u32[]{:S(2)}) collective-permute-start(bf16[2,128,1024]{2,1,0:T(8,128)(2,1)S(1)} %get-tuple-element.141.refs_2_), channel_id=1, source_target_pairs={{0,4},{4,0},{8,12},{12,8},{16,20},{20,16},{24,28},{28,24},{1,5},{5... | collective-permute-start | bytes 1572872 | tf_op jit(solution)/shard_map/ppermute | solution.py:261
  111.7 14.5 %collective-permute-start.30 = (bf16[2,96,128]{2,1,0:T(8,128)(2,1)S(1)}, bf16[2,96,128]{2,1,0:T(8,128)(2,1)S(1)}, u32[]{:S(2)}, u32[]{:S(2)}) collective-permute-start(bf16[2,96,128]{2,1,0:T(8,128)(2,1)S(1)} %get-tuple-element.144), channel_id=1, source_target_pairs={{0,4},{4,0},{8,12},{12,8},{16,20},{20,16},{24,28},{28,24},{1,5},{5... | collective-permute-start | bytes 147464 | tf_op jit(solution)/shard_map/ppermute | solution.py:261
  112.4 13.8 %collective-permute-start.31 = (bf16[2,96,128]{2,1,0:T(8,128)(2,1)S(1)}, bf16[2,96,128]{2,1,0:T(8,128)(2,1)S(1)}, u32[]{:S(2)}, u32[]{:S(2)}) collective-permute-start(bf16[2,96,128]{2,1,0:T(8,128)(2,1)S(1)} %get-tuple-element.145), channel_id=1, source_target_pairs={{0,8},{4,12},{8,0},{12,4},{16,24},{20,28},{24,16},{28,20},{1,9},{5... | collective-permute-start | bytes 147464 | tf_op jit(solution)/shard_map/ppermute | solution.py:261
  131.5 12.4 %collective-permute-start.39 = (bf16[96,384]{1,0:T(8,128)(2,1)S(1)}, bf16[96,384]{1,0:T(8,128)(2,1)S(1)}, u32[]{:S(2)}, u32[]{:S(2)}) collective-permute-start(bf16[96,384]{1,0:T(8,128)(2,1)S(1)} %get-tuple-element.158.refs_5_), channel_id=1, source_target_pairs={{0,12},{4,8},{8,4},{12,0},{16,28},{20,24},{24,20},{28,16},{1,13},{... | collective-permute-start | bytes 221192 | tf_op jit(solution)/shard_map/ppermute | solution.py:261
  133.8 12.5 %collective-permute-start.41 = (bf16[96,384]{1,0:T(8,128)(2,1)S(1)}, bf16[96,384]{1,0:T(8,128)(2,1)S(1)}, u32[]{:S(2)}, u32[]{:S(2)}) collective-permute-start(bf16[96,384]{1,0:T(8,128)(2,1)S(1)} %get-tuple-element.160.refs_7_), channel_id=1, source_target_pairs={{0,20},{4,16},{8,28},{12,24},{16,4},{20,0},{24,12},{28,8},{1,21},{... | collective-permute-start | bytes 221192 | tf_op jit(solution)/shard_map/ppermute | solution.py:261
  148.7 26.3 %collective-permute-start.49 = (bf16[2,128,1024]{2,1,0:T(8,128)(2,1)S(1)}, bf16[2,128,1024]{2,1,0:T(8,128)(2,1)S(1)}, u32[]{:S(2)}, u32[]{:S(2)}) collective-permute-start(bf16[2,128,1024]{2,1,0:T(8,128)(2,1)S(1)} %get-tuple-element.153.refs_8_), channel_id=1, source_target_pairs={{0,16},{4,20},{8,24},{12,28},{16,0},{20,4},{24,8},{28,12},{1,17},{... | collective-permute-start | bytes 1572872 | tf_op jit(solution)/shard_map/ppermute | solution.py:261
  151.5 24.5 %collective-permute-start.46 = (bf16[2,136,640]{2,1,0:T(8,128)(2,1)S(1)}, bf16[2,136,640]{2,1,0:T(8,128)(2,1)S(1)}, u32[]{:S(2)}, u32[]{:S(2)}) collective-permute-start(bf16[2,136,640]{2,1,0:T(8,128)(2,1)S(1)} %get-tuple-element.172), channel_id=1, source_target_pairs={{0,4},{4,0},{8,12},{12,8},{16,20},{20,16},{24,28},{28,24},{1,5},{5... | collective-permute-start | bytes 1044488 | tf_op jit(solution)/shard_map/ppermute | solution.py:261
  152.3 25.0 %collective-permute-start.47 = (bf16[2,136,640]{2,1,0:T(8,128)(2,1)S(1)}, bf16[2,136,640]{2,1,0:T(8,128)(2,1)S(1)}, u32[]{:S(2)}, u32[]{:S(2)}) collective-permute-start(bf16[2,136,640]{2,1,0:T(8,128)(2,1)S(1)} %get-tuple-element.173), channel_id=1, source_target_pairs={{0,8},{4,12},{8,0},{12,4},{16,24},{20,28},{24,16},{28,20},{1,9},{5... | collective-permute-start | bytes 1044488 | tf_op jit(solution)/shard_map/ppermute | solution.py:261
  152.3 27.5 %collective-permute-start.48 = (bf16[2,136,640]{2,1,0:T(8,128)(2,1)S(1)}, bf16[2,136,640]{2,1,0:T(8,128)(2,1)S(1)}, u32[]{:S(2)}, u32[]{:S(2)}) collective-permute-start(bf16[2,136,640]{2,1,0:T(8,128)(2,1)S(1)} %get-tuple-element.174), channel_id=1, source_target_pairs={{0,12},{4,8},{8,4},{12,0},{16,28},{20,24},{24,20},{28,16},{1,13},{... | collective-permute-start | bytes 1044488 | tf_op jit(solution)/shard_map/ppermute | solution.py:261
  155.2 28.0 %collective-permute-start.45 = (bf16[96,1024]{1,0:T(8,128)(2,1)S(1)}, bf16[96,1024]{1,0:T(8,128)(2,1)S(1)}, u32[]{:S(2)}, u32[]{:S(2)}) collective-permute-start(bf16[96,1024]{1,0:T(8,128)(2,1)S(1)} %get-tuple-element.171.refs_3_), channel_id=1, source_target_pairs={{0,2},{1,3},{2,0},{3,1},{4,6},{5,7},{6,4},{7,5},{8,10},{9,11},{10,... | collective-permute-start | bytes 589832 | tf_op jit(solution)/shard_map/ppermute | solution.py:261
  176.0 13.8 %collective-permute-start.50 = (bf16[96,1024]{1,0:T(8,128)(2,1)S(1)}, bf16[96,1024]{1,0:T(8,128)(2,1)S(1)}, u32[]{:S(2)}, u32[]{:S(2)}) collective-permute-start(bf16[96,1024]{1,0:T(8,128)(2,1)S(1)} %get-tuple-element.169.refs_2_), channel_id=1, source_target_pairs={{0,2},{1,3},{2,0},{3,1},{4,6},{5,7},{6,4},{7,5},{8,10},{9,11},{10,... | collective-permute-start | bytes 589832 | tf_op jit(solution)/shard_map/ppermute | solution.py:261
  180.0 16.3 %collective-permute-start.51 = (bf16[1,136,640]{2,1,0:T(8,128)(2,1)S(1)}, bf16[1,136,640]{2,1,0:T(8,128)(2,1)S(1)}, u32[]{:S(2)}, u32[]{:S(2)}) collective-permute-start(bf16[1,136,640]{2,1,0:T(8,128)(2,1)S(1)} %get-tuple-element.178.refs_8_), channel_id=1, source_target_pairs={{0,16},{4,20},{8,24},{12,28},{16,0},{20,4},{24,8},{28,12},{1,17},{... | collective-permute-start | bytes 522248 | tf_op jit(solution)/shard_map/ppermute | solution.py:261
  181.3 23.7 %collective-permute-start.60 = (bf16[128,1024]{1,0:T(8,128)(2,1)S(1)}, bf16[128,1024]{1,0:T(8,128)(2,1)S(1)}, u32[]{:S(2)}, u32[]{:S(2)}) collective-permute-start(bf16[128,1024]{1,0:T(8,128)(2,1)S(1)} %get-tuple-element.200), channel_id=1, source_target_pairs={{0,0},{1,8},{2,16},{3,24},{4,1},{5,9},{6,17},{7,25},{8,2},{9,10},{... | collective-permute-start | bytes 786440 | tf_op jit(solution)/shard_map/ppermute | solution.py:1036
  (47 other events, 343.8 us)

commit v4 on v3

--- a/solution.py
+++ b/solution.py
@@ -924,6 +924,7 @@
     near_rows = lax.all_gather(turned, "fsdp", axis=0, tiled=True)
     far_rows = lax.all_gather(turned_far, "fsdp", axis=0, tiled=True)
     w_across = call.hold(w_across, near_rows)
+    up_across = call.hold(up_across, far_rows)
     w_parts = (w_mine, exchange(w_beside, "fsdp", 4, 1), w_across, exchange(w_across, "ctx", 8, 1))
     up_beside, up_across = exchange(up_beside, "fsdp", 4, 1), swap_across(up_across, 0)
     far_heads, heads, stack, probs, norm1 = call(
@@ -946,10 +947,10 @@
         cut_rest_kernel, (local((part, 384), BF16),) * 4, (ids,), (), far=(w_qkv,),
         scratch=[dma((12,))], name="cut_rest", weight=0,
     )
-    heads = swap_in_two(call, heads, far_heads)
+    heads = swap_in_two(call, heads, far_heads, up_across)
     attended, send, keep, attn_part = call(
         out_kernel, (all_quarter, pair_bf, pair_f, local((4 * count, width), F32)),
-        (ids,), (*heads, w_out), name="attn_out", after=(up_across,),
+        (ids,), (*heads, w_out), name="attn_out", after=(up_across, both_x),
     )
     up_parts = (up_mine, up_beside, up_across, exchange(up_across, "ctx", 8, 1))
     rest = swap_pieces(rest)
@@ -1064,10 +1065,10 @@
     )
     qkv_chunks = swap_pieces(qkv_chunks)
     grad_out = lax.ppermute(grad_out, ("ctx", "fsdp"), owners)
+    row = sds((1, 32), F32)
     (grad_down,) = call(
         join_down_kernel, (sds((128, width), F32),), (), (down,), name="join_down"
     )
-    row = sds((1, 32), F32)
     grad_up, grad_gain_mlp = call(
         join_up_kernel, (sds((32, 4 * hidden), F32), row), (ids,), (*chunks, gain_mlp), name="join_up"
     )

time: 211 us -> 208 us (0.986)
  waiting for transfers between devices: 82.2 us -> 74.9 us
  starting transfers between devices: 62.4 us -> 67.1 us
    ppermute x56, waiting for transfers between devices: 75.7 us -> 68.9 us  [exchange(): return lax.ppermute(x, axis, [(i, i ^ mask) for i in range(size)])]
    ppermute x56, starting transfers between devices: 52.3 us -> 57.4 us  [exchange(): return lax.ppermute(x, axis, [(i, i ^ mask) for i in range(size)])]
    pallas_call x35 -> x36, Pallas kernels: 40.3 us -> 40.3 us  [__call__(): pl.pallas_call(body, out_shape=tuple(outs), in_specs=[pl.BlockSpec(memory...]
  transfers between devices with their start and end apart: 61 -> 61, of which waited for: 19 -> 20; matrix products, arithmetic and copies ran while one was open for 0% -> 0% of each run, Pallas kernels for 14% -> 15%
where the time goes in v4:
time: 208 us; the launch traced here: 207 us
  waiting for transfers between devices  74.9 us (36%)
  starting transfers between devices  67.1 us (32%)
  Pallas kernels  40.3 us (19%)
  blocking collectives  21.6 us (10%)
    ppermute x56, waiting for transfers between devices, exchange(): return lax.ppermute(x, axis, [(i, i ^ mask) for i in range(size)])  68.9 us
    ppermute x56, starting transfers between devices, exchange(): return lax.ppermute(x, axis, [(i, i ^ mask) for i in range(size)])  57.4 us
    pallas_call x36, Pallas kernels, __call__(): pl.pallas_call(body, out_shape=tuple(outs), in_specs=[pl.BlockSpec(memory...  40.3 us
    all_gather x1, blocking collectives, shards_8x4(): near_rows = lax.all_gather(turned, 'fsdp', axis=0, tiled=True)  12.7 us
    all_gather x1, blocking collectives, shards_8x4(): far_rows = lax.all_gather(turned_far, 'fsdp', axis=0, tiled=True)  8.84 us
  transfers between devices with their start and end apart: 61, of which 20 were waited for; matrix products, arithmetic and copies ran while one was open for 0% of the time, Pallas kernels for 15%

profile of v4, /device:TPU:4, one launch (start us, length us, event | category | flops | bytes accessed | tf_op | source)
XLA Modules:
  0.0 207.2 jit_solution(12142007418696276692)
XLA Ops:
  2.1 2.5 %front.1 = (bf16[104,1024]{1,0:T(8,128)(2,1)S(1)}, bf16[256,384]{1,0:T(8,128)(2,1)S(1)}, bf16[256,384]{1,0:T(8,128)(2,1)S(1)}, bf16[256,384]{1,0:T(8,128)(2,1)S(1)}) custom-call(s32[2]{0:T(128)S(1)} %pad_add_fusion.refs_0_, s32[16]{0:T(128)S(1)} %copy-done.9, bf16[3,256,1024]{2,1,0:T(8,128)(2,1)} %bitcast.21, bf16[256,3072]{1,0:T(8,128)(2,1)} %refs_1_.6, ...), custom_call_target="tpu_custom_call" | custom-call | flops 10000000000 | bytes 1000000 | tf_op jit(solution)/shard_map/front/pallas_call | solution.py:221
  11.7 2.6 %collective-permute-start.1 = (bf16[104,1024]{1,0:T(8,128)(2,1)S(1)}, bf16[104,1024]{1,0:T(8,128)(2,1)S(1)}, u32[]{:S(2)}, u32[]{:S(2)}) collective-permute-start(bf16[104,1024]{1,0:T(8,128)(2,1)S(1)} %collective-permute-done), channel_id=1, source_target_pairs={{0,16},{4,20},{8,24},{12,28},{16,0},{20,4},{24,8},{28,12},{1,17},{... | collective-permute-start | bytes 638984 | tf_op jit(solution)/shard_map/ppermute | solution.py:261
  14.3 12.7 %all_gather.6.refs_2_.refs_1_ = bf16[416,1024]{1,0:T(8,128)(2,1)S(1)} all-gather(bf16[104,1024]{1,0:T(8,128)(2,1)S(1)} %collective-permute-done), channel_id=1, replica_groups=mesh['ctx'=8,'fsdp'=4] {'fsdp'}, dimensions={0}, use_global_device_ids=true | all-gather | bytes 1064960 | tf_op jit(solution)/shard_map/all_gather | solution.py:924
  27.4 8.8 %all_gather.7.refs_2_ = bf16[416,1024]{1,0:T(8,128)(2,1)S(1)} all-gather(bf16[104,1024]{1,0:T(8,128)(2,1)S(1)} %collective-permute-done.1), channel_id=1, replica_groups=mesh['ctx'=8,'fsdp'=4] {'fsdp'}, dimensions={0}, use_global_device_ids=true | all-gather | bytes 1064960 | tf_op jit(solution)/shard_map/all_gather | solution.py:925
  37.2 3.3 %attend.1 = (bf16[4,96,128]{2,1,0:T(8,128)(2,1)S(1)}, bf16[4,96,128]{2,1,0:T(8,128)(2,1)S(1)}, bf16[3,256,384]{2,1,0:T(8,128)(2,1)S(1)}, f32[6,256,256]{2,1,0:T(8,128)S(1)}, bf16[768,1024]{1,0:T(8,128)(2,1)S(1)}) custom-call(s32[2]{0:T(128)S(1)} %pad_add_fusion.refs_0_, bf16[416,1024]{1,0:T(8,128)(2,1)S(1)} %all_gather.6.refs_2_.refs_1_, ...), custom_call_target="tpu_custom_call" | custom-call | flops 10000000000 | bytes 1000000 | tf_op jit(solution)/shard_map/attend/pallas_call | solution.py:221
  45.6 2.8 %collective-permute-done.5.refs_1_ = bf16[4,96,128]{2,1,0:T(8,128)(2,1)S(1)} collective-permute-done((bf16[4,96,128]{2,1,0:T(8,128)(2,1)S(1)}, bf16[4,96,128]{2,1,0:T(8,128)(2,1)S(1)}, u32[]{:S(2)}, u32[]{:S(2)}) %collective-permute-start.5) | collective-permute-done | bytes 98336 | tf_op jit(solution)/shard_map/ppermute | solution.py:261
  50.1 2.8 %collective-permute-start.7 = (bf16[2,96,128]{2,1,0:T(8,128)(2,1)S(1)}, bf16[2,96,128]{2,1,0:T(8,128)(2,1)S(1)}, u32[]{:S(2)}, u32[]{:S(2)}) collective-permute-start(bf16[2,96,128]{2,1,0:T(8,128)(2,1)S(1)} %get-tuple-element.115), channel_id=1, source_target_pairs={{0,4},{4,0},{8,12},{12,8},{16,20},{20,16},{24,28},{28,24},{1,5},{5... | collective-permute-start | bytes 147464 | tf_op jit(solution)/shard_map/ppermute | solution.py:261
  54.4 4.9 %collective-permute-done.10.refs_8_.refs_1_.refs_3_.refs_4_.refs_5_ = bf16[200,1024]{1,0:T(8,128)(2,1)S(1)} collective-permute-done((bf16[200,1024]{1,0:T(8,128)(2,1)S(1)}, bf16[200,1024]{1,0:T(8,128)(2,1)S(1)}, u32[]{:S(2)}, u32[]{:S(2)}) %collective-permute-start.10) | collective-permute-done | bytes 409632 | tf_op jit(solution)/shard_map/ppermute | solution.py:261
  64.9 8.5 %collective-permute-done.12.refs_1_ = bf16[2,96,1024]{2,1,0:T(8,128)(2,1)S(1)} collective-permute-done((bf16[2,96,1024]{2,1,0:T(8,128)(2,1)S(1)}, bf16[2,96,1024]{2,1,0:T(8,128)(2,1)S(1)}, u32[]{:S(2)}, u32[]{:S(2)}) %collective-permute-start.12) | collective-permute-done | bytes 393248 | tf_op jit(solution)/shard_map/ppermute | solution.py:261
  77.5 4.1 %mlp.1 = (bf16[2,96,1024]{2,1,0:T(8,128)(2,1)S(1)}, f32[2,96,1024]{2,1,0:T(8,128)S(1)}, bf16[384,512]{1,0:T(8,128)(2,1)S(1)}, bf16[384,512]{1,0:T(8,128)(2,1)S(1...) custom-call(s32[2]{0:T(128)S(1)} %pad_add_fusion.refs_0_, ...), custom_call_target="tpu_custom_call" | custom-call | flops 10000000000 | bytes 1000000 | tf_op jit(solution)/shard_map/mlp/pallas_call | solution.py:221
  88.1 6.4 %collective-permute-done.20.refs_8_.refs_5_ = bf16[384,512]{1,0:T(8,128)(2,1)S(1)} collective-permute-done((bf16[384,512]{1,0:T(8,128)(2,1)S(1)}, bf16[384,512]{1,0:T(8,128)(2,1)S(1)}, u32[]{:S(2)}, u32[]{:S(2)}) %collective-permute-start.20) | collective-permute-done | bytes 393248 | tf_op jit(solution)/shard_map/ppermute | solution.py:261
  113.7 9.7 %collective-permute-done.30.refs_2_ = bf16[2,96,128]{2,1,0:T(8,128)(2,1)S(1)} collective-permute-done((bf16[2,96,128]{2,1,0:T(8,128)(2,1)S(1)}, bf16[2,96,128]{2,1,0:T(8,128)(2,1)S(1)}, u32[]{:S(2)}, u32[]{:S(2)}) %collective-permute-start.30) | collective-permute-done | bytes 49184 | tf_op jit(solution)/shard_map/ppermute | solution.py:261
  123.4 3.0 %attend_back.1 = (bf16[96,384]{1,0:T(8,128)(2,1)S(1)}, bf16[96,384]{1,0:T(8,128)(2,1)S(1)}, bf16[96,384]{1,0:T(8,128)(2,1)S(1)}, bf16[96,384]{1,0:T(8,128)(2,1)S...) custom-call(s32[2]{0:T(128)S(1)} %pad_add_fusion.refs_0_, ...), custom_call_target="tpu_custom_call" | custom-call | flops 10000000000 | bytes 1000000 | tf_op jit(solution)/shard_map/attend_back/pallas_call | solution.py:221
  133.6 2.5 %collective-permute-start.42 = (bf16[96,384]{1,0:T(8,128)(2,1)S(1)}, bf16[96,384]{1,0:T(8,128)(2,1)S(1)}, u32[]{:S(2)}, u32[]{:S(2)}) collective-permute-start(bf16[96,384]{1,0:T(8,128)(2,1)S(1)} %get-tuple-element.161.refs_8_), channel_id=1, source_target_pairs={{0,24},{4,28},{8,16},{12,20},{16,8},{20,12},{24,0},{28,4},{1,25},{... | collective-permute-start | bytes 221192 | tf_op jit(solution)/shard_map/ppermute | solution.py:261
  141.1 2.5 %collective-permute-done.41.refs_6_ = bf16[96,384]{1,0:T(8,128)(2,1)S(1)} collective-permute-done((bf16[96,384]{1,0:T(8,128)(2,1)S(1)}, bf16[96,384]{1,0:T(8,128)(2,1)S(1)}, u32[]{:S(2)}, u32[]{:S(2)}) %collective-permute-start.41) | collective-permute-done | bytes 73760 | tf_op jit(solution)/shard_map/ppermute | solution.py:261
  146.0 3.2 %collective-permute-start.49 = (bf16[2,128,1024]{2,1,0:T(8,128)(2,1)S(1)}, bf16[2,128,1024]{2,1,0:T(8,128)(2,1)S(1)}, u32[]{:S(2)}, u32[]{:S(2)}) collective-permute-start(bf16[2,128,1024]{2,1,0:T(8,128)(2,1)S(1)} %get-tuple-element.153.refs_8_), channel_id=1, source_target_pairs={{0,16},{4,20},{8,24},{12,28},{16,0},{20,4},{24,8},{28,12},{1,17},{... | collective-permute-start | bytes 1572872 | tf_op jit(solution)/shard_map/ppermute | solution.py:261
  149.9 2.7 %collective-permute-start.48 = (bf16[2,136,640]{2,1,0:T(8,128)(2,1)S(1)}, bf16[2,136,640]{2,1,0:T(8,128)(2,1)S(1)}, u32[]{:S(2)}, u32[]{:S(2)}) collective-permute-start(bf16[2,136,640]{2,1,0:T(8,128)(2,1)S(1)} %get-tuple-element.174), channel_id=1, source_target_pairs={{0,12},{4,8},{8,4},{12,0},{16,28},{20,24},{24,20},{28,16},{1,13},{... | collective-permute-start | bytes 1044488 | tf_op jit(solution)/shard_map/ppermute | solution.py:261
  154.2 18.4 %collective-permute-done.49.refs_2_ = bf16[2,128,1024]{2,1,0:T(8,128)(2,1)S(1)} collective-permute-done((bf16[2,128,1024]{2,1,0:T(8,128)(2,1)S(1)}, bf16[2,128,1024]{2,1,0:T(8,128)(2,1)S(1)}, u32[]{:S(2)}, u32[]{:S(2)}) %collective-permute-start.49) | collective-permute-done | bytes 524320 | tf_op jit(solution)/shard_map/ppermute | solution.py:261
  176.7 2.8 %collective-permute-start.51 = (bf16[1,136,640]{2,1,0:T(8,128)(2,1)S(1)}, bf16[1,136,640]{2,1,0:T(8,128)(2,1)S(1)}, u32[]{:S(2)}, u32[]{:S(2)}) collective-permute-start(bf16[1,136,640]{2,1,0:T(8,128)(2,1)S(1)} %get-tuple-element.178.refs_8_), channel_id=1, source_target_pairs={{0,16},{4,20},{8,24},{12,28},{16,0},{20,4},{24,8},{28,12},{1,17},{... | collective-permute-start | bytes 522248 | tf_op jit(solution)/shard_map/ppermute | solution.py:261
  181.4 2.3 %output.1 = (f32[96,1]{1,0:T(8,128)S(1)}, bf16[3,256,1024]{2,1,0:T(8,128)(2,1)}) custom-call(s32[2]{0:T(128)S(1)} %pad_add_fusion.refs_0_, s32[3,32]{1,0:T(4,128)S(1)} %bitcast.25, f32[96,1024]{1,0:T(8,128)S(1)} %get-tuple-element.170.refs_2_, bf16[96,1024]{1,0:T(8,128)(2,1)S(1)} %collective-permute-done.45.refs_3_, ...), custom_call_target="tpu_custom_call" | custom-call | tf_op jit(solution)/shard_map/output/pallas_call | solution.py:221
  187.4 2.4 %input_grad.1 = bf16[3,256,1024]{2,1,0:T(8,128)(2,1)} custom-call(s32[2]{0:T(128)S(1)} %pad_add_fusion.refs_0_, s32[3,32]{1,0:T(4,128)S(1)} %bitcast.26, f32[96,1024]{1,0:T(8,128)S(1)} %get-tuple-element.180.refs_2_, bf16[96,1024]{1,0:T(8,128)(2,1)S(1)} %collective-permute-done.50.refs_3_, f32[96,1024]{1,0:T(8,128)S(1)} %get-tuple-element.135.refs_4_, ...), custom_call_target="tpu_custom_call" | custom-call | tf_op jit(solution)/shard_map/input_grad/pallas_call | solution.py:221
  189.9 3.9 %collective-permute-done.51.refs_2_ = bf16[1,136,640]{2,1,0:T(8,128)(2,1)S(1)} collective-permute-done((bf16[1,136,640]{2,1,0:T(8,128)(2,1)S(1)}, bf16[1,136,640]{2,1,0:T(8,128)(2,1)S(1)}, u32[]{:S(2)}, u32[]{:S(2)}) %collective-permute-start.51) | collective-permute-done | bytes 174112 | tf_op jit(solution)/shard_map/ppermute | solution.py:261
  196.4 2.8 %collective-permute-start.56 = (f32[32,1024]{1,0:T(8,128)S(1)}, f32[32,1024]{1,0:T(8,128)S(1)}, u32[]{:S(2)}, u32[]{:S(2)}) collective-permute-start(f32[32,1024]{1,0:T(8,128)S(1)} %get-tuple-element.194), channel_id=1, source_target_pairs={{0,0},{1,8},{2,16},{3,24},{4,1},{5,9},{6,17},{7,25},{8,2},{9,10},{... | collective-permute-start | bytes 393224 | tf_op jit(solution)/shard_map/ppermute | solution.py:1067
  202.9 3.7 %collective-permute-done.56 = f32[32,1024]{1,0:T(8,128)S(1)} collective-permute-done((f32[32,1024]{1,0:T(8,128)S(1)}, f32[32,1024]{1,0:T(8,128)S(1)}, u32[]{:S(2)}, u32[]{:S(2)}) %collective-permute-start.56) | collective-permute-done | bytes 131104 | tf_op jit(solution)/shard_map/ppermute | solution.py:1067
  (160 shorter events, 86.8 us)
Async XLA Ops:
  6.5 20.6 %collective-permute-start.3 = (bf16[256,384]{1,0:T(8,128)(2,1)S(1)}, bf16[256,384]{1,0:T(8,128)(2,1)S(1)}, u32[]{:S(2)}, u32[]{:S(2)}) collective-permute-start(bf16[256,384]{1,0:T(8,128)(2,1)S(1)} %get-tuple-element.108), channel_id=1, source_target_pairs={{0,2},{1,3},{2,0},{3,1},{4,7},{5,6},{6,5},{7,4},{8,10},{9,11},{10,... | collective-permute-start | bytes 589832 | tf_op jit(solution)/shard_map/ppermute | solution.py:863
  8.7 28.5 %collective-permute-start.2 = (bf16[256,384]{1,0:T(8,128)(2,1)S(1)}, bf16[256,384]{1,0:T(8,128)(2,1)S(1)}, u32[]{:S(2)}, u32[]{:S(2)}) collective-permute-start(bf16[256,384]{1,0:T(8,128)(2,1)S(1)} %get-tuple-element.107), channel_id=1, source_target_pairs={{0,1},{1,0},{2,3},{3,2},{4,5},{5,4},{6,7},{7,6},{8,9},{9,8},{10,11... | collective-permute-start | bytes 589832 | tf_op jit(solution)/shard_map/ppermute | solution.py:261
  11.7 15.7 %collective-permute-start.1 = (bf16[104,1024]{1,0:T(8,128)(2,1)S(1)}, bf16[104,1024]{1,0:T(8,128)(2,1)S(1)}, u32[]{:S(2)}, u32[]{:S(2)}) collective-permute-start(bf16[104,1024]{1,0:T(8,128)(2,1)S(1)} %collective-permute-done), channel_id=1, source_target_pairs={{0,16},{4,20},{8,24},{12,28},{16,0},{20,4},{24,8},{28,12},{1,17},{... | collective-permute-start | bytes 638984 | tf_op jit(solution)/shard_map/ppermute | solution.py:261
  36.3 13.8 %collective-permute-start.6 = (bf16[256,1024]{1,0:T(8,128)(2,1)S(1)}, bf16[256,1024]{1,0:T(8,128)(2,1)S(1)}, u32[]{:S(2)}, u32[]{:S(2)}) collective-permute-start(bf16[256,1024]{1,0:T(8,128)(2,1)S(1)} %hold.3.refs_8_), channel_id=1, source_target_pairs={{0,2},{1,3},{2,0},{3,1},{4,7},{5,6},{6,5},{7,4},{8,10},{9,11},{10,... | collective-permute-start | bytes 1572872 | tf_op jit(solution)/shard_map/ppermute | solution.py:863
  44.8 14.5 %collective-permute-start.10 = (bf16[200,1024]{1,0:T(8,128)(2,1)S(1)}, bf16[200,1024]{1,0:T(8,128)(2,1)S(1)}, u32[]{:S(2)}, u32[]{:S(2)}) collective-permute-start(bf16[200,1024]{1,0:T(8,128)(2,1)S(1)} %cot_rows.1.refs_2_.refs_0_.refs_3_.refs_4_.refs_5_), channel_id=1, source_target_pairs={{0,2},{1,3},{2,0},{3,1},{4,6},{5,7},{6,4},{7,5},{8,10},{9,11},{10,... | collective-permute-start | bytes 1228808 | tf_op jit(solution)/shard_map/ppermute | solution.py:261
  63.1 13.2 %collective-permute-start.16 = (bf16[256,1024]{1,0:T(8,128)(2,1)S(1)}, bf16[256,1024]{1,0:T(8,128)(2,1)S(1)}, u32[]{:S(2)}, u32[]{:S(2)}) collective-permute-start(bf16[256,1024]{1,0:T(8,128)(2,1)S(1)} %get-tuple-element.123), channel_id=1, source_target_pairs={{0,1},{1,0},{2,3},{3,2},{4,5},{5,4},{6,7},{7,6},{8,9},{9,8},{10,11... | collective-permute-start | bytes 1572872 | tf_op jit(solution)/shard_map/ppermute | solution.py:261
  63.1 14.3 %collective-permute-start.17 = (bf16[256,1024]{1,0:T(8,128)(2,1)S(1)}, bf16[256,1024]{1,0:T(8,128)(2,1)S(1)}, u32[]{:S(2)}, u32[]{:S(2)}) collective-permute-start(bf16[256,1024]{1,0:T(8,128)(2,1)S(1)} %collective-permute-done.6.refs_3_.refs_7_.refs_6_), channel_id=1, source_target_pairs={{0,4},{4,0},{8,12},{12,8},{16,20},{20,16},{24,28},{28,24},{1,5},{5... | collective-permute-start | bytes 1572872 | tf_op jit(solution)/shard_map/ppermute | solution.py:261
  74.8 11.9 %collective-permute-start.18 = (bf16[2,96,1024]{2,1,0:T(8,128)(2,1)S(1)}, bf16[2,96,1024]{2,1,0:T(8,128)(2,1)S(1)}, u32[]{:S(2)}, u32[]{:S(2)}) collective-permute-start(bf16[2,96,1024]{2,1,0:T(8,128)(2,1)S(1)} %get-tuple-element.122.refs_1_), channel_id=1, source_target_pairs={{0,4},{4,0},{8,12},{12,8},{16,20},{20,16},{24,28},{28,24},{1,5},{5... | collective-permute-start | bytes 1179656 | tf_op jit(solution)/shard_map/ppermute | solution.py:261
  81.6 12.8 %collective-permute-start.20 = (bf16[384,512]{1,0:T(8,128)(2,1)S(1)}, bf16[384,512]{1,0:T(8,128)(2,1)S(1)}, u32[]{:S(2)}, u32[]{:S(2)}) collective-permute-start(bf16[384,512]{1,0:T(8,128)(2,1)S(1)} %get-tuple-element.130), channel_id=1, source_target_pairs={{0,4},{4,0},{8,12},{12,8},{16,20},{20,16},{24,28},{28,24},{1,5},{5... | collective-permute-start | bytes 1179656 | tf_op jit(solution)/shard_map/ppermute | solution.py:261
  105.1 18.3 %collective-permute-start.26 = (bf16[2,256,512]{2,1,0:T(8,128)(2,1)S(1)}, bf16[2,256,512]{2,1,0:T(8,128)(2,1)S(1)}, u32[]{:S(2)}, u32[]{:S(2)}) collective-permute-start(bf16[2,256,512]{2,1,0:T(8,128)(2,1)S(1)} %get-tuple-element.138.refs_6_), channel_id=1, source_target_pairs={{0,8},{4,12},{8,0},{12,4},{16,24},{20,28},{24,16},{28,20},{1,9},{5... | collective-permute-start | bytes 1572872 | tf_op jit(solution)/shard_map/ppermute | solution.py:261
  107.9 15.5 %collective-permute-start.28 = (bf16[2,128,1024]{2,1,0:T(8,128)(2,1)S(1)}, bf16[2,128,1024]{2,1,0:T(8,128)(2,1)S(1)}, u32[]{:S(2)}, u32[]{:S(2)}) collective-permute-start(bf16[2,128,1024]{2,1,0:T(8,128)(2,1)S(1)} %get-tuple-element.141.refs_2_), channel_id=1, source_target_pairs={{0,4},{4,0},{8,12},{12,8},{16,20},{20,16},{24,28},{28,24},{1,5},{5... | collective-permute-start | bytes 1572872 | tf_op jit(solution)/shard_map/ppermute | solution.py:261
  109.5 13.9 %collective-permute-start.30 = (bf16[2,96,128]{2,1,0:T(8,128)(2,1)S(1)}, bf16[2,96,128]{2,1,0:T(8,128)(2,1)S(1)}, u32[]{:S(2)}, u32[]{:S(2)}) collective-permute-start(bf16[2,96,128]{2,1,0:T(8,128)(2,1)S(1)} %get-tuple-element.144), channel_id=1, source_target_pairs={{0,4},{4,0},{8,12},{12,8},{16,20},{20,16},{24,28},{28,24},{1,5},{5... | collective-permute-start | bytes 147464 | tf_op jit(solution)/shard_map/ppermute | solution.py:261
  110.0 13.4 %collective-permute-start.31 = (bf16[2,96,128]{2,1,0:T(8,128)(2,1)S(1)}, bf16[2,96,128]{2,1,0:T(8,128)(2,1)S(1)}, u32[]{:S(2)}, u32[]{:S(2)}) collective-permute-start(bf16[2,96,128]{2,1,0:T(8,128)(2,1)S(1)} %get-tuple-element.145), channel_id=1, source_target_pairs={{0,8},{4,12},{8,0},{12,4},{16,24},{20,28},{24,16},{28,20},{1,9},{5... | collective-permute-start | bytes 147464 | tf_op jit(solution)/shard_map/ppermute | solution.py:261
  128.3 12.8 %collective-permute-start.39 = (bf16[96,384]{1,0:T(8,128)(2,1)S(1)}, bf16[96,384]{1,0:T(8,128)(2,1)S(1)}, u32[]{:S(2)}, u32[]{:S(2)}) collective-permute-start(bf16[96,384]{1,0:T(8,128)(2,1)S(1)} %get-tuple-element.158.refs_5_), channel_id=1, source_target_pairs={{0,12},{4,8},{8,4},{12,0},{16,28},{20,24},{24,20},{28,16},{1,13},{... | collective-permute-start | bytes 221192 | tf_op jit(solution)/shard_map/ppermute | solution.py:261
  131.9 11.7 %collective-permute-start.41 = (bf16[96,384]{1,0:T(8,128)(2,1)S(1)}, bf16[96,384]{1,0:T(8,128)(2,1)S(1)}, u32[]{:S(2)}, u32[]{:S(2)}) collective-permute-start(bf16[96,384]{1,0:T(8,128)(2,1)S(1)} %get-tuple-element.160.refs_7_), channel_id=1, source_target_pairs={{0,20},{4,16},{8,28},{12,24},{16,4},{20,0},{24,12},{28,8},{1,21},{... | collective-permute-start | bytes 221192 | tf_op jit(solution)/shard_map/ppermute | solution.py:261
  146.0 26.7 %collective-permute-start.49 = (bf16[2,128,1024]{2,1,0:T(8,128)(2,1)S(1)}, bf16[2,128,1024]{2,1,0:T(8,128)(2,1)S(1)}, u32[]{:S(2)}, u32[]{:S(2)}) collective-permute-start(bf16[2,128,1024]{2,1,0:T(8,128)(2,1)S(1)} %get-tuple-element.153.refs_8_), channel_id=1, source_target_pairs={{0,16},{4,20},{8,24},{12,28},{16,0},{20,4},{24,8},{28,12},{1,17},{... | collective-permute-start | bytes 1572872 | tf_op jit(solution)/shard_map/ppermute | solution.py:261
  149.2 24.2 %collective-permute-start.46 = (bf16[2,136,640]{2,1,0:T(8,128)(2,1)S(1)}, bf16[2,136,640]{2,1,0:T(8,128)(2,1)S(1)}, u32[]{:S(2)}, u32[]{:S(2)}) collective-permute-start(bf16[2,136,640]{2,1,0:T(8,128)(2,1)S(1)} %get-tuple-element.172), channel_id=1, source_target_pairs={{0,4},{4,0},{8,12},{12,8},{16,20},{20,16},{24,28},{28,24},{1,5},{5... | collective-permute-start | bytes 1044488 | tf_op jit(solution)/shard_map/ppermute | solution.py:261
  149.7 25.0 %collective-permute-start.47 = (bf16[2,136,640]{2,1,0:T(8,128)(2,1)S(1)}, bf16[2,136,640]{2,1,0:T(8,128)(2,1)S(1)}, u32[]{:S(2)}, u32[]{:S(2)}) collective-permute-start(bf16[2,136,640]{2,1,0:T(8,128)(2,1)S(1)} %get-tuple-element.173), channel_id=1, source_target_pairs={{0,8},{4,12},{8,0},{12,4},{16,24},{20,28},{24,16},{28,20},{1,9},{5... | collective-permute-start | bytes 1044488 | tf_op jit(solution)/shard_map/ppermute | solution.py:261
  149.9 26.6 %collective-permute-start.48 = (bf16[2,136,640]{2,1,0:T(8,128)(2,1)S(1)}, bf16[2,136,640]{2,1,0:T(8,128)(2,1)S(1)}, u32[]{:S(2)}, u32[]{:S(2)}) collective-permute-start(bf16[2,136,640]{2,1,0:T(8,128)(2,1)S(1)} %get-tuple-element.174), channel_id=1, source_target_pairs={{0,12},{4,8},{8,4},{12,0},{16,28},{20,24},{24,20},{28,16},{1,13},{... | collective-permute-start | bytes 1044488 | tf_op jit(solution)/shard_map/ppermute | solution.py:261
  152.8 28.6 %collective-permute-start.45 = (bf16[96,1024]{1,0:T(8,128)(2,1)S(1)}, bf16[96,1024]{1,0:T(8,128)(2,1)S(1)}, u32[]{:S(2)}, u32[]{:S(2)}) collective-permute-start(bf16[96,1024]{1,0:T(8,128)(2,1)S(1)} %get-tuple-element.171.refs_3_), channel_id=1, source_target_pairs={{0,2},{1,3},{2,0},{3,1},{4,6},{5,7},{6,4},{7,5},{8,10},{9,11},{10,... | collective-permute-start | bytes 589832 | tf_op jit(solution)/shard_map/ppermute | solution.py:261
  172.7 11.7 %collective-permute-start.52 = (bf16[128,512]{1,0:T(8,128)(2,1)S(1)}, bf16[128,512]{1,0:T(8,128)(2,1)S(1)}, u32[]{:S(2)}, u32[]{:S(2)}) collective-permute-start(bf16[128,512]{1,0:T(8,128)(2,1)S(1)} %get-tuple-element.177.refs_4_), channel_id=1, source_target_pairs={{0,4},{4,0},{8,12},{12,8},{16,20},{20,16},{24,28},{28,24},{1,5},{5... | collective-permute-start | bytes 393224 | tf_op jit(solution)/shard_map/ppermute | solution.py:261
  173.4 14.1 %collective-permute-start.50 = (bf16[96,1024]{1,0:T(8,128)(2,1)S(1)}, bf16[96,1024]{1,0:T(8,128)(2,1)S(1)}, u32[]{:S(2)}, u32[]{:S(2)}) collective-permute-start(bf16[96,1024]{1,0:T(8,128)(2,1)S(1)} %get-tuple-element.169.refs_2_), channel_id=1, source_target_pairs={{0,2},{1,3},{2,0},{3,1},{4,6},{5,7},{6,4},{7,5},{8,10},{9,11},{10,... | collective-permute-start | bytes 589832 | tf_op jit(solution)/shard_map/ppermute | solution.py:261
  176.7 17.0 %collective-permute-start.51 = (bf16[1,136,640]{2,1,0:T(8,128)(2,1)S(1)}, bf16[1,136,640]{2,1,0:T(8,128)(2,1)S(1)}, u32[]{:S(2)}, u32[]{:S(2)}) collective-permute-start(bf16[1,136,640]{2,1,0:T(8,128)(2,1)S(1)} %get-tuple-element.178.refs_8_), channel_id=1, source_target_pairs={{0,16},{4,20},{8,24},{12,28},{16,0},{20,4},{24,8},{28,12},{1,17},{... | collective-permute-start | bytes 522248 | tf_op jit(solution)/shard_map/ppermute | solution.py:261
  179.5 22.6 %collective-permute-start.60 = (bf16[128,1024]{1,0:T(8,128)(2,1)S(1)}, bf16[128,1024]{1,0:T(8,128)(2,1)S(1)}, u32[]{:S(2)}, u32[]{:S(2)}) collective-permute-start(bf16[128,1024]{1,0:T(8,128)(2,1)S(1)} %get-tuple-element.200), channel_id=1, source_target_pairs={{0,0},{1,8},{2,16},{3,24},{4,1},{5,9},{6,17},{7,25},{8,2},{9,10},{... | collective-permute-start | bytes 786440 | tf_op jit(solution)/shard_map/ppermute | solution.py:1037
  (47 other events, 338.5 us)

commit v5 on v4

--- a/solution.py
+++ b/solution.py
@@ -751,7 +751,8 @@
     return jnp.sum(jnp.where(hit, vector[...], 0.0), axis=1, keepdims=True)
 
 
-def join_up_kernel(ids, p0, p1, p2, p3, gain, out, grad_gain):
+def join_up_kernel(ids, p0, p1, p2, p3, gain, token, out, grad_gain):
+    token[...] = jnp.zeros(token.shape, F32)
     rows, part = out.shape[0], out.shape[1] // 4
     total = jnp.zeros((rows, 1), F32)
     for k, piece in enumerate((p0, p1, p2, p3)):
@@ -778,7 +779,8 @@
     grad_router[...] = as_row(router)
 
 
-def join_down_kernel(block, out):
+def join_down_kernel(block, token, out):
+    token[...] = jnp.zeros(token.shape, F32)
     out[...] = block[...].astype(F32)
 
 
@@ -1066,11 +1068,13 @@
     qkv_chunks = swap_pieces(qkv_chunks)
     grad_out = lax.ppermute(grad_out, ("ctx", "fsdp"), owners)
     row = sds((1, 32), F32)
-    (grad_down,) = call(
-        join_down_kernel, (sds((128, width), F32),), (), (down,), name="join_down"
-    )
-    grad_up, grad_gain_mlp = call(
-        join_up_kernel, (sds((32, 4 * hidden), F32), row), (ids,), (*chunks, gain_mlp), name="join_up"
+    token = local((8, 128), F32)
+    _, grad_down = call(
+        join_down_kernel, (token, sds((128, width), F32)), (), (down,), name="join_down", weight=0
+    )
+    _, grad_up, grad_gain_mlp = call(
+        join_up_kernel, (token, sds((32, 4 * hidden), F32), row), (ids,), (*chunks, gain_mlp),
+        name="join_up", weight=0,
     )
     grad_qkv, grad_gain_attn, grad_router = call(
         join_qkv_kernel, (sds((32, 3 * width), F32), row, row), (ids,), (*qkv_chunks, gain_attn),

time: 208 us -> 214 us (1.029)
  waiting for transfers between devices: 74.9 us -> 81.5 us
    ppermute x56, waiting for transfers between devices: 68.9 us -> 71.4 us  [exchange(): return lax.ppermute(x, axis, [(i, i ^ mask) for i in range(size)])]
    ppermute x1, waiting for transfers between devices: 3.66 us -> 5.93 us  [shards_8x4(): grad_out = lax.ppermute(grad_out, ('ctx', 'fsdp'), owners)]
  transfers between devices with their start and end apart: 61 -> 61, of which waited for: 20 -> 21; matrix products, arithmetic and copies ran while one was open for 0% -> 0% of each run, Pallas kernels for 15% -> 15%
where the time goes in v5:
time: 214 us; the launch traced here: 213 us
  waiting for transfers between devices  81.5 us (38%)
  starting transfers between devices  66.5 us (31%)
  Pallas kernels  40.3 us (19%)
  blocking collectives  21.6 us (10%)
    ppermute x56, waiting for transfers between devices, exchange(): return lax.ppermute(x, axis, [(i, i ^ mask) for i in range(size)])  71.4 us
    ppermute x56, starting transfers between devices, exchange(): return lax.ppermute(x, axis, [(i, i ^ mask) for i in range(size)])  57.7 us
    pallas_call x36, Pallas kernels, __call__(): pl.pallas_call(body, out_shape=tuple(outs), in_specs=[pl.BlockSpec(memory...  40.3 us
    all_gather x1, blocking collectives, shards_8x4(): near_rows = lax.all_gather(turned, 'fsdp', axis=0, tiled=True)  12.7 us
    all_gather x1, blocking collectives, shards_8x4(): far_rows = lax.all_gather(turned_far, 'fsdp', axis=0, tiled=True)  8.84 us
    ppermute x1, waiting for transfers between devices, shards_8x4(): grad_out = lax.ppermute(grad_out, ('ctx', 'fsdp'), owners)  5.93 us
  transfers between devices with their start and end apart: 61, of which 21 were waited for; matrix products, arithmetic and copies ran while one was open for 0% of the time, Pallas kernels for 15%

profile of v5, /device:TPU:4, one launch (start us, length us, event | category | flops | bytes accessed | tf_op | source)
XLA Modules:
  0.0 213.2 jit_solution(2805354284079764426)
XLA Ops:
  2.1 2.5 %front.1 = (bf16[104,1024]{1,0:T(8,128)(2,1)S(1)}, bf16[256,384]{1,0:T(8,128)(2,1)S(1)}, bf16[256,384]{1,0:T(8,128)(2,1)S(1)}, bf16[256,384]{1,0:T(8,128)(2,1)S(1)}) custom-call(s32[2]{0:T(128)S(1)} %pad_add_fusion.refs_0_, s32[16]{0:T(128)S(1)} %copy-done.9, bf16[3,256,1024]{2,1,0:T(8,128)(2,1)} %bitcast.21, bf16[256,3072]{1,0:T(8,128)(2,1)} %refs_1_.6, ...), custom_call_target="tpu_custom_call" | custom-call | flops 10000000000 | bytes 1000000 | tf_op jit(solution)/shard_map/front/pallas_call | solution.py:221
  6.5 2.3 %collective-permute-start.3 = (bf16[256,384]{1,0:T(8,128)(2,1)S(1)}, bf16[256,384]{1,0:T(8,128)(2,1)S(1)}, u32[]{:S(2)}, u32[]{:S(2)}) collective-permute-start(bf16[256,384]{1,0:T(8,128)(2,1)S(1)} %get-tuple-element.111), channel_id=1, source_target_pairs={{0,2},{1,3},{2,0},{3,1},{4,7},{5,6},{6,5},{7,4},{8,10},{9,11},{10,... | collective-permute-start | bytes 589832 | tf_op jit(solution)/shard_map/ppermute | solution.py:865
  11.7 2.6 %collective-permute-start.1 = (bf16[104,1024]{1,0:T(8,128)(2,1)S(1)}, bf16[104,1024]{1,0:T(8,128)(2,1)S(1)}, u32[]{:S(2)}, u32[]{:S(2)}) collective-permute-start(bf16[104,1024]{1,0:T(8,128)(2,1)S(1)} %collective-permute-done), channel_id=1, source_target_pairs={{0,16},{4,20},{8,24},{12,28},{16,0},{20,4},{24,8},{28,12},{1,17},{... | collective-permute-start | bytes 638984 | tf_op jit(solution)/shard_map/ppermute | solution.py:261
  14.3 12.7 %all_gather.6.refs_2_.refs_1_ = bf16[416,1024]{1,0:T(8,128)(2,1)S(1)} all-gather(bf16[104,1024]{1,0:T(8,128)(2,1)S(1)} %collective-permute-done), channel_id=1, replica_groups=mesh['ctx'=8,'fsdp'=4] {'fsdp'}, dimensions={0}, use_global_device_ids=true | all-gather | bytes 1064960 | tf_op jit(solution)/shard_map/all_gather | solution.py:926
  27.4 8.8 %all_gather.7.refs_2_ = bf16[416,1024]{1,0:T(8,128)(2,1)S(1)} all-gather(bf16[104,1024]{1,0:T(8,128)(2,1)S(1)} %collective-permute-done.1), channel_id=1, replica_groups=mesh['ctx'=8,'fsdp'=4] {'fsdp'}, dimensions={0}, use_global_device_ids=true | all-gather | bytes 1064960 | tf_op jit(solution)/shard_map/all_gather | solution.py:927
  37.2 3.3 %attend.1 = (bf16[4,96,128]{2,1,0:T(8,128)(2,1)S(1)}, bf16[4,96,128]{2,1,0:T(8,128)(2,1)S(1)}, bf16[3,256,384]{2,1,0:T(8,128)(2,1)S(1)}, f32[6,256,256]{2,1,0:T(8,128)S(1)}, bf16[768,1024]{1,0:T(8,128)(2,1)S(1)}) custom-call(s32[2]{0:T(128)S(1)} %pad_add_fusion.refs_0_, bf16[416,1024]{1,0:T(8,128)(2,1)S(1)} %all_gather.6.refs_2_.refs_1_, ...), custom_call_target="tpu_custom_call" | custom-call | flops 10000000000 | bytes 1000000 | tf_op jit(solution)/shard_map/attend/pallas_call | solution.py:221
  45.6 2.8 %collective-permute-done.5.refs_1_ = bf16[4,96,128]{2,1,0:T(8,128)(2,1)S(1)} collective-permute-done((bf16[4,96,128]{2,1,0:T(8,128)(2,1)S(1)}, bf16[4,96,128]{2,1,0:T(8,128)(2,1)S(1)}, u32[]{:S(2)}, u32[]{:S(2)}) %collective-permute-start.5) | collective-permute-done | bytes 98336 | tf_op jit(solution)/shard_map/ppermute | solution.py:261
  50.1 2.8 %collective-permute-start.7 = (bf16[2,96,128]{2,1,0:T(8,128)(2,1)S(1)}, bf16[2,96,128]{2,1,0:T(8,128)(2,1)S(1)}, u32[]{:S(2)}, u32[]{:S(2)}) collective-permute-start(bf16[2,96,128]{2,1,0:T(8,128)(2,1)S(1)} %get-tuple-element.118), channel_id=1, source_target_pairs={{0,4},{4,0},{8,12},{12,8},{16,20},{20,16},{24,28},{28,24},{1,5},{5... | collective-permute-start | bytes 147464 | tf_op jit(solution)/shard_map/ppermute | solution.py:261
  54.4 4.9 %collective-permute-done.10.refs_8_.refs_1_.refs_3_.refs_4_.refs_5_ = bf16[200,1024]{1,0:T(8,128)(2,1)S(1)} collective-permute-done((bf16[200,1024]{1,0:T(8,128)(2,1)S(1)}, bf16[200,1024]{1,0:T(8,128)(2,1)S(1)}, u32[]{:S(2)}, u32[]{:S(2)}) %collective-permute-start.10) | collective-permute-done | bytes 409632 | tf_op jit(solution)/shard_map/ppermute | solution.py:261
  64.9 8.5 %collective-permute-done.12.refs_1_ = bf16[2,96,1024]{2,1,0:T(8,128)(2,1)S(1)} collective-permute-done((bf16[2,96,1024]{2,1,0:T(8,128)(2,1)S(1)}, bf16[2,96,1024]{2,1,0:T(8,128)(2,1)S(1)}, u32[]{:S(2)}, u32[]{:S(2)}) %collective-permute-start.12) | collective-permute-done | bytes 393248 | tf_op jit(solution)/shard_map/ppermute | solution.py:261
  77.5 4.1 %mlp.1 = (bf16[2,96,1024]{2,1,0:T(8,128)(2,1)S(1)}, f32[2,96,1024]{2,1,0:T(8,128)S(1)}, bf16[384,512]{1,0:T(8,128)(2,1)S(1)}, bf16[384,512]{1,0:T(8,128)(2,1)S(1...) custom-call(s32[2]{0:T(128)S(1)} %pad_add_fusion.refs_0_, ...), custom_call_target="tpu_custom_call" | custom-call | flops 10000000000 | bytes 1000000 | tf_op jit(solution)/shard_map/mlp/pallas_call | solution.py:221
  88.1 6.4 %collective-permute-done.20.refs_8_.refs_5_ = bf16[384,512]{1,0:T(8,128)(2,1)S(1)} collective-permute-done((bf16[384,512]{1,0:T(8,128)(2,1)S(1)}, bf16[384,512]{1,0:T(8,128)(2,1)S(1)}, u32[]{:S(2)}, u32[]{:S(2)}) %collective-permute-start.20) | collective-permute-done | bytes 393248 | tf_op jit(solution)/shard_map/ppermute | solution.py:261
  113.7 9.7 %collective-permute-done.30.refs_2_ = bf16[2,96,128]{2,1,0:T(8,128)(2,1)S(1)} collective-permute-done((bf16[2,96,128]{2,1,0:T(8,128)(2,1)S(1)}, bf16[2,96,128]{2,1,0:T(8,128)(2,1)S(1)}, u32[]{:S(2)}, u32[]{:S(2)}) %collective-permute-start.30) | collective-permute-done | bytes 49184 | tf_op jit(solution)/shard_map/ppermute | solution.py:261
  123.4 3.0 %attend_back.1 = (bf16[96,384]{1,0:T(8,128)(2,1)S(1)}, bf16[96,384]{1,0:T(8,128)(2,1)S(1)}, bf16[96,384]{1,0:T(8,128)(2,1)S(1)}, bf16[96,384]{1,0:T(8,128)(2,1)S...) custom-call(s32[2]{0:T(128)S(1)} %pad_add_fusion.refs_0_, ...), custom_call_target="tpu_custom_call" | custom-call | flops 10000000000 | bytes 1000000 | tf_op jit(solution)/shard_map/attend_back/pallas_call | solution.py:221
  133.6 2.5 %collective-permute-start.42 = (bf16[96,384]{1,0:T(8,128)(2,1)S(1)}, bf16[96,384]{1,0:T(8,128)(2,1)S(1)}, u32[]{:S(2)}, u32[]{:S(2)}) collective-permute-start(bf16[96,384]{1,0:T(8,128)(2,1)S(1)} %get-tuple-element.164.refs_8_), channel_id=1, source_target_pairs={{0,24},{4,28},{8,16},{12,20},{16,8},{20,12},{24,0},{28,4},{1,25},{... | collective-permute-start | bytes 221192 | tf_op jit(solution)/shard_map/ppermute | solution.py:261
  141.1 2.5 %collective-permute-done.41.refs_6_ = bf16[96,384]{1,0:T(8,128)(2,1)S(1)} collective-permute-done((bf16[96,384]{1,0:T(8,128)(2,1)S(1)}, bf16[96,384]{1,0:T(8,128)(2,1)S(1)}, u32[]{:S(2)}, u32[]{:S(2)}) %collective-permute-start.41) | collective-permute-done | bytes 73760 | tf_op jit(solution)/shard_map/ppermute | solution.py:261
  146.0 3.2 %collective-permute-start.49 = (bf16[2,128,1024]{2,1,0:T(8,128)(2,1)S(1)}, bf16[2,128,1024]{2,1,0:T(8,128)(2,1)S(1)}, u32[]{:S(2)}, u32[]{:S(2)}) collective-permute-start(bf16[2,128,1024]{2,1,0:T(8,128)(2,1)S(1)} %get-tuple-element.156.refs_8_), channel_id=1, source_target_pairs={{0,16},{4,20},{8,24},{12,28},{16,0},{20,4},{24,8},{28,12},{1,17},{... | collective-permute-start | bytes 1572872 | tf_op jit(solution)/shard_map/ppermute | solution.py:261
  149.9 2.7 %collective-permute-start.48 = (bf16[2,136,640]{2,1,0:T(8,128)(2,1)S(1)}, bf16[2,136,640]{2,1,0:T(8,128)(2,1)S(1)}, u32[]{:S(2)}, u32[]{:S(2)}) collective-permute-start(bf16[2,136,640]{2,1,0:T(8,128)(2,1)S(1)} %get-tuple-element.177), channel_id=1, source_target_pairs={{0,12},{4,8},{8,4},{12,0},{16,28},{20,24},{24,20},{28,16},{1,13},{... | collective-permute-start | bytes 1044488 | tf_op jit(solution)/shard_map/ppermute | solution.py:261
  154.2 18.4 %collective-permute-done.49.refs_2_ = bf16[2,128,1024]{2,1,0:T(8,128)(2,1)S(1)} collective-permute-done((bf16[2,128,1024]{2,1,0:T(8,128)(2,1)S(1)}, bf16[2,128,1024]{2,1,0:T(8,128)(2,1)S(1)}, u32[]{:S(2)}, u32[]{:S(2)}) %collective-permute-start.49) | collective-permute-done | bytes 524320 | tf_op jit(solution)/shard_map/ppermute | solution.py:261
  176.7 2.8 %collective-permute-start.51 = (bf16[1,136,640]{2,1,0:T(8,128)(2,1)S(1)}, bf16[1,136,640]{2,1,0:T(8,128)(2,1)S(1)}, u32[]{:S(2)}, u32[]{:S(2)}) collective-permute-start(bf16[1,136,640]{2,1,0:T(8,128)(2,1)S(1)} %get-tuple-element.181.refs_8_), channel_id=1, source_target_pairs={{0,16},{4,20},{8,24},{12,28},{16,0},{20,4},{24,8},{28,12},{1,17},{... | collective-permute-start | bytes 522248 | tf_op jit(solution)/shard_map/ppermute | solution.py:261
  181.4 2.3 %output.1 = (f32[96,1]{1,0:T(8,128)S(1)}, bf16[3,256,1024]{2,1,0:T(8,128)(2,1)}) custom-call(s32[2]{0:T(128)S(1)} %pad_add_fusion.refs_0_, s32[3,32]{1,0:T(4,128)S(1)} %bitcast.25, f32[96,1024]{1,0:T(8,128)S(1)} %get-tuple-element.173.refs_2_, bf16[96,1024]{1,0:T(8,128)(2,1)S(1)} %collective-permute-done.45.refs_3_, ...), custom_call_target="tpu_custom_call" | custom-call | tf_op jit(solution)/shard_map/output/pallas_call | solution.py:221
  187.4 6.4 %collective-permute-done.51.refs_2_ = bf16[1,136,640]{2,1,0:T(8,128)(2,1)S(1)} collective-permute-done((bf16[1,136,640]{2,1,0:T(8,128)(2,1)S(1)}, bf16[1,136,640]{2,1,0:T(8,128)(2,1)S(1)}, u32[]{:S(2)}, u32[]{:S(2)}) %collective-permute-start.51) | collective-permute-done | bytes 174112 | tf_op jit(solution)/shard_map/ppermute | solution.py:261
  198.5 2.4 %input_grad.1 = bf16[3,256,1024]{2,1,0:T(8,128)(2,1)} custom-call(s32[2]{0:T(128)S(1)} %pad_add_fusion.refs_0_, s32[3,32]{1,0:T(4,128)S(1)} %bitcast.26, f32[96,1024]{1,0:T(8,128)S(1)} %get-tuple-element.183.refs_2_, bf16[96,1024]{1,0:T(8,128)(2,1)S(1)} %collective-permute-done.50.refs_3_, f32[96,1024]{1,0:T(8,128)S(1)} %get-tuple-element.138.refs_4_, ...), custom_call_target="tpu_custom_call" | custom-call | tf_op jit(solution)/shard_map/input_grad/pallas_call | solution.py:221
  206.6 5.9 %collective-permute-done.60 = f32[32,1024]{1,0:T(8,128)S(1)} collective-permute-done((f32[32,1024]{1,0:T(8,128)S(1)}, f32[32,1024]{1,0:T(8,128)S(1)}, u32[]{:S(2)}, u32[]{:S(2)}) %collective-permute-start.60) | collective-permute-done | bytes 131104 | tf_op jit(solution)/shard_map/ppermute | solution.py:1069
  (160 shorter events, 88.5 us)
Async XLA Ops:
  6.5 20.6 %collective-permute-start.3 = (bf16[256,384]{1,0:T(8,128)(2,1)S(1)}, bf16[256,384]{1,0:T(8,128)(2,1)S(1)}, u32[]{:S(2)}, u32[]{:S(2)}) collective-permute-start(bf16[256,384]{1,0:T(8,128)(2,1)S(1)} %get-tuple-element.111), channel_id=1, source_target_pairs={{0,2},{1,3},{2,0},{3,1},{4,7},{5,6},{6,5},{7,4},{8,10},{9,11},{10,... | collective-permute-start | bytes 589832 | tf_op jit(solution)/shard_map/ppermute | solution.py:865
  8.7 28.5 %collective-permute-start.2 = (bf16[256,384]{1,0:T(8,128)(2,1)S(1)}, bf16[256,384]{1,0:T(8,128)(2,1)S(1)}, u32[]{:S(2)}, u32[]{:S(2)}) collective-permute-start(bf16[256,384]{1,0:T(8,128)(2,1)S(1)} %get-tuple-element.110), channel_id=1, source_target_pairs={{0,1},{1,0},{2,3},{3,2},{4,5},{5,4},{6,7},{7,6},{8,9},{9,8},{10,11... | collective-permute-start | bytes 589832 | tf_op jit(solution)/shard_map/ppermute | solution.py:261
  11.7 15.7 %collective-permute-start.1 = (bf16[104,1024]{1,0:T(8,128)(2,1)S(1)}, bf16[104,1024]{1,0:T(8,128)(2,1)S(1)}, u32[]{:S(2)}, u32[]{:S(2)}) collective-permute-start(bf16[104,1024]{1,0:T(8,128)(2,1)S(1)} %collective-permute-done), channel_id=1, source_target_pairs={{0,16},{4,20},{8,24},{12,28},{16,0},{20,4},{24,8},{28,12},{1,17},{... | collective-permute-start | bytes 638984 | tf_op jit(solution)/shard_map/ppermute | solution.py:261
  36.3 13.8 %collective-permute-start.6 = (bf16[256,1024]{1,0:T(8,128)(2,1)S(1)}, bf16[256,1024]{1,0:T(8,128)(2,1)S(1)}, u32[]{:S(2)}, u32[]{:S(2)}) collective-permute-start(bf16[256,1024]{1,0:T(8,128)(2,1)S(1)} %hold.3.refs_8_), channel_id=1, source_target_pairs={{0,2},{1,3},{2,0},{3,1},{4,7},{5,6},{6,5},{7,4},{8,10},{9,11},{10,... | collective-permute-start | bytes 1572872 | tf_op jit(solution)/shard_map/ppermute | solution.py:865
  44.8 14.5 %collective-permute-start.10 = (bf16[200,1024]{1,0:T(8,128)(2,1)S(1)}, bf16[200,1024]{1,0:T(8,128)(2,1)S(1)}, u32[]{:S(2)}, u32[]{:S(2)}) collective-permute-start(bf16[200,1024]{1,0:T(8,128)(2,1)S(1)} %cot_rows.1.refs_2_.refs_0_.refs_3_.refs_4_.refs_5_), channel_id=1, source_target_pairs={{0,2},{1,3},{2,0},{3,1},{4,6},{5,7},{6,4},{7,5},{8,10},{9,11},{10,... | collective-permute-start | bytes 1228808 | tf_op jit(solution)/shard_map/ppermute | solution.py:261
  63.1 13.2 %collective-permute-start.16 = (bf16[256,1024]{1,0:T(8,128)(2,1)S(1)}, bf16[256,1024]{1,0:T(8,128)(2,1)S(1)}, u32[]{:S(2)}, u32[]{:S(2)}) collective-permute-start(bf16[256,1024]{1,0:T(8,128)(2,1)S(1)} %get-tuple-element.126), channel_id=1, source_target_pairs={{0,1},{1,0},{2,3},{3,2},{4,5},{5,4},{6,7},{7,6},{8,9},{9,8},{10,11... | collective-permute-start | bytes 1572872 | tf_op jit(solution)/shard_map/ppermute | solution.py:261
  63.1 14.3 %collective-permute-start.17 = (bf16[256,1024]{1,0:T(8,128)(2,1)S(1)}, bf16[256,1024]{1,0:T(8,128)(2,1)S(1)}, u32[]{:S(2)}, u32[]{:S(2)}) collective-permute-start(bf16[256,1024]{1,0:T(8,128)(2,1)S(1)} %collective-permute-done.6.refs_3_.refs_7_.refs_6_), channel_id=1, source_target_pairs={{0,4},{4,0},{8,12},{12,8},{16,20},{20,16},{24,28},{28,24},{1,5},{5... | collective-permute-start | bytes 1572872 | tf_op jit(solution)/shard_map/ppermute | solution.py:261
  74.8 11.9 %collective-permute-start.18 = (bf16[2,96,1024]{2,1,0:T(8,128)(2,1)S(1)}, bf16[2,96,1024]{2,1,0:T(8,128)(2,1)S(1)}, u32[]{:S(2)}, u32[]{:S(2)}) collective-permute-start(bf16[2,96,1024]{2,1,0:T(8,128)(2,1)S(1)} %get-tuple-element.125.refs_1_), channel_id=1, source_target_pairs={{0,4},{4,0},{8,12},{12,8},{16,20},{20,16},{24,28},{28,24},{1,5},{5... | collective-permute-start | bytes 1179656 | tf_op jit(solution)/shard_map/ppermute | solution.py:261
  81.6 12.8 %collective-permute-start.20 = (bf16[384,512]{1,0:T(8,128)(2,1)S(1)}, bf16[384,512]{1,0:T(8,128)(2,1)S(1)}, u32[]{:S(2)}, u32[]{:S(2)}) collective-permute-start(bf16[384,512]{1,0:T(8,128)(2,1)S(1)} %get-tuple-element.133), channel_id=1, source_target_pairs={{0,4},{4,0},{8,12},{12,8},{16,20},{20,16},{24,28},{28,24},{1,5},{5... | collective-permute-start | bytes 1179656 | tf_op jit(solution)/shard_map/ppermute | solution.py:261
  105.1 18.3 %collective-permute-start.26 = (bf16[2,256,512]{2,1,0:T(8,128)(2,1)S(1)}, bf16[2,256,512]{2,1,0:T(8,128)(2,1)S(1)}, u32[]{:S(2)}, u32[]{:S(2)}) collective-permute-start(bf16[2,256,512]{2,1,0:T(8,128)(2,1)S(1)} %get-tuple-element.141.refs_6_), channel_id=1, source_target_pairs={{0,8},{4,12},{8,0},{12,4},{16,24},{20,28},{24,16},{28,20},{1,9},{5... | collective-permute-start | bytes 1572872 | tf_op jit(solution)/shard_map/ppermute | solution.py:261
  107.8 15.5 %collective-permute-start.28 = (bf16[2,128,1024]{2,1,0:T(8,128)(2,1)S(1)}, bf16[2,128,1024]{2,1,0:T(8,128)(2,1)S(1)}, u32[]{:S(2)}, u32[]{:S(2)}) collective-permute-start(bf16[2,128,1024]{2,1,0:T(8,128)(2,1)S(1)} %get-tuple-element.144.refs_2_), channel_id=1, source_target_pairs={{0,4},{4,0},{8,12},{12,8},{16,20},{20,16},{24,28},{28,24},{1,5},{5... | collective-permute-start | bytes 1572872 | tf_op jit(solution)/shard_map/ppermute | solution.py:261
  109.5 13.9 %collective-permute-start.30 = (bf16[2,96,128]{2,1,0:T(8,128)(2,1)S(1)}, bf16[2,96,128]{2,1,0:T(8,128)(2,1)S(1)}, u32[]{:S(2)}, u32[]{:S(2)}) collective-permute-start(bf16[2,96,128]{2,1,0:T(8,128)(2,1)S(1)} %get-tuple-element.147), channel_id=1, source_target_pairs={{0,4},{4,0},{8,12},{12,8},{16,20},{20,16},{24,28},{28,24},{1,5},{5... | collective-permute-start | bytes 147464 | tf_op jit(solution)/shard_map/ppermute | solution.py:261
  110.0 13.4 %collective-permute-start.31 = (bf16[2,96,128]{2,1,0:T(8,128)(2,1)S(1)}, bf16[2,96,128]{2,1,0:T(8,128)(2,1)S(1)}, u32[]{:S(2)}, u32[]{:S(2)}) collective-permute-start(bf16[2,96,128]{2,1,0:T(8,128)(2,1)S(1)} %get-tuple-element.148), channel_id=1, source_target_pairs={{0,8},{4,12},{8,0},{12,4},{16,24},{20,28},{24,16},{28,20},{1,9},{5... | collective-permute-start | bytes 147464 | tf_op jit(solution)/shard_map/ppermute | solution.py:261
  128.3 12.8 %collective-permute-start.39 = (bf16[96,384]{1,0:T(8,128)(2,1)S(1)}, bf16[96,384]{1,0:T(8,128)(2,1)S(1)}, u32[]{:S(2)}, u32[]{:S(2)}) collective-permute-start(bf16[96,384]{1,0:T(8,128)(2,1)S(1)} %get-tuple-element.161.refs_5_), channel_id=1, source_target_pairs={{0,12},{4,8},{8,4},{12,0},{16,28},{20,24},{24,20},{28,16},{1,13},{... | collective-permute-start | bytes 221192 | tf_op jit(solution)/shard_map/ppermute | solution.py:261
  131.9 11.7 %collective-permute-start.41 = (bf16[96,384]{1,0:T(8,128)(2,1)S(1)}, bf16[96,384]{1,0:T(8,128)(2,1)S(1)}, u32[]{:S(2)}, u32[]{:S(2)}) collective-permute-start(bf16[96,384]{1,0:T(8,128)(2,1)S(1)} %get-tuple-element.163.refs_7_), channel_id=1, source_target_pairs={{0,20},{4,16},{8,28},{12,24},{16,4},{20,0},{24,12},{28,8},{1,21},{... | collective-permute-start | bytes 221192 | tf_op jit(solution)/shard_map/ppermute | solution.py:261
  146.0 26.7 %collective-permute-start.49 = (bf16[2,128,1024]{2,1,0:T(8,128)(2,1)S(1)}, bf16[2,128,1024]{2,1,0:T(8,128)(2,1)S(1)}, u32[]{:S(2)}, u32[]{:S(2)}) collective-permute-start(bf16[2,128,1024]{2,1,0:T(8,128)(2,1)S(1)} %get-tuple-element.156.refs_8_), channel_id=1, source_target_pairs={{0,16},{4,20},{8,24},{12,28},{16,0},{20,4},{24,8},{28,12},{1,17},{... | collective-permute-start | bytes 1572872 | tf_op jit(solution)/shard_map/ppermute | solution.py:261
  149.1 24.2 %collective-permute-start.46 = (bf16[2,136,640]{2,1,0:T(8,128)(2,1)S(1)}, bf16[2,136,640]{2,1,0:T(8,128)(2,1)S(1)}, u32[]{:S(2)}, u32[]{:S(2)}) collective-permute-start(bf16[2,136,640]{2,1,0:T(8,128)(2,1)S(1)} %get-tuple-element.175), channel_id=1, source_target_pairs={{0,4},{4,0},{8,12},{12,8},{16,20},{20,16},{24,28},{28,24},{1,5},{5... | collective-permute-start | bytes 1044488 | tf_op jit(solution)/shard_map/ppermute | solution.py:261
  149.7 25.0 %collective-permute-start.47 = (bf16[2,136,640]{2,1,0:T(8,128)(2,1)S(1)}, bf16[2,136,640]{2,1,0:T(8,128)(2,1)S(1)}, u32[]{:S(2)}, u32[]{:S(2)}) collective-permute-start(bf16[2,136,640]{2,1,0:T(8,128)(2,1)S(1)} %get-tuple-element.176), channel_id=1, source_target_pairs={{0,8},{4,12},{8,0},{12,4},{16,24},{20,28},{24,16},{28,20},{1,9},{5... | collective-permute-start | bytes 1044488 | tf_op jit(solution)/shard_map/ppermute | solution.py:261
  149.9 26.6 %collective-permute-start.48 = (bf16[2,136,640]{2,1,0:T(8,128)(2,1)S(1)}, bf16[2,136,640]{2,1,0:T(8,128)(2,1)S(1)}, u32[]{:S(2)}, u32[]{:S(2)}) collective-permute-start(bf16[2,136,640]{2,1,0:T(8,128)(2,1)S(1)} %get-tuple-element.177), channel_id=1, source_target_pairs={{0,12},{4,8},{8,4},{12,0},{16,28},{20,24},{24,20},{28,16},{1,13},{... | collective-permute-start | bytes 1044488 | tf_op jit(solution)/shard_map/ppermute | solution.py:261
  152.8 28.6 %collective-permute-start.45 = (bf16[96,1024]{1,0:T(8,128)(2,1)S(1)}, bf16[96,1024]{1,0:T(8,128)(2,1)S(1)}, u32[]{:S(2)}, u32[]{:S(2)}) collective-permute-start(bf16[96,1024]{1,0:T(8,128)(2,1)S(1)} %get-tuple-element.174.refs_3_), channel_id=1, source_target_pairs={{0,2},{1,3},{2,0},{3,1},{4,6},{5,7},{6,4},{7,5},{8,10},{9,11},{10,... | collective-permute-start | bytes 589832 | tf_op jit(solution)/shard_map/ppermute | solution.py:261
  173.3 21.1 %collective-permute-start.50 = (bf16[96,1024]{1,0:T(8,128)(2,1)S(1)}, bf16[96,1024]{1,0:T(8,128)(2,1)S(1)}, u32[]{:S(2)}, u32[]{:S(2)}) collective-permute-start(bf16[96,1024]{1,0:T(8,128)(2,1)S(1)} %get-tuple-element.172.refs_2_), channel_id=1, source_target_pairs={{0,2},{1,3},{2,0},{3,1},{4,6},{5,7},{6,4},{7,5},{8,10},{9,11},{10,... | collective-permute-start | bytes 589832 | tf_op jit(solution)/shard_map/ppermute | solution.py:261
  176.7 17.0 %collective-permute-start.51 = (bf16[1,136,640]{2,1,0:T(8,128)(2,1)S(1)}, bf16[1,136,640]{2,1,0:T(8,128)(2,1)S(1)}, u32[]{:S(2)}, u32[]{:S(2)}) collective-permute-start(bf16[1,136,640]{2,1,0:T(8,128)(2,1)S(1)} %get-tuple-element.181.refs_8_), channel_id=1, source_target_pairs={{0,16},{4,20},{8,24},{12,28},{16,0},{20,4},{24,8},{28,12},{1,17},{... | collective-permute-start | bytes 522248 | tf_op jit(solution)/shard_map/ppermute | solution.py:261
  179.5 19.0 %collective-permute-start.59 = (bf16[128,1024]{1,0:T(8,128)(2,1)S(1)}, bf16[128,1024]{1,0:T(8,128)(2,1)S(1)}, u32[]{:S(2)}, u32[]{:S(2)}) collective-permute-start(bf16[128,1024]{1,0:T(8,128)(2,1)S(1)} %get-tuple-element.197), channel_id=1, source_target_pairs={{0,0},{1,8},{2,16},{3,24},{4,1},{5,9},{6,17},{7,25},{8,2},{9,10},{... | collective-permute-start | bytes 786440 | tf_op jit(solution)/shard_map/ppermute | solution.py:1039
  185.2 16.5 %collective-permute-start.57 = (bf16[32,1152]{1,0:T(8,128)(2,1)S(1)}, bf16[32,1152]{1,0:T(8,128)(2,1)S(1)}, u32[]{:S(2)}, u32[]{:S(2)}) collective-permute-start(bf16[32,1152]{1,0:T(8,128)(2,1)S(1)} %get-tuple-element.195), channel_id=1, source_target_pairs={{0,2},{1,3},{2,0},{3,1},{4,6},{5,7},{6,4},{7,5},{8,10},{9,11},{10,... | collective-permute-start | bytes 221192 | tf_op jit(solution)/shard_map/ppermute | solution.py:261
  (47 other events, 355.4 us)

commit v6 on v4

--- a/solution.py
+++ b/solution.py
@@ -778,7 +778,8 @@
     grad_router[...] = as_row(router)
 
 
-def join_down_kernel(block, out):
+def join_down_kernel(block, token, out):
+    token[...] = jnp.zeros(token.shape, F32)
     out[...] = block[...].astype(F32)
 
 
@@ -1066,8 +1067,8 @@
     qkv_chunks = swap_pieces(qkv_chunks)
     grad_out = lax.ppermute(grad_out, ("ctx", "fsdp"), owners)
     row = sds((1, 32), F32)
-    (grad_down,) = call(
-        join_down_kernel, (sds((128, width), F32),), (), (down,), name="join_down"
+    _, grad_down = call(
+        join_down_kernel, (local((8, 128), F32), sds((128, width), F32)), (), (down,), name="join_down"
     )
     grad_up, grad_gain_mlp = call(
         join_up_kernel, (sds((32, 4 * hidden), F32), row), (ids,), (*chunks, gain_mlp), name="join_up"

time: 208 us -> 212 us (1.019)
  waiting for transfers between devices: 74.9 us -> 80.7 us
    ppermute x1, waiting for transfers between devices: 0.01 us -> 3.96 us  [shards_8x4(): down = lax.ppermute(down, ('ctx', 'fsdp'), owners)]
  transfers between devices with their start and end apart: 61 -> 61, of which waited for: 20 -> 21; matrix products, arithmetic and copies ran while one was open for 0% -> 0% of each run, Pallas kernels for 15% -> 15%
where the time goes in v6:
time: 212 us; the launch traced here: 211 us
  waiting for transfers between devices  80.7 us (38%)
  starting transfers between devices  65.7 us (31%)
  Pallas kernels  40.3 us (19%)
  blocking collectives  21.6 us (10%)
    ppermute x56, waiting for transfers between devices, exchange(): return lax.ppermute(x, axis, [(i, i ^ mask) for i in range(size)])  68.9 us
    ppermute x56, starting transfers between devices, exchange(): return lax.ppermute(x, axis, [(i, i ^ mask) for i in range(size)])  56.8 us
    pallas_call x36, Pallas kernels, __call__(): pl.pallas_call(body, out_shape=tuple(outs), in_specs=[pl.BlockSpec(memory...  40.3 us
    all_gather x1, blocking collectives, shards_8x4(): near_rows = lax.all_gather(turned, 'fsdp', axis=0, tiled=True)  12.7 us
    all_gather x1, blocking collectives, shards_8x4(): far_rows = lax.all_gather(turned_far, 'fsdp', axis=0, tiled=True)  8.84 us
    ppermute x1, waiting for transfers between devices, shards_8x4(): grad_out = lax.ppermute(grad_out, ('ctx', 'fsdp'), owners)  5.43 us
  transfers between devices with their start and end apart: 61, of which 21 were waited for; matrix products, arithmetic and copies ran while one was open for 0% of the time, Pallas kernels for 15%

profile of v6, /device:TPU:4, one launch (start us, length us, event | category | flops | bytes accessed | tf_op | source)
XLA Modules:
  0.0 211.5 jit_solution(6113083754628641149)
XLA Ops:
  2.1 2.5 %front.1 = (bf16[104,1024]{1,0:T(8,128)(2,1)S(1)}, bf16[256,384]{1,0:T(8,128)(2,1)S(1)}, bf16[256,384]{1,0:T(8,128)(2,1)S(1)}, bf16[256,384]{1,0:T(8,128)(2,1)S(1)}) custom-call(s32[2]{0:T(128)S(1)} %pad_add_fusion.refs_0_, s32[16]{0:T(128)S(1)} %copy-done.9, bf16[3,256,1024]{2,1,0:T(8,128)(2,1)} %bitcast.21, bf16[256,3072]{1,0:T(8,128)(2,1)} %refs_1_.6, ...), custom_call_target="tpu_custom_call" | custom-call | flops 10000000000 | bytes 1000000 | tf_op jit(solution)/shard_map/front/pallas_call | solution.py:221
  11.7 2.6 %collective-permute-start.1 = (bf16[104,1024]{1,0:T(8,128)(2,1)S(1)}, bf16[104,1024]{1,0:T(8,128)(2,1)S(1)}, u32[]{:S(2)}, u32[]{:S(2)}) collective-permute-start(bf16[104,1024]{1,0:T(8,128)(2,1)S(1)} %collective-permute-done), channel_id=1, source_target_pairs={{0,16},{4,20},{8,24},{12,28},{16,0},{20,4},{24,8},{28,12},{1,17},{... | collective-permute-start | bytes 638984 | tf_op jit(solution)/shard_map/ppermute | solution.py:261
  14.3 12.7 %all_gather.6.refs_2_.refs_1_ = bf16[416,1024]{1,0:T(8,128)(2,1)S(1)} all-gather(bf16[104,1024]{1,0:T(8,128)(2,1)S(1)} %collective-permute-done), channel_id=1, replica_groups=mesh['ctx'=8,'fsdp'=4] {'fsdp'}, dimensions={0}, use_global_device_ids=true | all-gather | bytes 1064960 | tf_op jit(solution)/shard_map/all_gather | solution.py:925
  27.4 8.8 %all_gather.7.refs_2_ = bf16[416,1024]{1,0:T(8,128)(2,1)S(1)} all-gather(bf16[104,1024]{1,0:T(8,128)(2,1)S(1)} %collective-permute-done.1), channel_id=1, replica_groups=mesh['ctx'=8,'fsdp'=4] {'fsdp'}, dimensions={0}, use_global_device_ids=true | all-gather | bytes 1064960 | tf_op jit(solution)/shard_map/all_gather | solution.py:926
  37.2 3.3 %attend.1 = (bf16[4,96,128]{2,1,0:T(8,128)(2,1)S(1)}, bf16[4,96,128]{2,1,0:T(8,128)(2,1)S(1)}, bf16[3,256,384]{2,1,0:T(8,128)(2,1)S(1)}, f32[6,256,256]{2,1,0:T(8,128)S(1)}, bf16[768,1024]{1,0:T(8,128)(2,1)S(1)}) custom-call(s32[2]{0:T(128)S(1)} %pad_add_fusion.refs_0_, bf16[416,1024]{1,0:T(8,128)(2,1)S(1)} %all_gather.6.refs_2_.refs_1_, ...), custom_call_target="tpu_custom_call" | custom-call | flops 10000000000 | bytes 1000000 | tf_op jit(solution)/shard_map/attend/pallas_call | solution.py:221
  45.6 2.8 %collective-permute-done.5.refs_1_ = bf16[4,96,128]{2,1,0:T(8,128)(2,1)S(1)} collective-permute-done((bf16[4,96,128]{2,1,0:T(8,128)(2,1)S(1)}, bf16[4,96,128]{2,1,0:T(8,128)(2,1)S(1)}, u32[]{:S(2)}, u32[]{:S(2)}) %collective-permute-start.5) | collective-permute-done | bytes 98336 | tf_op jit(solution)/shard_map/ppermute | solution.py:261
  50.1 2.8 %collective-permute-start.7 = (bf16[2,96,128]{2,1,0:T(8,128)(2,1)S(1)}, bf16[2,96,128]{2,1,0:T(8,128)(2,1)S(1)}, u32[]{:S(2)}, u32[]{:S(2)}) collective-permute-start(bf16[2,96,128]{2,1,0:T(8,128)(2,1)S(1)} %get-tuple-element.117), channel_id=1, source_target_pairs={{0,4},{4,0},{8,12},{12,8},{16,20},{20,16},{24,28},{28,24},{1,5},{5... | collective-permute-start | bytes 147464 | tf_op jit(solution)/shard_map/ppermute | solution.py:261
  54.4 4.9 %collective-permute-done.10.refs_8_.refs_1_.refs_3_.refs_4_.refs_5_ = bf16[200,1024]{1,0:T(8,128)(2,1)S(1)} collective-permute-done((bf16[200,1024]{1,0:T(8,128)(2,1)S(1)}, bf16[200,1024]{1,0:T(8,128)(2,1)S(1)}, u32[]{:S(2)}, u32[]{:S(2)}) %collective-permute-start.10) | collective-permute-done | bytes 409632 | tf_op jit(solution)/shard_map/ppermute | solution.py:261
  64.9 8.5 %collective-permute-done.12.refs_1_ = bf16[2,96,1024]{2,1,0:T(8,128)(2,1)S(1)} collective-permute-done((bf16[2,96,1024]{2,1,0:T(8,128)(2,1)S(1)}, bf16[2,96,1024]{2,1,0:T(8,128)(2,1)S(1)}, u32[]{:S(2)}, u32[]{:S(2)}) %collective-permute-start.12) | collective-permute-done | bytes 393248 | tf_op jit(solution)/shard_map/ppermute | solution.py:261
  77.5 4.1 %mlp.1 = (bf16[2,96,1024]{2,1,0:T(8,128)(2,1)S(1)}, f32[2,96,1024]{2,1,0:T(8,128)S(1)}, bf16[384,512]{1,0:T(8,128)(2,1)S(1)}, bf16[384,512]{1,0:T(8,128)(2,1)S(1...) custom-call(s32[2]{0:T(128)S(1)} %pad_add_fusion.refs_0_, ...), custom_call_target="tpu_custom_call" | custom-call | flops 10000000000 | bytes 1000000 | tf_op jit(solution)/shard_map/mlp/pallas_call | solution.py:221
  88.1 6.4 %collective-permute-done.20.refs_8_.refs_5_ = bf16[384,512]{1,0:T(8,128)(2,1)S(1)} collective-permute-done((bf16[384,512]{1,0:T(8,128)(2,1)S(1)}, bf16[384,512]{1,0:T(8,128)(2,1)S(1)}, u32[]{:S(2)}, u32[]{:S(2)}) %collective-permute-start.20) | collective-permute-done | bytes 393248 | tf_op jit(solution)/shard_map/ppermute | solution.py:261
  113.7 9.7 %collective-permute-done.30.refs_2_ = bf16[2,96,128]{2,1,0:T(8,128)(2,1)S(1)} collective-permute-done((bf16[2,96,128]{2,1,0:T(8,128)(2,1)S(1)}, bf16[2,96,128]{2,1,0:T(8,128)(2,1)S(1)}, u32[]{:S(2)}, u32[]{:S(2)}) %collective-permute-start.30) | collective-permute-done | bytes 49184 | tf_op jit(solution)/shard_map/ppermute | solution.py:261
  123.4 3.0 %attend_back.1 = (bf16[96,384]{1,0:T(8,128)(2,1)S(1)}, bf16[96,384]{1,0:T(8,128)(2,1)S(1)}, bf16[96,384]{1,0:T(8,128)(2,1)S(1)}, bf16[96,384]{1,0:T(8,128)(2,1)S...) custom-call(s32[2]{0:T(128)S(1)} %pad_add_fusion.refs_0_, ...), custom_call_target="tpu_custom_call" | custom-call | flops 10000000000 | bytes 1000000 | tf_op jit(solution)/shard_map/attend_back/pallas_call | solution.py:221
  133.6 2.5 %collective-permute-start.42 = (bf16[96,384]{1,0:T(8,128)(2,1)S(1)}, bf16[96,384]{1,0:T(8,128)(2,1)S(1)}, u32[]{:S(2)}, u32[]{:S(2)}) collective-permute-start(bf16[96,384]{1,0:T(8,128)(2,1)S(1)} %get-tuple-element.163.refs_8_), channel_id=1, source_target_pairs={{0,24},{4,28},{8,16},{12,20},{16,8},{20,12},{24,0},{28,4},{1,25},{... | collective-permute-start | bytes 221192 | tf_op jit(solution)/shard_map/ppermute | solution.py:261
  141.1 2.5 %collective-permute-done.41.refs_6_ = bf16[96,384]{1,0:T(8,128)(2,1)S(1)} collective-permute-done((bf16[96,384]{1,0:T(8,128)(2,1)S(1)}, bf16[96,384]{1,0:T(8,128)(2,1)S(1)}, u32[]{:S(2)}, u32[]{:S(2)}) %collective-permute-start.41) | collective-permute-done | bytes 73760 | tf_op jit(solution)/shard_map/ppermute | solution.py:261
  146.0 3.2 %collective-permute-start.49 = (bf16[2,128,1024]{2,1,0:T(8,128)(2,1)S(1)}, bf16[2,128,1024]{2,1,0:T(8,128)(2,1)S(1)}, u32[]{:S(2)}, u32[]{:S(2)}) collective-permute-start(bf16[2,128,1024]{2,1,0:T(8,128)(2,1)S(1)} %get-tuple-element.155.refs_8_), channel_id=1, source_target_pairs={{0,16},{4,20},{8,24},{12,28},{16,0},{20,4},{24,8},{28,12},{1,17},{... | collective-permute-start | bytes 1572872 | tf_op jit(solution)/shard_map/ppermute | solution.py:261
  149.9 2.7 %collective-permute-start.48 = (bf16[2,136,640]{2,1,0:T(8,128)(2,1)S(1)}, bf16[2,136,640]{2,1,0:T(8,128)(2,1)S(1)}, u32[]{:S(2)}, u32[]{:S(2)}) collective-permute-start(bf16[2,136,640]{2,1,0:T(8,128)(2,1)S(1)} %get-tuple-element.176), channel_id=1, source_target_pairs={{0,12},{4,8},{8,4},{12,0},{16,28},{20,24},{24,20},{28,16},{1,13},{... | collective-permute-start | bytes 1044488 | tf_op jit(solution)/shard_map/ppermute | solution.py:261
  154.2 18.4 %collective-permute-done.49.refs_2_ = bf16[2,128,1024]{2,1,0:T(8,128)(2,1)S(1)} collective-permute-done((bf16[2,128,1024]{2,1,0:T(8,128)(2,1)S(1)}, bf16[2,128,1024]{2,1,0:T(8,128)(2,1)S(1)}, u32[]{:S(2)}, u32[]{:S(2)}) %collective-permute-start.49) | collective-permute-done | bytes 524320 | tf_op jit(solution)/shard_map/ppermute | solution.py:261
  176.7 2.8 %collective-permute-start.51 = (bf16[1,136,640]{2,1,0:T(8,128)(2,1)S(1)}, bf16[1,136,640]{2,1,0:T(8,128)(2,1)S(1)}, u32[]{:S(2)}, u32[]{:S(2)}) collective-permute-start(bf16[1,136,640]{2,1,0:T(8,128)(2,1)S(1)} %get-tuple-element.180.refs_8_), channel_id=1, source_target_pairs={{0,16},{4,20},{8,24},{12,28},{16,0},{20,4},{24,8},{28,12},{1,17},{... | collective-permute-start | bytes 522248 | tf_op jit(solution)/shard_map/ppermute | solution.py:261
  181.4 2.3 %output.1 = (f32[96,1]{1,0:T(8,128)S(1)}, bf16[3,256,1024]{2,1,0:T(8,128)(2,1)}) custom-call(s32[2]{0:T(128)S(1)} %pad_add_fusion.refs_0_, s32[3,32]{1,0:T(4,128)S(1)} %bitcast.25, f32[96,1024]{1,0:T(8,128)S(1)} %get-tuple-element.172.refs_2_, bf16[96,1024]{1,0:T(8,128)(2,1)S(1)} %collective-permute-done.45.refs_3_, ...), custom_call_target="tpu_custom_call" | custom-call | tf_op jit(solution)/shard_map/output/pallas_call | solution.py:221
  187.4 2.4 %input_grad.1 = bf16[3,256,1024]{2,1,0:T(8,128)(2,1)} custom-call(s32[2]{0:T(128)S(1)} %pad_add_fusion.refs_0_, s32[3,32]{1,0:T(4,128)S(1)} %bitcast.26, f32[96,1024]{1,0:T(8,128)S(1)} %get-tuple-element.182.refs_2_, bf16[96,1024]{1,0:T(8,128)(2,1)S(1)} %collective-permute-done.50.refs_3_, f32[96,1024]{1,0:T(8,128)S(1)} %get-tuple-element.137.refs_4_, ...), custom_call_target="tpu_custom_call" | custom-call | tf_op jit(solution)/shard_map/input_grad/pallas_call | solution.py:221
  189.9 3.9 %collective-permute-done.51.refs_2_ = bf16[1,136,640]{2,1,0:T(8,128)(2,1)S(1)} collective-permute-done((bf16[1,136,640]{2,1,0:T(8,128)(2,1)S(1)}, bf16[1,136,640]{2,1,0:T(8,128)(2,1)S(1)}, u32[]{:S(2)}, u32[]{:S(2)}) %collective-permute-start.51) | collective-permute-done | bytes 174112 | tf_op jit(solution)/shard_map/ppermute | solution.py:261
  194.5 4.0 %collective-permute-done.56.refs_0_ = bf16[128,1024]{1,0:T(8,128)(2,1)S(1)} collective-permute-done((bf16[128,1024]{1,0:T(8,128)(2,1)S(1)}, bf16[128,1024]{1,0:T(8,128)(2,1)S(1)}, u32[]{:S(2)}, u32[]{:S(2)}) %collective-permute-start.56) | collective-permute-done | bytes 262176 | tf_op jit(solution)/shard_map/ppermute | solution.py:1038
  205.4 5.4 %collective-permute-done.57 = f32[32,1024]{1,0:T(8,128)S(1)} collective-permute-done((f32[32,1024]{1,0:T(8,128)S(1)}, f32[32,1024]{1,0:T(8,128)S(1)}, u32[]{:S(2)}, u32[]{:S(2)}) %collective-permute-start.57) | collective-permute-done | bytes 131104 | tf_op jit(solution)/shard_map/ppermute | solution.py:1068
  (160 shorter events, 88.1 us)
Async XLA Ops:
  6.5 20.6 %collective-permute-start.3 = (bf16[256,384]{1,0:T(8,128)(2,1)S(1)}, bf16[256,384]{1,0:T(8,128)(2,1)S(1)}, u32[]{:S(2)}, u32[]{:S(2)}) collective-permute-start(bf16[256,384]{1,0:T(8,128)(2,1)S(1)} %get-tuple-element.110), channel_id=1, source_target_pairs={{0,2},{1,3},{2,0},{3,1},{4,7},{5,6},{6,5},{7,4},{8,10},{9,11},{10,... | collective-permute-start | bytes 589832 | tf_op jit(solution)/shard_map/ppermute | solution.py:864
  8.7 28.5 %collective-permute-start.2 = (bf16[256,384]{1,0:T(8,128)(2,1)S(1)}, bf16[256,384]{1,0:T(8,128)(2,1)S(1)}, u32[]{:S(2)}, u32[]{:S(2)}) collective-permute-start(bf16[256,384]{1,0:T(8,128)(2,1)S(1)} %get-tuple-element.109), channel_id=1, source_target_pairs={{0,1},{1,0},{2,3},{3,2},{4,5},{5,4},{6,7},{7,6},{8,9},{9,8},{10,11... | collective-permute-start | bytes 589832 | tf_op jit(solution)/shard_map/ppermute | solution.py:261
  11.7 15.7 %collective-permute-start.1 = (bf16[104,1024]{1,0:T(8,128)(2,1)S(1)}, bf16[104,1024]{1,0:T(8,128)(2,1)S(1)}, u32[]{:S(2)}, u32[]{:S(2)}) collective-permute-start(bf16[104,1024]{1,0:T(8,128)(2,1)S(1)} %collective-permute-done), channel_id=1, source_target_pairs={{0,16},{4,20},{8,24},{12,28},{16,0},{20,4},{24,8},{28,12},{1,17},{... | collective-permute-start | bytes 638984 | tf_op jit(solution)/shard_map/ppermute | solution.py:261
  36.3 13.8 %collective-permute-start.6 = (bf16[256,1024]{1,0:T(8,128)(2,1)S(1)}, bf16[256,1024]{1,0:T(8,128)(2,1)S(1)}, u32[]{:S(2)}, u32[]{:S(2)}) collective-permute-start(bf16[256,1024]{1,0:T(8,128)(2,1)S(1)} %hold.3.refs_8_), channel_id=1, source_target_pairs={{0,2},{1,3},{2,0},{3,1},{4,7},{5,6},{6,5},{7,4},{8,10},{9,11},{10,... | collective-permute-start | bytes 1572872 | tf_op jit(solution)/shard_map/ppermute | solution.py:864
  44.8 14.5 %collective-permute-start.10 = (bf16[200,1024]{1,0:T(8,128)(2,1)S(1)}, bf16[200,1024]{1,0:T(8,128)(2,1)S(1)}, u32[]{:S(2)}, u32[]{:S(2)}) collective-permute-start(bf16[200,1024]{1,0:T(8,128)(2,1)S(1)} %cot_rows.1.refs_2_.refs_0_.refs_3_.refs_4_.refs_5_), channel_id=1, source_target_pairs={{0,2},{1,3},{2,0},{3,1},{4,6},{5,7},{6,4},{7,5},{8,10},{9,11},{10,... | collective-permute-start | bytes 1228808 | tf_op jit(solution)/shard_map/ppermute | solution.py:261
  63.1 13.2 %collective-permute-start.16 = (bf16[256,1024]{1,0:T(8,128)(2,1)S(1)}, bf16[256,1024]{1,0:T(8,128)(2,1)S(1)}, u32[]{:S(2)}, u32[]{:S(2)}) collective-permute-start(bf16[256,1024]{1,0:T(8,128)(2,1)S(1)} %get-tuple-element.125), channel_id=1, source_target_pairs={{0,1},{1,0},{2,3},{3,2},{4,5},{5,4},{6,7},{7,6},{8,9},{9,8},{10,11... | collective-permute-start | bytes 1572872 | tf_op jit(solution)/shard_map/ppermute | solution.py:261
  63.1 14.3 %collective-permute-start.17 = (bf16[256,1024]{1,0:T(8,128)(2,1)S(1)}, bf16[256,1024]{1,0:T(8,128)(2,1)S(1)}, u32[]{:S(2)}, u32[]{:S(2)}) collective-permute-start(bf16[256,1024]{1,0:T(8,128)(2,1)S(1)} %collective-permute-done.6.refs_3_.refs_7_.refs_6_), channel_id=1, source_target_pairs={{0,4},{4,0},{8,12},{12,8},{16,20},{20,16},{24,28},{28,24},{1,5},{5... | collective-permute-start | bytes 1572872 | tf_op jit(solution)/shard_map/ppermute | solution.py:261
  81.6 12.8 %collective-permute-start.20 = (bf16[384,512]{1,0:T(8,128)(2,1)S(1)}, bf16[384,512]{1,0:T(8,128)(2,1)S(1)}, u32[]{:S(2)}, u32[]{:S(2)}) collective-permute-start(bf16[384,512]{1,0:T(8,128)(2,1)S(1)} %get-tuple-element.132), channel_id=1, source_target_pairs={{0,4},{4,0},{8,12},{12,8},{16,20},{20,16},{24,28},{28,24},{1,5},{5... | collective-permute-start | bytes 1179656 | tf_op jit(solution)/shard_map/ppermute | solution.py:261
  105.1 18.3 %collective-permute-start.26 = (bf16[2,256,512]{2,1,0:T(8,128)(2,1)S(1)}, bf16[2,256,512]{2,1,0:T(8,128)(2,1)S(1)}, u32[]{:S(2)}, u32[]{:S(2)}) collective-permute-start(bf16[2,256,512]{2,1,0:T(8,128)(2,1)S(1)} %get-tuple-element.140.refs_6_), channel_id=1, source_target_pairs={{0,8},{4,12},{8,0},{12,4},{16,24},{20,28},{24,16},{28,20},{1,9},{5... | collective-permute-start | bytes 1572872 | tf_op jit(solution)/shard_map/ppermute | solution.py:261
  107.9 15.5 %collective-permute-start.28 = (bf16[2,128,1024]{2,1,0:T(8,128)(2,1)S(1)}, bf16[2,128,1024]{2,1,0:T(8,128)(2,1)S(1)}, u32[]{:S(2)}, u32[]{:S(2)}) collective-permute-start(bf16[2,128,1024]{2,1,0:T(8,128)(2,1)S(1)} %get-tuple-element.143.refs_2_), channel_id=1, source_target_pairs={{0,4},{4,0},{8,12},{12,8},{16,20},{20,16},{24,28},{28,24},{1,5},{5... | collective-permute-start | bytes 1572872 | tf_op jit(solution)/shard_map/ppermute | solution.py:261
  109.5 13.9 %collective-permute-start.30 = (bf16[2,96,128]{2,1,0:T(8,128)(2,1)S(1)}, bf16[2,96,128]{2,1,0:T(8,128)(2,1)S(1)}, u32[]{:S(2)}, u32[]{:S(2)}) collective-permute-start(bf16[2,96,128]{2,1,0:T(8,128)(2,1)S(1)} %get-tuple-element.146), channel_id=1, source_target_pairs={{0,4},{4,0},{8,12},{12,8},{16,20},{20,16},{24,28},{28,24},{1,5},{5... | collective-permute-start | bytes 147464 | tf_op jit(solution)/shard_map/ppermute | solution.py:261
  110.0 13.4 %collective-permute-start.31 = (bf16[2,96,128]{2,1,0:T(8,128)(2,1)S(1)}, bf16[2,96,128]{2,1,0:T(8,128)(2,1)S(1)}, u32[]{:S(2)}, u32[]{:S(2)}) collective-permute-start(bf16[2,96,128]{2,1,0:T(8,128)(2,1)S(1)} %get-tuple-element.147), channel_id=1, source_target_pairs={{0,8},{4,12},{8,0},{12,4},{16,24},{20,28},{24,16},{28,20},{1,9},{5... | collective-permute-start | bytes 147464 | tf_op jit(solution)/shard_map/ppermute | solution.py:261
  128.3 12.8 %collective-permute-start.39 = (bf16[96,384]{1,0:T(8,128)(2,1)S(1)}, bf16[96,384]{1,0:T(8,128)(2,1)S(1)}, u32[]{:S(2)}, u32[]{:S(2)}) collective-permute-start(bf16[96,384]{1,0:T(8,128)(2,1)S(1)} %get-tuple-element.160.refs_5_), channel_id=1, source_target_pairs={{0,12},{4,8},{8,4},{12,0},{16,28},{20,24},{24,20},{28,16},{1,13},{... | collective-permute-start | bytes 221192 | tf_op jit(solution)/shard_map/ppermute | solution.py:261
  146.0 26.7 %collective-permute-start.49 = (bf16[2,128,1024]{2,1,0:T(8,128)(2,1)S(1)}, bf16[2,128,1024]{2,1,0:T(8,128)(2,1)S(1)}, u32[]{:S(2)}, u32[]{:S(2)}) collective-permute-start(bf16[2,128,1024]{2,1,0:T(8,128)(2,1)S(1)} %get-tuple-element.155.refs_8_), channel_id=1, source_target_pairs={{0,16},{4,20},{8,24},{12,28},{16,0},{20,4},{24,8},{28,12},{1,17},{... | collective-permute-start | bytes 1572872 | tf_op jit(solution)/shard_map/ppermute | solution.py:261
  149.2 24.2 %collective-permute-start.46 = (bf16[2,136,640]{2,1,0:T(8,128)(2,1)S(1)}, bf16[2,136,640]{2,1,0:T(8,128)(2,1)S(1)}, u32[]{:S(2)}, u32[]{:S(2)}) collective-permute-start(bf16[2,136,640]{2,1,0:T(8,128)(2,1)S(1)} %get-tuple-element.174), channel_id=1, source_target_pairs={{0,4},{4,0},{8,12},{12,8},{16,20},{20,16},{24,28},{28,24},{1,5},{5... | collective-permute-start | bytes 1044488 | tf_op jit(solution)/shard_map/ppermute | solution.py:261
  149.7 25.0 %collective-permute-start.47 = (bf16[2,136,640]{2,1,0:T(8,128)(2,1)S(1)}, bf16[2,136,640]{2,1,0:T(8,128)(2,1)S(1)}, u32[]{:S(2)}, u32[]{:S(2)}) collective-permute-start(bf16[2,136,640]{2,1,0:T(8,128)(2,1)S(1)} %get-tuple-element.175), channel_id=1, source_target_pairs={{0,8},{4,12},{8,0},{12,4},{16,24},{20,28},{24,16},{28,20},{1,9},{5... | collective-permute-start | bytes 1044488 | tf_op jit(solution)/shard_map/ppermute | solution.py:261
  149.9 26.6 %collective-permute-start.48 = (bf16[2,136,640]{2,1,0:T(8,128)(2,1)S(1)}, bf16[2,136,640]{2,1,0:T(8,128)(2,1)S(1)}, u32[]{:S(2)}, u32[]{:S(2)}) collective-permute-start(bf16[2,136,640]{2,1,0:T(8,128)(2,1)S(1)} %get-tuple-element.176), channel_id=1, source_target_pairs={{0,12},{4,8},{8,4},{12,0},{16,28},{20,24},{24,20},{28,16},{1,13},{... | collective-permute-start | bytes 1044488 | tf_op jit(solution)/shard_map/ppermute | solution.py:261
  152.8 28.6 %collective-permute-start.45 = (bf16[96,1024]{1,0:T(8,128)(2,1)S(1)}, bf16[96,1024]{1,0:T(8,128)(2,1)S(1)}, u32[]{:S(2)}, u32[]{:S(2)}) collective-permute-start(bf16[96,1024]{1,0:T(8,128)(2,1)S(1)} %get-tuple-element.173.refs_3_), channel_id=1, source_target_pairs={{0,2},{1,3},{2,0},{3,1},{4,6},{5,7},{6,4},{7,5},{8,10},{9,11},{10,... | collective-permute-start | bytes 589832 | tf_op jit(solution)/shard_map/ppermute | solution.py:261
  173.4 14.1 %collective-permute-start.50 = (bf16[96,1024]{1,0:T(8,128)(2,1)S(1)}, bf16[96,1024]{1,0:T(8,128)(2,1)S(1)}, u32[]{:S(2)}, u32[]{:S(2)}) collective-permute-start(bf16[96,1024]{1,0:T(8,128)(2,1)S(1)} %get-tuple-element.171.refs_2_), channel_id=1, source_target_pairs={{0,2},{1,3},{2,0},{3,1},{4,6},{5,7},{6,4},{7,5},{8,10},{9,11},{10,... | collective-permute-start | bytes 589832 | tf_op jit(solution)/shard_map/ppermute | solution.py:261
  176.7 17.0 %collective-permute-start.51 = (bf16[1,136,640]{2,1,0:T(8,128)(2,1)S(1)}, bf16[1,136,640]{2,1,0:T(8,128)(2,1)S(1)}, u32[]{:S(2)}, u32[]{:S(2)}) collective-permute-start(bf16[1,136,640]{2,1,0:T(8,128)(2,1)S(1)} %get-tuple-element.180.refs_8_), channel_id=1, source_target_pairs={{0,16},{4,20},{8,24},{12,28},{16,0},{20,4},{24,8},{28,12},{1,17},{... | collective-permute-start | bytes 522248 | tf_op jit(solution)/shard_map/ppermute | solution.py:261
  179.5 19.0 %collective-permute-start.56 = (bf16[128,1024]{1,0:T(8,128)(2,1)S(1)}, bf16[128,1024]{1,0:T(8,128)(2,1)S(1)}, u32[]{:S(2)}, u32[]{:S(2)}) collective-permute-start(bf16[128,1024]{1,0:T(8,128)(2,1)S(1)} %get-tuple-element.193), channel_id=1, source_target_pairs={{0,0},{1,8},{2,16},{3,24},{4,1},{5,9},{6,17},{7,25},{8,2},{9,10},{... | collective-permute-start | bytes 786440 | tf_op jit(solution)/shard_map/ppermute | solution.py:1038
  185.1 14.2 %collective-permute-start.58 = (bf16[32,1152]{1,0:T(8,128)(2,1)S(1)}, bf16[32,1152]{1,0:T(8,128)(2,1)S(1)}, u32[]{:S(2)}, u32[]{:S(2)}) collective-permute-start(bf16[32,1152]{1,0:T(8,128)(2,1)S(1)} %get-tuple-element.199), channel_id=1, source_target_pairs={{0,1},{1,0},{2,3},{3,2},{4,5},{5,4},{6,7},{7,6},{8,9},{9,8},{10,11... | collective-permute-start | bytes 221192 | tf_op jit(solution)/shard_map/ppermute | solution.py:261
  185.2 15.3 %collective-permute-start.59 = (bf16[32,1152]{1,0:T(8,128)(2,1)S(1)}, bf16[32,1152]{1,0:T(8,128)(2,1)S(1)}, u32[]{:S(2)}, u32[]{:S(2)}) collective-permute-start(bf16[32,1152]{1,0:T(8,128)(2,1)S(1)} %get-tuple-element.200), channel_id=1, source_target_pairs={{0,2},{1,3},{2,0},{3,1},{4,6},{5,7},{6,4},{7,5},{8,10},{9,11},{10,... | collective-permute-start | bytes 221192 | tf_op jit(solution)/shard_map/ppermute | solution.py:261
  187.4 15.1 %collective-permute-start.60 = (bf16[32,1152]{1,0:T(8,128)(2,1)S(1)}, bf16[32,1152]{1,0:T(8,128)(2,1)S(1)}, u32[]{:S(2)}, u32[]{:S(2)}) collective-permute-start(bf16[32,1152]{1,0:T(8,128)(2,1)S(1)} %get-tuple-element.201), channel_id=1, source_target_pairs={{0,3},{1,2},{2,1},{3,0},{4,7},{5,6},{6,5},{7,4},{8,11},{9,10},{10,... | collective-permute-start | bytes 221192 | tf_op jit(solution)/shard_map/ppermute | solution.py:261
  (47 other events, 347.5 us)
